TPU v7x, 512 devices: a whole 4x4x16 slice. The times are simulated.
512 devices in a mesh: pair: 64 (over z_lo, x, core), aux: 8 (over y, z_hi).
Axes of the slice: x: 4, y: 4, z: 16 (z_hi: 2, z_lo: 8; z = z_hi * 8 + z_lo), core: 2. Of those that a mesh axis runs over, the one named last changes fastest.
Arguments:
- doubles: bfloat16 [128, 512, 512], P('pair', 'aux'), may hold values from -1.796875 to 1.796875
- singles: bfloat16 [256, 512], replicated, may hold values from -0.8984375 to 0.8984375
- vir_slabs: bfloat16 [4096, 8, 512], P(('aux', 'pair')), may hold values from -0.059814453 to 0.059814453
- occ_slabs: bfloat16 [4096, 256, 512], P(('aux', 'pair')), may hold values from -0.029907227 to 0.029907227
- occ_energy: float32 [256], replicated, may hold values from -2 to -0.5
- vir_energy: float32 [8], replicated, may hold values from 0.1 to 1.5
- pair_list: int32 [128, 2], P('pair'), may hold values from 0 to 255
Outputs:
- new_doubles: float32 [128, 8, 8], P('pair', 'aux')
All inputs are finite; a program needn't handle non-finite values.
Results may differ from a plain program's by a relative error of at most 0.0005.
Values may be sent and summed in bfloat16 or wider, within the bound.
No kernel may reach another device: no remote copies, remote signals or barrier semaphores. Data moves between devices by JAX's collectives and lax.ppermute only.
A program may use at most 64 MiB of HBM per device.

v0:
```python
import jax
import jax.numpy as jnp
from jax import lax
from jax.experimental import pallas as pl
from jax.experimental.pallas import tpu as pltpu
from jax.sharding import Mesh, PartitionSpec as P


NWIN = 8
GROUP = 256
BLOCK = 512
PAIR = ("zm", "zb", "x", "k")
AUX = ("y", "zh")
SWAP = [(0, 1), (1, 0)]
UP = [(i, (i + 1) % 4) for i in range(4)]
DOWN = [(i, (i + 3) % 4) for i in range(4)]
SMEM = pl.BlockSpec(memory_space=pltpu.SMEM)
VMEM = pl.BlockSpec(memory_space=pltpu.VMEM)


def start_kernel(
    pairs_ref, place_ref, occ_energy_ref, vir_energy_ref, doubles_ref, singles_ref, vir_ref, occ_ref,
    dressed_ref, tau_ref, denominator_ref, window_ref, cols_ref,
):
    local_pairs, chunk, _ = doubles_ref.shape

    @pl.when(pl.program_id(0) == 0)
    def _():
        window_ref[...] = singles_ref[:, :128].astype(jnp.float32).T[:NWIN].astype(jnp.bfloat16)

    dressed = vir_ref[0].astype(jnp.float32) - jnp.dot(
        window_ref[...], occ_ref[0], preferred_element_type=jnp.float32
    )
    dressed_ref[...] = jnp.broadcast_to(dressed.astype(jnp.bfloat16)[None], dressed_ref.shape)

    @pl.when(pl.program_id(0) == 0)
    def _():
        aux = place_ref[0]
        singles = singles_ref[...]
        occ = singles.shape[0]
        ids = lax.broadcasted_iota(jnp.int32, (occ, 128), 0)
        lane = lax.broadcasted_iota(jnp.int32, (occ, 128), 1)
        first = jnp.zeros((occ, 128), jnp.float32)
        for pair in range(local_pairs):
            first = jnp.where((lane == pair) & (ids == pairs_ref[pair, 0]), 1.0, first)
        cols_ref[...] = lax.dot_general(
            singles, first.astype(jnp.bfloat16), (((0,), (0,)), ((), ())), preferred_element_type=jnp.float32
        )
        cols = cols_ref[pl.ds(pl.multiple_of(aux * chunk, chunk), chunk), :]
        ids = lax.broadcasted_iota(jnp.int32, (16, occ), 1)
        row = lax.broadcasted_iota(jnp.int32, (16, occ), 0)
        second = jnp.zeros((16, occ), jnp.float32)
        for pair in range(local_pairs):
            second = jnp.where((row == pair) & (ids == pairs_ref[pair, 1]), 1.0, second)
        rows = jnp.dot(second.astype(jnp.bfloat16), singles, preferred_element_type=jnp.float32)
        for pair in range(local_pairs):
            outer = cols[:, pair : pair + 1] * rows[pair : pair + 1, :]
            tau_ref[place_ref[1], pair] = (doubles_ref[pair].astype(jnp.float32) + outer).astype(jnp.bfloat16)
        lane = lax.broadcasted_iota(jnp.int32, (1, 128), 1)
        vir = jnp.zeros((1, 128), jnp.float32)
        for b in range(NWIN):
            vir = jnp.where(lane == b, vir_energy_ref[b], vir)
        for pair in range(local_pairs):
            energy = occ_energy_ref[pairs_ref[pair, 0]] + occ_energy_ref[pairs_ref[pair, 1]]
            value = (energy - vir_energy_ref[aux]) - vir
            denominator_ref[pair : pair + 1] = jnp.where(lane < NWIN, value, 1.0)


def start(doubles, singles, vir_slabs, occ_slabs, occ_energy, vir_energy, pair_list, aux, zh):
    local_pairs, chunk, virt = doubles.shape
    slabs, occ, _ = occ_slabs.shape
    return pl.pallas_call(
        start_kernel,
        grid=(slabs,),
        out_shape=(
            jax.ShapeDtypeStruct((4, slabs * NWIN, virt), jnp.bfloat16),
            jax.ShapeDtypeStruct((2, local_pairs, chunk, virt), jnp.bfloat16),
            jax.ShapeDtypeStruct((local_pairs, 128), jnp.float32),
        ),
        in_specs=[
            SMEM, SMEM, SMEM, SMEM,
            pl.BlockSpec(doubles.shape, lambda q: (0, 0, 0)),
            pl.BlockSpec(singles.shape, lambda q: (0, 0)),
            pl.BlockSpec((1, NWIN, virt), lambda q: (q, 0, 0)),
            pl.BlockSpec((1, occ, virt), lambda q: (q, 0, 0)),
        ],
        out_specs=(
            pl.BlockSpec((4, NWIN, virt), lambda q: (0, q, 0)),
            pl.BlockSpec((2, local_pairs, chunk, virt), lambda q: (0, 0, 0, 0)),
            pl.BlockSpec((local_pairs, 128), lambda q: (0, 0)),
        ),
        scratch_shapes=[pltpu.VMEM((NWIN, occ), jnp.bfloat16), pltpu.VMEM((virt, 128), jnp.float32)],
        cost_estimate=pl.CostEstimate(flops=slabs * NWIN * occ * virt * 2, bytes_accessed=3 << 20, transcendentals=0),
        name="start",
    )(pair_list, jnp.stack([aux, zh]), occ_energy, vir_energy, doubles, singles, vir_slabs, occ_slabs)


def gather_tau(y_ref, refs, tau_ref):
    for shift, ref in enumerate(refs):
        halves, pairs, chunk, _ = ref.shape
        base = lax.rem(y_ref[0] + shift, 4) * (halves * chunk)
        for half in range(halves):
            rows = pl.ds(pl.multiple_of(base + half * chunk, chunk), chunk)
            for pair in range(pairs):
                tau_ref[pair, rows, :] = ref[half, pair]


def add_block(slab_ref, tau_ref, gram_ref):
    slabs = slab_ref[...]
    groups = [slabs[s : s + GROUP] for s in range(0, BLOCK, GROUP)]
    for pair in range(tau_ref.shape[0]):
        half = jnp.dot(slabs, tau_ref[pair], preferred_element_type=jnp.float32).astype(jnp.bfloat16)
        total = gram_ref[pair]
        for number, group in enumerate(groups):
            rows = half[number * GROUP : (number + 1) * GROUP]
            total = total + lax.dot_general(
                rows, group, (((1,), (1,)), ((), ())), preferred_element_type=jnp.float32
            )
        gram_ref[pair] = total


def fold(gram):
    row = lax.broadcasted_iota(jnp.int32, (GROUP, GROUP), 0) // NWIN
    col = lax.broadcasted_iota(jnp.int32, (GROUP, GROUP), 1) // NWIN
    kept = jnp.where(row == col, gram, 0.0)
    folded = jnp.sum(kept.reshape(GROUP // NWIN, NWIN, GROUP), axis=0)
    folded = folded[:, :128] + folded[:, 128:]
    shift = 64
    while shift >= NWIN:
        folded = folded + pltpu.roll(folded, shift, 1)
        shift //= 2
    return folded


def ladder_step(y_ref, a_ref, b_ref, tau_refs, tau_ref, gram_ref):
    step = pl.program_id(0)
    half_way = pl.num_programs(0) // 2

    @pl.when(step == 0)
    def _():
        gram_ref[...] = jnp.zeros_like(gram_ref)
        gather_tau(y_ref, tau_refs, tau_ref)

    @pl.when(step < half_way)
    def _():
        add_block(a_ref, tau_ref, gram_ref)

    @pl.when(step >= half_way)
    def _():
        add_block(b_ref, tau_ref, gram_ref)


def first_kernel(place_ref, a_ref, b_ref, t0, t1, t2, t3, out_ref, tau_ref, gram_ref):
    ladder_step(place_ref, a_ref, b_ref, (t0, t1, t2, t3), tau_ref, gram_ref)

    @pl.when(pl.program_id(0) == pl.num_programs(0) - 1)
    def _():
        for pair in range(gram_ref.shape[0]):
            out_ref[pair] = fold(gram_ref[pair])


def second_kernel(
    place_ref, a_ref, b_ref, t0, t1, t2, t3, earlier_ref, doubles_ref, out_ref, tau_ref, gram_ref
):
    ladder_step(place_ref, a_ref, b_ref, (t0, t1, t2, t3), tau_ref, gram_ref)

    @pl.when(pl.program_id(0) == pl.num_programs(0) - 1)
    def _():
        lane = lax.broadcasted_iota(jnp.int32, (NWIN, 128), 1)
        with_doubles = (lane < 2 * NWIN) & (place_ref[1] == 0)
        for pair in range(gram_ref.shape[0]):
            residual = fold(gram_ref[pair]) + earlier_ref[pair]
            doubles = pltpu.roll(doubles_ref[pair].astype(jnp.float32)[:NWIN], NWIN, 1)
            row = jnp.where(lane < NWIN, residual, jnp.where(with_doubles, doubles, 0.0))
            for a in range(NWIN):
                out_ref[a, pair : pair + 1, :] = row[a : a + 1]


def ladder(slabs_a, slabs_b, taus, place, earlier=None, doubles=None):
    rows, virt = slabs_a.shape
    pairs = taus[0].shape[1]
    steps = rows // BLOCK
    whole = pl.BlockSpec(taus[0].shape, lambda i: (0, 0, 0, 0))
    specs = [
        SMEM,
        pl.BlockSpec((BLOCK, virt), lambda i: (jnp.minimum(i, steps - 1), 0)),
        pl.BlockSpec((BLOCK, virt), lambda i: (jnp.maximum(i - steps, 0), 0)),
    ] + [whole] * 4
    operands = [place, slabs_a, slabs_b, *taus]
    if earlier is None:
        kernel, out = first_kernel, (pairs, NWIN, 128)
    else:
        kernel, out = second_kernel, (NWIN, pairs, 128)
        specs += [pl.BlockSpec(earlier.shape, lambda i: (0, 0, 0)), pl.BlockSpec((pairs, 16, 128), lambda i: (0, 0, 0))]
        operands += [earlier, doubles]
    return pl.pallas_call(
        kernel,
        out_shape=jax.ShapeDtypeStruct(out, jnp.float32),
        grid=(2 * steps,),
        in_specs=specs,
        out_specs=pl.BlockSpec(out, lambda i: (0, 0, 0)),
        scratch_shapes=[
            pltpu.VMEM((pairs, virt, virt), jnp.bfloat16),
            pltpu.VMEM((pairs, GROUP, GROUP), jnp.float32),
        ],
        cost_estimate=pl.CostEstimate(
            flops=pairs * rows * virt * (virt + GROUP) * 4,
            bytes_accessed=4 * rows * virt + 2 * pairs * virt * virt,
            transcendentals=0,
        ),
        name="ladder",
    )(*operands)


def last_kernel(parts_ref, denominator_ref, out_ref):
    total = jnp.sum(parts_ref[...], axis=0)
    value = pltpu.roll(total, 128 - NWIN, 1) + total / denominator_ref[...]
    out_ref[...] = value[:, :NWIN]


def last(parts, denominator):
    return pl.pallas_call(
        last_kernel,
        out_shape=jax.ShapeDtypeStruct((parts.shape[1], NWIN), jnp.float32),
        in_specs=[VMEM, VMEM],
        out_specs=VMEM,
        name="last",
    )(parts, denominator)


def exchange(copies, axis):
    return lax.all_to_all(copies, axis, split_axis=0, concat_axis=0, tiled=True)


def spread(value, axis):
    return exchange(jnp.broadcast_to(value[None], (lax.axis_size(axis),) + value.shape), axis)


def body(doubles, singles, vir_slabs, occ_slabs, occ_energy, vir_energy, pair_list):
    virt = doubles.shape[2]
    y, zh = lax.axis_index("y"), lax.axis_index("zh")
    aux = y * 2 + zh
    copies, tau, denominator = start(doubles, singles, vir_slabs, occ_slabs, occ_energy, vir_energy, pair_list, aux, zh)
    dressed = exchange(copies, "zm").reshape(-1, virt)
    own_tau = lax.dynamic_index_in_dim(tau, zh, 0, keepdims=False)
    other = lax.ppermute(own_tau, "zh", SWAP)
    first = spread(dressed, "x").reshape(-1, virt)
    dressed_next = lax.ppermute(dressed, "zb", SWAP)
    tau = lax.dynamic_update_index_in_dim(tau, other, 1 - zh, 0)
    below = lax.ppermute(tau, "y", UP)
    above = lax.ppermute(tau, "y", DOWN)
    second = spread(dressed_next, "x").reshape(-1, virt)
    first_other = lax.ppermute(first, "k", SWAP)
    far = lax.ppermute(below, "y", UP)
    second_other = lax.ppermute(second, "k", SWAP)
    place = jnp.stack([y, aux])
    taus = (tau, above, far, below)
    parts = ladder(first, first_other, taus, place)
    parts = ladder(second, second_other, taus, place, parts, doubles)
    parts = exchange(parts, AUX)
    return last(parts, denominator)[:, None, :]


def solution(mesh):
    fine = Mesh(mesh.devices.reshape(4, 2, 4, 2, 4, 2), PAIR + AUX)
    placed = (
        P(PAIR, AUX, None),
        P(),
        P(AUX + PAIR, None, None),
        P(AUX + PAIR, None, None),
        P(),
        P(),
        P(PAIR, None),
    )
    return jax.shard_map(
        body, mesh=fine, in_specs=placed, out_specs=P(PAIR, AUX, None), check_vma=False
    )
```

profile of v0, /device:TPU:66, one launch (start us, length us, event | category | flops | bytes accessed | tf_op | source)
XLA Modules:
  0.0 145.5 jit_solution(9805661959470372678)
XLA Ops:
  0.6 6.5 %start.1 = (bf16[4,64,512]{2,1,0:T(8,128)(2,1)}, bf16[2,2,64,512]{3,2,1,0:T(8,128)(2,1)}, f32[2,128]{1,0:T(2,128)}) custom-call(s32[2,2]{1,0:T(2,128)} %pairs_ref.1, s32[2]{0:T(128)} %pad_add_fusion.1.place_ref, f32[256]{0:T(256)} %occ_energy_ref.1, f32[8]{0:T(128)} %vir_energy_ref.1, bf16[2,64,512]{2,1,0:T(8,128)(2,1)} %doubles_ref.3, ...), custom_call_target="tpu_custom_call" | custom-call | flops 16777216 | bytes 3145728 | tf_op jit(solution)/shard_map/start/pallas_call | solution.py:72
  7.1 25.0 %all_to_all.20 = bf16[4,64,512]{2,1,0:T(8,128)(2,1)S(1)} all-to-all(bf16[4,64,512]{2,1,0:T(8,128)(2,1)} %get-tuple-element.8), channel_id=1, replica_groups=mesh['zm'=4,'zb'=2,'x'=4,'k'=2,'y'=4,'zh'=2] {'zm'}, dimensions={0} | all-to-all | bytes 524288 | tf_op jit(solution)/shard_map/all_to_all | solution.py:232
  32.1 1.1 broadcast_in_dim.20
  33.2 4.8 %all-to-all-start.2 = ((bf16[4,256,512]{2,1,0:T(8,128)(2,1)}), bf16[4,256,512]{2,1,0:T(8,128)(2,1)S(1)}, u32[]{:S(2)}, u32[]{:S(2)}) async-start(bf16[4,256,512]{2,1,0:T(8,128)(2,1)} %broadcast_in_dim.20), calls=%async_computation.2 | async-start | bytes 2097152 | tf_op jit(solution)/shard_map/all_to_all | solution.py:232
  38.0 3.2 %collective-permute-start = (bf16[256,512]{1,0:T(8,128)(2,1)S(1)}, bf16[256,512]{1,0:T(8,128)(2,1)S(1)}, u32[]{:S(2)}, u32[]{:S(2)}) collective-permute-start(bf16[256,512]{1,0:T(8,128)(2,1)S(1)} %bitcast.14), channel_id=1, source_target_pairs={{0,64},{64,0},{1,65},{65,1},{2,66},{66,2},{3,67},{67,3},{4,68},{68... | collective-permute-start | bytes 786440 | tf_op jit(solution)/shard_map/ppermute | solution.py:248
  41.2 5.3 %collective-permute-done = bf16[256,512]{1,0:T(8,128)(2,1)S(1)} collective-permute-done((bf16[256,512]{1,0:T(8,128)(2,1)S(1)}, bf16[256,512]{1,0:T(8,128)(2,1)S(1)}, u32[]{:S(2)}, u32[]{:S(2)}) %collective-permute-start) | collective-permute-done | bytes 262176 | tf_op jit(solution)/shard_map/ppermute | solution.py:248
  46.4 4.1 %all-to-all-done.2 = bf16[4,256,512]{2,1,0:T(8,128)(2,1)S(1)} async-done(((bf16[4,256,512]{2,1,0:T(8,128)(2,1)}), bf16[4,256,512]{2,1,0:T(8,128)(2,1)S(1)}, u32[]{:S(2)}, u32[]{:S(2)}) %all-to-all-start.2) | async-done | bytes 1048608 | tf_op jit(solution)/shard_map/all_to_all | solution.py:232
  50.5 1.1 broadcast_in_dim.18
  51.7 4.9 %all-to-all-start.1 = ((bf16[4,256,512]{2,1,0:T(8,128)(2,1)}), bf16[4,256,512]{2,1,0:T(8,128)(2,1)S(1)}, u32[]{:S(2)}, u32[]{:S(2)}) async-start(bf16[4,256,512]{2,1,0:T(8,128)(2,1)} %broadcast_in_dim.18), calls=%async_computation.1 | async-start | bytes 2097152 | tf_op jit(solution)/shard_map/all_to_all | solution.py:232
  56.6 1.9 %collective-permute-start.6 = (bf16[1024,512]{1,0:T(8,128)(2,1)S(1)}, bf16[1024,512]{1,0:T(8,128)(2,1)}, u32[]{:S(2)}, u32[]{:S(2)}) collective-permute-start(bf16[1024,512]{1,0:T(8,128)(2,1)S(1)} %bitcast.15), channel_id=1, source_target_pairs={{0,8},{8,0},{1,9},{9,1},{2,10},{10,2},{3,11},{11,3},{4,12},{12,4},... | collective-permute-start | bytes 3145736 | tf_op jit(solution)/shard_map/ppermute | solution.py:253
  58.6 9.6 %collective-permute-start.2 = (bf16[2,64,512]{2,1,0:T(8,128)(2,1)S(1)}, bf16[2,64,512]{2,1,0:T(8,128)(2,1)S(1)}, u32[]{:S(2)}, u32[]{:S(2)}) collective-permute-start(bf16[2,64,512]{2,1,0:T(8,128)(2,1)S(1)} %dynamic-slice_bitcast_fusion), channel_id=1, source_target_pairs={{0,1},{1,0},{2,3},{3,2},{4,5},{5,4},{6,7},{7,6},{8,9},{9,8},{10,11... | collective-permute-start | bytes 393224 | tf_op jit(solution)/shard_map/ppermute | solution.py:246
  68.3 2.0 %collective-permute-start.1 = (bf16[1024,512]{1,0:T(8,128)(2,1)S(1)}, bf16[1024,512]{1,0:T(8,128)(2,1)}, u32[]{:S(2)}, u32[]{:S(2)}) collective-permute-start(bf16[1024,512]{1,0:T(8,128)(2,1)S(1)} %bitcast.17), channel_id=1, source_target_pairs={{0,8},{8,0},{1,9},{9,1},{2,10},{10,2},{3,11},{11,3},{4,12},{12,4},... | collective-permute-start | bytes 3145736 | tf_op jit(solution)/shard_map/ppermute | solution.py:255
  70.3 13.2 %collective-permute-done.2 = bf16[2,64,512]{2,1,0:T(8,128)(2,1)S(1)} collective-permute-done((bf16[2,64,512]{2,1,0:T(8,128)(2,1)S(1)}, bf16[2,64,512]{2,1,0:T(8,128)(2,1)S(1)}, u32[]{:S(2)}, u32[]{:S(2)}) %collective-permute-start.2) | collective-permute-done | bytes 131104 | tf_op jit(solution)/shard_map/ppermute | solution.py:246
  83.5 3.5 %collective-permute-start.4 = (bf16[2,2,64,512]{3,2,1,0:T(8,128)(2,1)S(1)}, bf16[2,2,64,512]{3,2,1,0:T(8,128)(2,1)S(1)}, u32[]{:S(2)}, u32[]{:S(2)}) collective-permute-start(bf16[2,2,64,512]{3,2,1,0:T(8,128)(2,1)S(1)} %bitcast_dynamic-update-slice_fusion.t0), channel_id=1, source_target_pairs={{0,2},{2,4},{4,6},{6,0},{1,3},{3,5},{5,7},{7,1},{8,10},{10,12},{12... | collective-permute-start | bytes 786440 | tf_op jit(solution)/shard_map/ppermute | solution.py:250
  87.0 3.6 %collective-permute-start.3 = (bf16[2,2,64,512]{3,2,1,0:T(8,128)(2,1)S(1)}, bf16[2,2,64,512]{3,2,1,0:T(8,128)(2,1)S(1)}, u32[]{:S(2)}, u32[]{:S(2)}) collective-permute-start(bf16[2,2,64,512]{3,2,1,0:T(8,128)(2,1)S(1)} %bitcast_dynamic-update-slice_fusion.t0), channel_id=1, source_target_pairs={{0,6},{2,0},{4,2},{6,4},{1,7},{3,1},{5,3},{7,5},{8,14},{10,8},{12,... | collective-permute-start | bytes 786440 | tf_op jit(solution)/shard_map/ppermute | solution.py:251
  90.6 4.0 %collective-permute-done.4.t3 = bf16[2,2,64,512]{3,2,1,0:T(8,128)(2,1)S(1)} collective-permute-done((bf16[2,2,64,512]{3,2,1,0:T(8,128)(2,1)S(1)}, bf16[2,2,64,512]{3,2,1,0:T(8,128)(2,1)S(1)}, u32[]{:S(2)}, u32[]{:S(2)}) %collective-permute-start.4) | collective-permute-done | bytes 262176 | tf_op jit(solution)/shard_map/ppermute | solution.py:250
  94.6 2.2 %collective-permute-start.5 = (bf16[2,2,64,512]{3,2,1,0:T(8,128)(2,1)S(1)}, bf16[2,2,64,512]{3,2,1,0:T(8,128)(2,1)S(1)}, u32[]{:S(2)}, u32[]{:S(2)}) collective-permute-start(bf16[2,2,64,512]{3,2,1,0:T(8,128)(2,1)S(1)} %collective-permute-done.4.t3), channel_id=1, source_target_pairs={{0,2},{2,4},{4,6},{6,0},{1,3},{3,5},{5,7},{7,1},{8,10},{10,12},{12... | collective-permute-start | bytes 786440 | tf_op jit(solution)/shard_map/ppermute | solution.py:254
  96.8 0.6 pad_add_fusion.place_ref
  97.4 7.4 %collective-permute-done.5.t2 = bf16[2,2,64,512]{3,2,1,0:T(8,128)(2,1)S(1)} collective-permute-done((bf16[2,2,64,512]{3,2,1,0:T(8,128)(2,1)S(1)}, bf16[2,2,64,512]{3,2,1,0:T(8,128)(2,1)S(1)}, u32[]{:S(2)}, u32[]{:S(2)}) %collective-permute-start.5) | collective-permute-done | bytes 262176 | tf_op jit(solution)/shard_map/ppermute | solution.py:254
  104.8 0.7 copy-done.6
  105.4 7.4 %ladder.2.earlier_ref = f32[2,8,128]{2,1,0:T(8,128)} custom-call(s32[2]{0:T(128)} %pad_add_fusion.place_ref, bf16[1024,512]{1,0:T(8,128)(2,1)} %bitcast.16, bf16[1024,512]{1,0:T(8,128)(2,1)} %collective-permute-done.6.b_ref, bf16[2,2,64,512]{3,2,1,0:T(8,128)(2,1)} %copy-done.3, bf16[2,2,64,512]{3,2,1,0:T(8,128)(2,1)} %copy-done.5, ...), custom_call_target="tpu_custom_call" | custom-call | flops 3221225472 | bytes 3145728 | tf_op jit(solution)/shard_map/ladder/pallas_call | solution.py:196
  112.9 7.5 %ladder.3 = f32[8,2,128]{2,1,0:T(2,128)} custom-call(s32[2]{0:T(128)} %pad_add_fusion.place_ref, bf16[1024,512]{1,0:T(8,128)(2,1)} %bitcast.18, bf16[1024,512]{1,0:T(8,128)(2,1)} %collective-permute-done.1.b_ref, bf16[2,2,64,512]{3,2,1,0:T(8,128)(2,1)} %copy-done.3, bf16[2,2,64,512]{3,2,1,0:T(8,128)(2,1)} %copy-done.5, bf16[2,2,64,512]{3,2,1,0:T(8,128)(2,1)} %copy-done.6, ...), custom_call_target="tpu_custom_call" | custom-call | flops 3221225472 | bytes 3145728 | tf_op jit(solution)/shard_map/ladder/pallas_call | solution.py:196
  120.4 23.8 %all_to_all.21.parts_ref = f32[8,2,128]{2,1,0:T(2,128)} all-to-all(f32[8,2,128]{2,1,0:T(2,128)} %ladder.3), channel_id=1, replica_groups=mesh['zm'=4,'zb'=2,'x'=4,'k'=2,'y'=4,'zh'=2] {'y','zh'}, dimensions={0} | all-to-all | bytes 16384 | tf_op jit(solution)/shard_map/all_to_all | solution.py:232
  144.2 1.4 last.1
  (20 shorter events, 0.8 us)
Async XLA Ops:
  33.2 17.4 %all-to-all-start.2 = ((bf16[4,256,512]{2,1,0:T(8,128)(2,1)}), bf16[4,256,512]{2,1,0:T(8,128)(2,1)S(1)}, u32[]{:S(2)}, u32[]{:S(2)}) async-start(bf16[4,256,512]{2,1,0:T(8,128)(2,1)} %broadcast_in_dim.20), calls=%async_computation.2 | async-start | bytes 2097152 | tf_op jit(solution)/shard_map/all_to_all | solution.py:232
  38.0 20.6 %copy-start.2 = (bf16[2,2,64,512]{3,2,1,0:T(8,128)(2,1)S(1)}, bf16[2,2,64,512]{3,2,1,0:T(8,128)(2,1)}, u32[]{:S(2)}) copy-start(bf16[2,2,64,512]{3,2,1,0:T(8,128)(2,1)} %get-tuple-element.9) | copy-start | bytes 786436
  38.0 8.4 %collective-permute-start = (bf16[256,512]{1,0:T(8,128)(2,1)S(1)}, bf16[256,512]{1,0:T(8,128)(2,1)S(1)}, u32[]{:S(2)}, u32[]{:S(2)}) collective-permute-start(bf16[256,512]{1,0:T(8,128)(2,1)S(1)} %bitcast.14), channel_id=1, source_target_pairs={{0,64},{64,0},{1,65},{65,1},{2,66},{66,2},{3,67},{67,3},{4,68},{68... | collective-permute-start | bytes 786440 | tf_op jit(solution)/shard_map/ppermute | solution.py:248
  50.5 54.2 %copy-start = (bf16[4,256,512]{2,1,0:T(8,128)(2,1)}, bf16[4,256,512]{2,1,0:T(8,128)(2,1)S(1)}, u32[]{:S(2)}) copy-start(bf16[4,256,512]{2,1,0:T(8,128)(2,1)S(1)} %all-to-all-done.2) | copy-start | bytes 3145732
  51.7 16.6 %all-to-all-start.1 = ((bf16[4,256,512]{2,1,0:T(8,128)(2,1)}), bf16[4,256,512]{2,1,0:T(8,128)(2,1)S(1)}, u32[]{:S(2)}, u32[]{:S(2)}) async-start(bf16[4,256,512]{2,1,0:T(8,128)(2,1)} %broadcast_in_dim.18), calls=%async_computation.1 | async-start | bytes 2097152 | tf_op jit(solution)/shard_map/all_to_all | solution.py:232
  56.6 48.1 %collective-permute-start.6 = (bf16[1024,512]{1,0:T(8,128)(2,1)S(1)}, bf16[1024,512]{1,0:T(8,128)(2,1)}, u32[]{:S(2)}, u32[]{:S(2)}) collective-permute-start(bf16[1024,512]{1,0:T(8,128)(2,1)S(1)} %bitcast.15), channel_id=1, source_target_pairs={{0,8},{8,0},{1,9},{9,1},{2,10},{10,2},{3,11},{11,3},{4,12},{12,4},... | collective-permute-start | bytes 3145736 | tf_op jit(solution)/shard_map/ppermute | solution.py:253
  58.6 24.9 %collective-permute-start.2 = (bf16[2,64,512]{2,1,0:T(8,128)(2,1)S(1)}, bf16[2,64,512]{2,1,0:T(8,128)(2,1)S(1)}, u32[]{:S(2)}, u32[]{:S(2)}) collective-permute-start(bf16[2,64,512]{2,1,0:T(8,128)(2,1)S(1)} %dynamic-slice_bitcast_fusion), channel_id=1, source_target_pairs={{0,1},{1,0},{2,3},{3,2},{4,5},{5,4},{6,7},{7,6},{8,9},{9,8},{10,11... | collective-permute-start | bytes 393224 | tf_op jit(solution)/shard_map/ppermute | solution.py:246
  68.3 44.5 %copy-start.1 = (bf16[4,256,512]{2,1,0:T(8,128)(2,1)}, bf16[4,256,512]{2,1,0:T(8,128)(2,1)S(1)}, u32[]{:S(2)}) copy-start(bf16[4,256,512]{2,1,0:T(8,128)(2,1)S(1)} %all-to-all-done.1) | copy-start | bytes 3145732
  68.3 44.5 %collective-permute-start.1 = (bf16[1024,512]{1,0:T(8,128)(2,1)S(1)}, bf16[1024,512]{1,0:T(8,128)(2,1)}, u32[]{:S(2)}, u32[]{:S(2)}) collective-permute-start(bf16[1024,512]{1,0:T(8,128)(2,1)S(1)} %bitcast.17), channel_id=1, source_target_pairs={{0,8},{8,0},{1,9},{9,1},{2,10},{10,2},{3,11},{11,3},{4,12},{12,4},... | collective-permute-start | bytes 3145736 | tf_op jit(solution)/shard_map/ppermute | solution.py:255
  83.5 21.2 %copy-start.3 = (bf16[2,2,64,512]{3,2,1,0:T(8,128)(2,1)}, bf16[2,2,64,512]{3,2,1,0:T(8,128)(2,1)S(1)}, u32[]{:S(2)}) copy-start(bf16[2,2,64,512]{3,2,1,0:T(8,128)(2,1)S(1)} %bitcast_dynamic-update-slice_fusion.t0) | copy-start | bytes 786436
  83.5 11.0 %collective-permute-start.4 = (bf16[2,2,64,512]{3,2,1,0:T(8,128)(2,1)S(1)}, bf16[2,2,64,512]{3,2,1,0:T(8,128)(2,1)S(1)}, u32[]{:S(2)}, u32[]{:S(2)}) collective-permute-start(bf16[2,2,64,512]{3,2,1,0:T(8,128)(2,1)S(1)} %bitcast_dynamic-update-slice_fusion.t0), channel_id=1, source_target_pairs={{0,2},{2,4},{4,6},{6,0},{1,3},{3,5},{5,7},{7,1},{8,10},{10,12},{12... | collective-permute-start | bytes 786440 | tf_op jit(solution)/shard_map/ppermute | solution.py:250
  87.0 10.3 %collective-permute-start.3 = (bf16[2,2,64,512]{3,2,1,0:T(8,128)(2,1)S(1)}, bf16[2,2,64,512]{3,2,1,0:T(8,128)(2,1)S(1)}, u32[]{:S(2)}, u32[]{:S(2)}) collective-permute-start(bf16[2,2,64,512]{3,2,1,0:T(8,128)(2,1)S(1)} %bitcast_dynamic-update-slice_fusion.t0), channel_id=1, source_target_pairs={{0,6},{2,0},{4,2},{6,4},{1,7},{3,1},{5,3},{7,5},{8,14},{10,8},{12,... | collective-permute-start | bytes 786440 | tf_op jit(solution)/shard_map/ppermute | solution.py:251
  94.6 10.2 %copy-start.4 = (bf16[2,2,64,512]{3,2,1,0:T(8,128)(2,1)}, bf16[2,2,64,512]{3,2,1,0:T(8,128)(2,1)S(1)}, u32[]{:S(2)}) copy-start(bf16[2,2,64,512]{3,2,1,0:T(8,128)(2,1)S(1)} %collective-permute-done.4.t3) | copy-start | bytes 786436
  94.6 10.2 %collective-permute-start.5 = (bf16[2,2,64,512]{3,2,1,0:T(8,128)(2,1)S(1)}, bf16[2,2,64,512]{3,2,1,0:T(8,128)(2,1)S(1)}, u32[]{:S(2)}, u32[]{:S(2)}) collective-permute-start(bf16[2,2,64,512]{3,2,1,0:T(8,128)(2,1)S(1)} %collective-permute-done.4.t3), channel_id=1, source_target_pairs={{0,2},{2,4},{4,6},{6,0},{1,3},{3,5},{5,7},{7,1},{8,10},{10,12},{12... | collective-permute-start | bytes 786440 | tf_op jit(solution)/shard_map/ppermute | solution.py:254
  97.4 7.4 %copy-start.5 = (bf16[2,2,64,512]{3,2,1,0:T(8,128)(2,1)}, bf16[2,2,64,512]{3,2,1,0:T(8,128)(2,1)S(1)}, u32[]{:S(2)}) copy-start(bf16[2,2,64,512]{3,2,1,0:T(8,128)(2,1)S(1)} %collective-permute-done.3.t1) | copy-start | bytes 786436
  104.7 0.7 copy-start.6
where the time goes:
time: 146 us
  blocking collectives  48.8 us (33%)
  starting transfers between devices  35.7 us (24%)
  waiting for transfers between devices  34.1 us (23%)
  Pallas kernels  22.8 us (16%)
  local copies, waits for them, and re-layouts  2.91 us (2%)
    all_to_all x2, blocking collectives, exchange(): return lax.all_to_all(copies, axis, split_axis=0, concat_axis=0, tiled=True)  48.8 us
    pallas_call x2, Pallas kernels, ladder(): pl.pallas_call(kernel, out_shape=jax.ShapeDtypeStruct(out, jnp.float32),...  14.9 us
    ppermute x1, waiting for transfers between devices, body(): other = lax.ppermute(own_tau, 'zh', SWAP)  13.2 us
    all_to_all x2, starting transfers between devices, exchange(): return lax.all_to_all(copies, axis, split_axis=0, concat_axis=0, tiled=True)  9.76 us
    ppermute x1, starting transfers between devices, body(): other = lax.ppermute(own_tau, 'zh', SWAP)  9.59 us
    ppermute x1, waiting for transfers between devices, body(): far = lax.ppermute(below, 'y', UP)  7.37 us
    pallas_call x1, Pallas kernels, start(): pl.pallas_call(start_kernel, grid=(slabs,), out_shape=(jax.ShapeDtypeStru...  6.54 us
    ppermute x1, waiting for transfers between devices, body(): dressed_next = lax.ppermute(dressed, 'zb', SWAP)  5.25 us
  transfers between devices with their start and end apart: 9, of which 6 were waited for; matrix products, arithmetic and copies ran while one was open for 0% of the time, Pallas kernels for 5%

commit v1 on v0

v1 whole, which is shorter than its diff:
```python
import jax
import jax.numpy as jnp
from jax import lax
from jax.experimental import pallas as pl
from jax.experimental.pallas import tpu as pltpu
from jax.sharding import Mesh, PartitionSpec as P


NWIN = 8
GROUP = 256
BLOCK = 512
PAIR = ("zm", "zb", "x", "k")
AUX = ("y", "zh")
SWAP = [(0, 1), (1, 0)]
UP = [(i, (i + 1) % 4) for i in range(4)]
DOWN = [(i, (i + 3) % 4) for i in range(4)]
SMEM = pl.BlockSpec(memory_space=pltpu.SMEM)
VMEM = pl.BlockSpec(memory_space=pltpu.VMEM)


def start_kernel(
    pairs_ref, occ_energy_ref, vir_energy_ref, doubles_ref, singles_ref, vir_ref, occ_ref,
    dressed_ref, own_ref, tau_ref, denominator_ref, cols_ref,
):
    local_pairs, chunk, _ = doubles_ref.shape
    zh = lax.axis_index("zh")
    aux = lax.axis_index("y") * 2 + zh
    singles = singles_ref[...]
    occ = singles.shape[0]
    window = singles[:, :128].astype(jnp.float32).T[:NWIN].astype(jnp.bfloat16)
    for slab in range(occ_ref.shape[0]):
        dressed = vir_ref[slab].astype(jnp.float32) - jnp.dot(
            window, occ_ref[slab], preferred_element_type=jnp.float32
        )
        dressed = dressed.astype(jnp.bfloat16)
        for copy in range(dressed_ref.shape[0]):
            dressed_ref[copy, slab * NWIN : (slab + 1) * NWIN, :] = dressed
    ids = lax.broadcasted_iota(jnp.int32, (occ, 128), 0)
    lane = lax.broadcasted_iota(jnp.int32, (occ, 128), 1)
    first = jnp.zeros((occ, 128), jnp.float32)
    for pair in range(local_pairs):
        first = jnp.where((lane == pair) & (ids == pairs_ref[pair, 0]), 1.0, first)
    cols_ref[...] = lax.dot_general(
        singles, first.astype(jnp.bfloat16), (((0,), (0,)), ((), ())), preferred_element_type=jnp.float32
    )
    cols = cols_ref[pl.ds(pl.multiple_of(aux * chunk, chunk), chunk), :]
    ids = lax.broadcasted_iota(jnp.int32, (16, occ), 1)
    row = lax.broadcasted_iota(jnp.int32, (16, occ), 0)
    second = jnp.zeros((16, occ), jnp.float32)
    for pair in range(local_pairs):
        second = jnp.where((row == pair) & (ids == pairs_ref[pair, 1]), 1.0, second)
    rows = jnp.dot(second.astype(jnp.bfloat16), singles, preferred_element_type=jnp.float32)
    for pair in range(local_pairs):
        outer = cols[:, pair : pair + 1] * rows[pair : pair + 1, :]
        tau = (doubles_ref[pair].astype(jnp.float32) + outer).astype(jnp.bfloat16)
        own_ref[pair] = tau
        tau_ref[zh, pair] = tau
    lane = lax.broadcasted_iota(jnp.int32, (1, 128), 1)
    vir = jnp.zeros((1, 128), jnp.float32)
    for b in range(NWIN):
        vir = jnp.where(lane == b, vir_energy_ref[b], vir)
    for pair in range(local_pairs):
        energy = occ_energy_ref[pairs_ref[pair, 0]] + occ_energy_ref[pairs_ref[pair, 1]]
        value = (energy - vir_energy_ref[aux]) - vir
        denominator_ref[pair : pair + 1] = jnp.where(lane < NWIN, value, 1.0)


def start(doubles, singles, vir_slabs, occ_slabs, occ_energy, vir_energy, pair_list):
    local_pairs, chunk, virt = doubles.shape
    slabs, occ, _ = occ_slabs.shape
    return pl.pallas_call(
        start_kernel,
        out_shape=(
            jax.ShapeDtypeStruct((4, slabs * NWIN, virt), jnp.bfloat16),
            jax.ShapeDtypeStruct((local_pairs, chunk, virt), jnp.bfloat16),
            jax.ShapeDtypeStruct((2, local_pairs, chunk, virt), jnp.bfloat16),
            jax.ShapeDtypeStruct((local_pairs, 128), jnp.float32),
        ),
        in_specs=[SMEM] * 3 + [VMEM] * 4,
        out_specs=(VMEM,) * 4,
        scratch_shapes=[pltpu.VMEM((virt, 128), jnp.float32)],
        cost_estimate=pl.CostEstimate(flops=slabs * NWIN * occ * virt * 2, bytes_accessed=3 << 20, transcendentals=0),
        name="start",
    )(pair_list, occ_energy, vir_energy, doubles, singles, vir_slabs, occ_slabs)


def gather_tau(refs, tau_ref):
    y = lax.axis_index("y")
    for shift, ref in enumerate(refs):
        halves, pairs, chunk, _ = ref.shape
        base = lax.rem(y + shift, 4) * (halves * chunk)
        for half in range(halves):
            rows = pl.ds(pl.multiple_of(base + half * chunk, chunk), chunk)
            for pair in range(pairs):
                tau_ref[pair, rows, :] = ref[half, pair]


def add_block(slab_ref, tau_ref, gram_ref):
    slabs = slab_ref[...]
    groups = [slabs[s : s + GROUP] for s in range(0, BLOCK, GROUP)]
    for pair in range(tau_ref.shape[0]):
        half = jnp.dot(slabs, tau_ref[pair], preferred_element_type=jnp.float32).astype(jnp.bfloat16)
        total = gram_ref[pair]
        for number, group in enumerate(groups):
            rows = half[number * GROUP : (number + 1) * GROUP]
            total = total + lax.dot_general(
                rows, group, (((1,), (1,)), ((), ())), preferred_element_type=jnp.float32
            )
        gram_ref[pair] = total


def fold(gram):
    row = lax.broadcasted_iota(jnp.int32, (GROUP, GROUP), 0) // NWIN
    col = lax.broadcasted_iota(jnp.int32, (GROUP, GROUP), 1) // NWIN
    kept = jnp.where(row == col, gram, 0.0)
    folded = jnp.sum(kept.reshape(GROUP // NWIN, NWIN, GROUP), axis=0)
    folded = folded[:, :128] + folded[:, 128:]
    shift = 64
    while shift >= NWIN:
        folded = folded + pltpu.roll(folded, shift, 1)
        shift //= 2
    return folded


def ladder_step(slab_ref, tau_refs, tau_ref, gram_ref):
    @pl.when(pl.program_id(0) == 0)
    def _():
        gram_ref[...] = jnp.zeros_like(gram_ref)
        gather_tau(tau_refs, tau_ref)

    add_block(slab_ref, tau_ref, gram_ref)


def first_kernel(slab_ref, t0, t1, t2, t3, out_ref, tau_ref, gram_ref):
    ladder_step(slab_ref, (t0, t1, t2, t3), tau_ref, gram_ref)

    @pl.when(pl.program_id(0) == pl.num_programs(0) - 1)
    def _():
        for pair in range(gram_ref.shape[0]):
            out_ref[pair] = fold(gram_ref[pair])


def second_kernel(slab_ref, t0, t1, t2, t3, earlier_ref, doubles_ref, out_ref, tau_ref, gram_ref):
    ladder_step(slab_ref, (t0, t1, t2, t3), tau_ref, gram_ref)

    @pl.when(pl.program_id(0) == pl.num_programs(0) - 1)
    def _():
        lane = lax.broadcasted_iota(jnp.int32, (NWIN, 128), 1)
        holds = (lax.axis_index("y") == 0) & (lax.axis_index("zh") == 0)
        with_doubles = (lane < 2 * NWIN) & holds
        for pair in range(gram_ref.shape[0]):
            residual = fold(gram_ref[pair]) + earlier_ref[pair]
            doubles = pltpu.roll(doubles_ref[pair].astype(jnp.float32)[:NWIN], NWIN, 1)
            row = jnp.where(lane < NWIN, residual, jnp.where(with_doubles, doubles, 0.0))
            for a in range(NWIN):
                out_ref[a, pair : pair + 1, :] = row[a : a + 1]


def ladder(slabs, taus, earlier=None, doubles=None):
    rows, virt = slabs.shape
    pairs = taus[0].shape[1]
    whole = pl.BlockSpec(taus[0].shape, lambda i: (0, 0, 0, 0))
    specs = [pl.BlockSpec((BLOCK, virt), lambda i: (i, 0))] + [whole] * 4
    operands = [slabs, *taus]
    if earlier is None:
        kernel, out = first_kernel, (pairs, NWIN, 128)
    else:
        kernel, out = second_kernel, (NWIN, pairs, 128)
        specs += [pl.BlockSpec(earlier.shape, lambda i: (0, 0, 0)), pl.BlockSpec((pairs, 16, 128), lambda i: (0, 0, 0))]
        operands += [earlier, doubles]
    return pl.pallas_call(
        kernel,
        out_shape=jax.ShapeDtypeStruct(out, jnp.float32),
        grid=(rows // BLOCK,),
        in_specs=specs,
        out_specs=pl.BlockSpec(out, lambda i: (0, 0, 0)),
        scratch_shapes=[
            pltpu.VMEM((pairs, virt, virt), jnp.bfloat16),
            pltpu.VMEM((pairs, GROUP, GROUP), jnp.float32),
        ],
        cost_estimate=pl.CostEstimate(
            flops=pairs * rows * virt * (virt + GROUP) * 2,
            bytes_accessed=2 * rows * virt + 2 * pairs * virt * virt,
            transcendentals=0,
        ),
        name="ladder",
    )(*operands)


def last_kernel(parts_ref, denominator_ref, out_ref):
    total = jnp.sum(parts_ref[...], axis=0)
    value = pltpu.roll(total, 128 - NWIN, 1) + total / denominator_ref[...]
    out_ref[...] = value[:, :NWIN]


def last(parts, denominator):
    return pl.pallas_call(
        last_kernel,
        out_shape=jax.ShapeDtypeStruct((parts.shape[1], NWIN), jnp.float32),
        in_specs=[VMEM, VMEM],
        out_specs=VMEM,
        name="last",
    )(parts, denominator)


def exchange(copies, axis):
    return lax.all_to_all(copies, axis, split_axis=0, concat_axis=0, tiled=True)


def spread(value, axis):
    return exchange(jnp.broadcast_to(value[None], (lax.axis_size(axis),) + value.shape), axis)


def body(doubles, singles, vir_slabs, occ_slabs, occ_energy, vir_energy, pair_list):
    virt = doubles.shape[2]
    zh = lax.axis_index("zh")
    copies, own, tau, denominator = start(doubles, singles, vir_slabs, occ_slabs, occ_energy, vir_energy, pair_list)
    dressed = exchange(copies, "zm").reshape(-1, virt)
    dressed_next = lax.ppermute(dressed, "zb", SWAP)
    other = lax.ppermute(own, "zh", SWAP)
    dressed = spread(jnp.stack([dressed, dressed_next]), "x").reshape(-1, virt)
    tau = lax.dynamic_update_index_in_dim(tau, other, 1 - zh, 0)
    below = lax.ppermute(tau, "y", UP)
    above = lax.ppermute(tau, "y", DOWN)
    far = lax.ppermute(below, "y", UP)
    dressed_other = lax.ppermute(dressed, "k", SWAP)
    taus = (tau, above, far, below)
    parts = ladder(dressed, taus)
    parts = ladder(dressed_other, taus, parts, doubles)
    parts = exchange(parts, AUX)
    return last(parts, denominator)[:, None, :]


def solution(mesh):
    fine = Mesh(mesh.devices.reshape(4, 2, 4, 2, 4, 2), PAIR + AUX)
    placed = (
        P(PAIR, AUX, None),
        P(),
        P(AUX + PAIR, None, None),
        P(AUX + PAIR, None, None),
        P(),
        P(),
        P(PAIR, None),
    )
    return jax.shard_map(
        body, mesh=fine, in_specs=placed, out_specs=P(PAIR, AUX, None), check_vma=False
    )
```

time: 146 us -> 152 us (1.041)
  the two profiles are of different devices: /device:TPU:66 before, /device:TPU:2 now
where the time goes in v1:
time: 152 us; the launch traced here: 151 us
  blocking collectives  84 us (55%)
  starting transfers between devices  24.6 us (16%)
  waiting for transfers between devices  22.9 us (15%)
  Pallas kernels  18.9 us (12%)
    all_to_all x3, blocking collectives, exchange(): return lax.all_to_all(copies, axis, split_axis=0, concat_axis=0, tiled=True)  84 us
    pallas_call x2, Pallas kernels, ladder(): pl.pallas_call(kernel, out_shape=jax.ShapeDtypeStruct(out, jnp.float32),...  14.3 us
    ppermute x1, starting transfers between devices, body(): other = lax.ppermute(own, 'zh', SWAP)  11.1 us
    ppermute x1, waiting for transfers between devices, body(): far = lax.ppermute(below, 'y', UP)  7.63 us
    ppermute x1, waiting for transfers between devices, body(): dressed_next = lax.ppermute(dressed, 'zb', SWAP)  5.83 us
    ppermute x1, waiting for transfers between devices, body(): other = lax.ppermute(own, 'zh', SWAP)  5.75 us
    ppermute x1, waiting for transfers between devices, body(): below = lax.ppermute(tau, 'y', UP)  3.65 us
    ppermute x1, starting transfers between devices, body(): above = lax.ppermute(tau, 'y', DOWN)  3.58 us
  transfers between devices with their start and end apart: 6, of which 4 were waited for; matrix products, arithmetic and copies ran while one was open for 0% of the time, Pallas kernels for 5%

profile of v1, /device:TPU:2, one launch (start us, length us, event | category | flops | bytes accessed | tf_op | source)
XLA Modules:
  0.0 151.5 jit_solution(5550826890921800078)
XLA Ops:
  0.0 3.2 %start.1 = (bf16[4,64,512]{2,1,0:T(8,128)(2,1)}, bf16[2,64,512]{2,1,0:T(8,128)(2,1)}, bf16[2,2,64,512]{3,2,1,0:T(8,128)(2,1)}, f32[2,128]{1,0:T(2,128)}) custom-call(s32[2,2]{1,0:T(2,128)} %pairs_ref.1, f32[256]{0:T(256)} %occ_energy_ref.1, f32[8]{0:T(128)} %vir_energy_ref.1, bf16[2,64,512]{2,1,0:T(8,128)(2,1)} %doubles_ref.3, bf16[256,512]{1,0:T(8,128)(2,1)} %singles_ref.1, ...), custom_call_target="tpu_custom_call" | custom-call | flops 16777216 | bytes 3145728 | tf_op jit(solution)/shard_map/start/pallas_call | solution.py:71
  3.2 28.7 %all_to_all.15 = bf16[4,64,512]{2,1,0:T(8,128)(2,1)S(1)} all-to-all(bf16[4,64,512]{2,1,0:T(8,128)(2,1)} %get-tuple-element.9), channel_id=1, replica_groups=mesh['zm'=4,'zb'=2,'x'=4,'k'=2,'y'=4,'zh'=2] {'zm'}, dimensions={0} | all-to-all | bytes 524288 | tf_op jit(solution)/shard_map/all_to_all | solution.py:207
  31.9 2.4 %collective-permute-start = (bf16[256,512]{1,0:T(8,128)(2,1)S(1)}, bf16[256,512]{1,0:T(8,128)(2,1)S(1)}, u32[]{:S(2)}, u32[]{:S(2)}) collective-permute-start(bf16[256,512]{1,0:T(8,128)(2,1)S(1)} %bitcast.11), channel_id=1, source_target_pairs={{0,64},{64,0},{1,65},{65,1},{2,66},{66,2},{3,67},{67,3},{4,68},{68... | collective-permute-start | bytes 786440 | tf_op jit(solution)/shard_map/ppermute | solution.py:219
  34.3 5.8 %collective-permute-done = bf16[256,512]{1,0:T(8,128)(2,1)S(1)} collective-permute-done((bf16[256,512]{1,0:T(8,128)(2,1)S(1)}, bf16[256,512]{1,0:T(8,128)(2,1)S(1)}, u32[]{:S(2)}, u32[]{:S(2)}) %collective-permute-start) | collective-permute-done | bytes 262176 | tf_op jit(solution)/shard_map/ppermute | solution.py:219
  40.1 0.1 pad_maximum_fusion
  40.2 0.2 broadcast_in_dim.13
  40.4 0.0 copy-start.6
  40.4 27.4 %all_to_all.16 = bf16[4,2,256,512]{3,2,1,0:T(8,128)(2,1)S(1)} all-to-all(bf16[4,2,256,512]{3,2,1,0:T(8,128)(2,1)S(1)} %broadcast_in_dim.13), channel_id=1, replica_groups=mesh['zm'=4,'zb'=2,'x'=4,'k'=2,'y'=4,'zh'=2] {'x'}, dimensions={0} | all-to-all | bytes 4194304 | tf_op jit(solution)/shard_map/all_to_all | solution.py:207
  67.8 1.9 %collective-permute-start.1 = (bf16[2048,512]{1,0:T(8,128)(2,1)S(1)}, bf16[2048,512]{1,0:T(8,128)(2,1)}, u32[]{:S(2)}, u32[]{:S(2)}) collective-permute-start(bf16[2048,512]{1,0:T(8,128)(2,1)S(1)} %bitcast.9), channel_id=1, source_target_pairs={{0,8},{8,0},{1,9},{9,1},{2,10},{10,2},{3,11},{11,3},{4,12},{12,4},... | collective-permute-start | bytes 6291464 | tf_op jit(solution)/shard_map/ppermute | solution.py:226
  69.7 11.1 %collective-permute-start.2 = (bf16[2,64,512]{2,1,0:T(8,128)(2,1)S(1)}, bf16[2,64,512]{2,1,0:T(8,128)(2,1)S(1)}, u32[]{:S(2)}, u32[]{:S(2)}) collective-permute-start(bf16[2,64,512]{2,1,0:T(8,128)(2,1)S(1)} %copy-done.6), channel_id=1, source_target_pairs={{0,1},{1,0},{2,3},{3,2},{4,5},{5,4},{6,7},{7,6},{8,9},{9,8},{10,11... | collective-permute-start | bytes 393224 | tf_op jit(solution)/shard_map/ppermute | solution.py:220
  80.8 5.7 %collective-permute-done.2 = bf16[2,64,512]{2,1,0:T(8,128)(2,1)S(1)} collective-permute-done((bf16[2,64,512]{2,1,0:T(8,128)(2,1)S(1)}, bf16[2,64,512]{2,1,0:T(8,128)(2,1)S(1)}, u32[]{:S(2)}, u32[]{:S(2)}) %collective-permute-start.2) | collective-permute-done | bytes 131104 | tf_op jit(solution)/shard_map/ppermute | solution.py:220
  86.5 3.5 %collective-permute-start.4 = (bf16[2,2,64,512]{3,2,1,0:T(8,128)(2,1)S(1)}, bf16[2,2,64,512]{3,2,1,0:T(8,128)(2,1)S(1)}, u32[]{:S(2)}, u32[]{:S(2)}) collective-permute-start(bf16[2,2,64,512]{3,2,1,0:T(8,128)(2,1)S(1)} %bitcast_dynamic-update-slice_fusion.t0), channel_id=1, source_target_pairs={{0,2},{2,4},{4,6},{6,0},{1,3},{3,5},{5,7},{7,1},{8,10},{10,12},{12... | collective-permute-start | bytes 786440 | tf_op jit(solution)/shard_map/ppermute | solution.py:223
  90.0 3.6 %collective-permute-start.3 = (bf16[2,2,64,512]{3,2,1,0:T(8,128)(2,1)S(1)}, bf16[2,2,64,512]{3,2,1,0:T(8,128)(2,1)S(1)}, u32[]{:S(2)}, u32[]{:S(2)}) collective-permute-start(bf16[2,2,64,512]{3,2,1,0:T(8,128)(2,1)S(1)} %bitcast_dynamic-update-slice_fusion.t0), channel_id=1, source_target_pairs={{0,6},{2,0},{4,2},{6,4},{1,7},{3,1},{5,3},{7,5},{8,14},{10,8},{12,... | collective-permute-start | bytes 786440 | tf_op jit(solution)/shard_map/ppermute | solution.py:224
  93.6 3.7 %collective-permute-done.4.t3 = bf16[2,2,64,512]{3,2,1,0:T(8,128)(2,1)S(1)} collective-permute-done((bf16[2,2,64,512]{3,2,1,0:T(8,128)(2,1)S(1)}, bf16[2,2,64,512]{3,2,1,0:T(8,128)(2,1)S(1)}, u32[]{:S(2)}, u32[]{:S(2)}) %collective-permute-start.4) | collective-permute-done | bytes 262176 | tf_op jit(solution)/shard_map/ppermute | solution.py:223
  97.3 2.2 %collective-permute-start.5 = (bf16[2,2,64,512]{3,2,1,0:T(8,128)(2,1)S(1)}, bf16[2,2,64,512]{3,2,1,0:T(8,128)(2,1)S(1)}, u32[]{:S(2)}, u32[]{:S(2)}) collective-permute-start(bf16[2,2,64,512]{3,2,1,0:T(8,128)(2,1)S(1)} %collective-permute-done.4.t3), channel_id=1, source_target_pairs={{0,2},{2,4},{4,6},{6,0},{1,3},{3,5},{5,7},{7,1},{8,10},{10,12},{12... | collective-permute-start | bytes 786440 | tf_op jit(solution)/shard_map/ppermute | solution.py:225
  99.5 0.0 collective-permute-done.3.t1
  99.5 7.6 %collective-permute-done.5.t2 = bf16[2,2,64,512]{3,2,1,0:T(8,128)(2,1)S(1)} collective-permute-done((bf16[2,2,64,512]{3,2,1,0:T(8,128)(2,1)S(1)}, bf16[2,2,64,512]{3,2,1,0:T(8,128)(2,1)S(1)}, u32[]{:S(2)}, u32[]{:S(2)}) %collective-permute-start.5) | collective-permute-done | bytes 262176 | tf_op jit(solution)/shard_map/ppermute | solution.py:225
  107.1 0.0 copy-done
  107.2 0.7 copy-done.5
  107.9 7.1 %ladder.2.earlier_ref = f32[2,8,128]{2,1,0:T(8,128)} custom-call(bf16[2048,512]{1,0:T(8,128)(2,1)} %bitcast.10, bf16[2,2,64,512]{3,2,1,0:T(8,128)(2,1)} %copy-done.2, bf16[2,2,64,512]{3,2,1,0:T(8,128)(2,1)} %copy-done.4, bf16[2,2,64,512]{3,2,1,0:T(8,128)(2,1)} %copy-done.5, bf16[2,2,64,512]{3,2,1,0:T(8,128)(2,1)} %copy-done.3), custom_call_target="tpu_custom_call" | custom-call | flops 3221225472 | bytes 3145728 | tf_op jit(solution)/shard_map/ladder/pallas_call | solution.py:171
  115.0 0.0 collective-permute-done.1.slab_ref
  115.0 7.2 %ladder.3 = f32[8,2,128]{2,1,0:T(2,128)} custom-call(bf16[2048,512]{1,0:T(8,128)(2,1)} %collective-permute-done.1.slab_ref, bf16[2,2,64,512]{3,2,1,0:T(8,128)(2,1)} %copy-done.2, bf16[2,2,64,512]{3,2,1,0:T(8,128)(2,1)} %copy-done.4, bf16[2,2,64,512]{3,2,1,0:T(8,128)(2,1)} %copy-done.5, bf16[2,2,64,512]{3,2,1,0:T(8,128)(2,1)} %copy-done.3, ...), custom_call_target="tpu_custom_call" | custom-call | flops 3221225472 | bytes 3145728 | tf_op jit(solution)/shard_map/ladder/pallas_call | solution.py:171
  122.2 28.0 %all_to_all.17.parts_ref = f32[8,2,128]{2,1,0:T(2,128)} all-to-all(f32[8,2,128]{2,1,0:T(2,128)} %ladder.3), channel_id=1, replica_groups=mesh['zm'=4,'zb'=2,'x'=4,'k'=2,'y'=4,'zh'=2] {'y','zh'}, dimensions={0} | all-to-all | bytes 16384 | tf_op jit(solution)/shard_map/all_to_all | solution.py:207
  150.1 1.3 last.1
  (12 shorter events, 0.0 us)
Async XLA Ops:
  31.9 8.3 %collective-permute-start = (bf16[256,512]{1,0:T(8,128)(2,1)S(1)}, bf16[256,512]{1,0:T(8,128)(2,1)S(1)}, u32[]{:S(2)}, u32[]{:S(2)}) collective-permute-start(bf16[256,512]{1,0:T(8,128)(2,1)S(1)} %bitcast.11), channel_id=1, source_target_pairs={{0,64},{64,0},{1,65},{65,1},{2,66},{66,2},{3,67},{67,3},{4,68},{68... | collective-permute-start | bytes 786440 | tf_op jit(solution)/shard_map/ppermute | solution.py:219
  40.4 29.3 %copy-start.6 = (bf16[2,64,512]{2,1,0:T(8,128)(2,1)S(1)}, bf16[2,64,512]{2,1,0:T(8,128)(2,1)}, u32[]{:S(2)}) copy-start(bf16[2,64,512]{2,1,0:T(8,128)(2,1)} %get-tuple-element.11) | copy-start | bytes 393220
  40.4 46.1 %copy-start.1 = (bf16[2,2,64,512]{3,2,1,0:T(8,128)(2,1)S(1)}, bf16[2,2,64,512]{3,2,1,0:T(8,128)(2,1)}, u32[]{:S(2)}) copy-start(bf16[2,2,64,512]{3,2,1,0:T(8,128)(2,1)} %get-tuple-element.10) | copy-start | bytes 786436
  67.8 39.3 %copy-start = (bf16[4,2,256,512]{3,2,1,0:T(8,128)(2,1)}, bf16[4,2,256,512]{3,2,1,0:T(8,128)(2,1)S(1)}, u32[]{:S(2)}) copy-start(bf16[4,2,256,512]{3,2,1,0:T(8,128)(2,1)S(1)} %all_to_all.16) | copy-start | bytes 6291460
  67.8 47.2 %collective-permute-start.1 = (bf16[2048,512]{1,0:T(8,128)(2,1)S(1)}, bf16[2048,512]{1,0:T(8,128)(2,1)}, u32[]{:S(2)}, u32[]{:S(2)}) collective-permute-start(bf16[2048,512]{1,0:T(8,128)(2,1)S(1)} %bitcast.9), channel_id=1, source_target_pairs={{0,8},{8,0},{1,9},{9,1},{2,10},{10,2},{3,11},{11,3},{4,12},{12,4},... | collective-permute-start | bytes 6291464 | tf_op jit(solution)/shard_map/ppermute | solution.py:226
  69.7 16.8 %collective-permute-start.2 = (bf16[2,64,512]{2,1,0:T(8,128)(2,1)S(1)}, bf16[2,64,512]{2,1,0:T(8,128)(2,1)S(1)}, u32[]{:S(2)}, u32[]{:S(2)}) collective-permute-start(bf16[2,64,512]{2,1,0:T(8,128)(2,1)S(1)} %copy-done.6), channel_id=1, source_target_pairs={{0,1},{1,0},{2,3},{3,2},{4,5},{5,4},{6,7},{7,6},{8,9},{9,8},{10,11... | collective-permute-start | bytes 393224 | tf_op jit(solution)/shard_map/ppermute | solution.py:220
  86.5 20.6 %copy-start.2 = (bf16[2,2,64,512]{3,2,1,0:T(8,128)(2,1)}, bf16[2,2,64,512]{3,2,1,0:T(8,128)(2,1)S(1)}, u32[]{:S(2)}) copy-start(bf16[2,2,64,512]{3,2,1,0:T(8,128)(2,1)S(1)} %bitcast_dynamic-update-slice_fusion.t0) | copy-start | bytes 786436
  86.5 10.7 %collective-permute-start.4 = (bf16[2,2,64,512]{3,2,1,0:T(8,128)(2,1)S(1)}, bf16[2,2,64,512]{3,2,1,0:T(8,128)(2,1)S(1)}, u32[]{:S(2)}, u32[]{:S(2)}) collective-permute-start(bf16[2,2,64,512]{3,2,1,0:T(8,128)(2,1)S(1)} %bitcast_dynamic-update-slice_fusion.t0), channel_id=1, source_target_pairs={{0,2},{2,4},{4,6},{6,0},{1,3},{3,5},{5,7},{7,1},{8,10},{10,12},{12... | collective-permute-start | bytes 786440 | tf_op jit(solution)/shard_map/ppermute | solution.py:223
  90.0 9.4 %collective-permute-start.3 = (bf16[2,2,64,512]{3,2,1,0:T(8,128)(2,1)S(1)}, bf16[2,2,64,512]{3,2,1,0:T(8,128)(2,1)S(1)}, u32[]{:S(2)}, u32[]{:S(2)}) collective-permute-start(bf16[2,2,64,512]{3,2,1,0:T(8,128)(2,1)S(1)} %bitcast_dynamic-update-slice_fusion.t0), channel_id=1, source_target_pairs={{0,6},{2,0},{4,2},{6,4},{1,7},{3,1},{5,3},{7,5},{8,14},{10,8},{12,... | collective-permute-start | bytes 786440 | tf_op jit(solution)/shard_map/ppermute | solution.py:224
  97.3 9.9 %copy-start.3 = (bf16[2,2,64,512]{3,2,1,0:T(8,128)(2,1)}, bf16[2,2,64,512]{3,2,1,0:T(8,128)(2,1)S(1)}, u32[]{:S(2)}) copy-start(bf16[2,2,64,512]{3,2,1,0:T(8,128)(2,1)S(1)} %collective-permute-done.4.t3) | copy-start | bytes 786436
  97.3 9.8 %collective-permute-start.5 = (bf16[2,2,64,512]{3,2,1,0:T(8,128)(2,1)S(1)}, bf16[2,2,64,512]{3,2,1,0:T(8,128)(2,1)S(1)}, u32[]{:S(2)}, u32[]{:S(2)}) collective-permute-start(bf16[2,2,64,512]{3,2,1,0:T(8,128)(2,1)S(1)} %collective-permute-done.4.t3), channel_id=1, source_target_pairs={{0,2},{2,4},{4,6},{6,0},{1,3},{3,5},{5,7},{7,1},{8,10},{10,12},{12... | collective-permute-start | bytes 786440 | tf_op jit(solution)/shard_map/ppermute | solution.py:225
  99.5 7.7 %copy-start.4 = (bf16[2,2,64,512]{3,2,1,0:T(8,128)(2,1)}, bf16[2,2,64,512]{3,2,1,0:T(8,128)(2,1)S(1)}, u32[]{:S(2)}) copy-start(bf16[2,2,64,512]{3,2,1,0:T(8,128)(2,1)S(1)} %collective-permute-done.3.t1) | copy-start | bytes 786436
  107.1 0.7 copy-start.5

commit v2 on v1

--- a/solution.py
+++ b/solution.py
@@ -9,7 +9,7 @@
 NWIN = 8
 GROUP = 256
 BLOCK = 512
-PAIR = ("zm", "zb", "x", "k")
+PAIR = ("zl", "x", "k")
 AUX = ("y", "zh")
 SWAP = [(0, 1), (1, 0)]
 UP = [(i, (i + 1) % 4) for i in range(4)]
@@ -20,7 +20,7 @@
 
 def start_kernel(
     pairs_ref, occ_energy_ref, vir_energy_ref, doubles_ref, singles_ref, vir_ref, occ_ref,
-    dressed_ref, own_ref, tau_ref, denominator_ref, cols_ref,
+    dressed_ref, low_ref, high_ref, own_ref, tau_ref, denominator_ref, cols_ref,
 ):
     local_pairs, chunk, _ = doubles_ref.shape
     zh = lax.axis_index("zh")
@@ -32,9 +32,10 @@
         dressed = vir_ref[slab].astype(jnp.float32) - jnp.dot(
             window, occ_ref[slab], preferred_element_type=jnp.float32
         )
-        dressed = dressed.astype(jnp.bfloat16)
-        for copy in range(dressed_ref.shape[0]):
-            dressed_ref[copy, slab * NWIN : (slab + 1) * NWIN, :] = dressed
+        dressed_ref[slab * NWIN : (slab + 1) * NWIN, :] = dressed.astype(jnp.bfloat16)
+    half = dressed_ref.shape[0] // 2
+    low_ref[...] = dressed_ref[:half]
+    high_ref[...] = dressed_ref[half:]
     ids = lax.broadcasted_iota(jnp.int32, (occ, 128), 0)
     lane = lax.broadcasted_iota(jnp.int32, (occ, 128), 1)
     first = jnp.zeros((occ, 128), jnp.float32)
@@ -71,13 +72,15 @@
     return pl.pallas_call(
         start_kernel,
         out_shape=(
-            jax.ShapeDtypeStruct((4, slabs * NWIN, virt), jnp.bfloat16),
+            jax.ShapeDtypeStruct((slabs * NWIN, virt), jnp.bfloat16),
+            jax.ShapeDtypeStruct((slabs * NWIN // 2, virt), jnp.bfloat16),
+            jax.ShapeDtypeStruct((slabs * NWIN // 2, virt), jnp.bfloat16),
             jax.ShapeDtypeStruct((local_pairs, chunk, virt), jnp.bfloat16),
             jax.ShapeDtypeStruct((2, local_pairs, chunk, virt), jnp.bfloat16),
             jax.ShapeDtypeStruct((local_pairs, 128), jnp.float32),
         ),
         in_specs=[SMEM] * 3 + [VMEM] * 4,
-        out_specs=(VMEM,) * 4,
+        out_specs=(VMEM,) * 6,
         scratch_shapes=[pltpu.VMEM((virt, 128), jnp.float32)],
         cost_estimate=pl.CostEstimate(flops=slabs * NWIN * occ * virt * 2, bytes_accessed=3 << 20, transcendentals=0),
         name="start",
@@ -183,6 +186,7 @@
             bytes_accessed=2 * rows * virt + 2 * pairs * virt * virt,
             transcendentals=0,
         ),
+        compiler_params=pltpu.CompilerParams(vmem_limit_bytes=16 << 20),
         name="ladder",
     )(*operands)
 
@@ -207,6 +211,14 @@
     return lax.all_to_all(copies, axis, split_axis=0, concat_axis=0, tiled=True)
 
 
+def shift_z(value, step):
+    moves = []
+    for z in range(16):
+        to = (z + step) % 16
+        moves.append((z % 8 * 2 + z // 8, to % 8 * 2 + to // 8))
+    return lax.ppermute(value, ("zl", "zh"), moves)
+
+
 def spread(value, axis):
     return exchange(jnp.broadcast_to(value[None], (lax.axis_size(axis),) + value.shape), axis)
 
@@ -214,10 +226,16 @@
 def body(doubles, singles, vir_slabs, occ_slabs, occ_energy, vir_energy, pair_list):
     virt = doubles.shape[2]
     zh = lax.axis_index("zh")
-    copies, own, tau, denominator = start(doubles, singles, vir_slabs, occ_slabs, occ_energy, vir_energy, pair_list)
-    dressed = exchange(copies, "zm").reshape(-1, virt)
-    dressed_next = lax.ppermute(dressed, "zb", SWAP)
+    dressed, low, high, own, tau, denominator = start(
+        doubles, singles, vir_slabs, occ_slabs, occ_energy, vir_energy, pair_list
+    )
+    below_4 = shift_z(low, 4)
+    above_4 = shift_z(high, -4)
+    below_2 = shift_z(dressed, 2)
+    above_2 = shift_z(dressed, -2)
     other = lax.ppermute(own, "zh", SWAP)
+    dressed = jnp.concatenate([dressed, below_2, above_2, below_4, above_4])
+    dressed_next = shift_z(dressed, 1)
     dressed = spread(jnp.stack([dressed, dressed_next]), "x").reshape(-1, virt)
     tau = lax.dynamic_update_index_in_dim(tau, other, 1 - zh, 0)
     below = lax.ppermute(tau, "y", UP)
@@ -232,7 +250,7 @@
 
 
 def solution(mesh):
-    fine = Mesh(mesh.devices.reshape(4, 2, 4, 2, 4, 2), PAIR + AUX)
+    fine = Mesh(mesh.devices.reshape(8, 4, 2, 4, 2), PAIR + AUX)
     placed = (
         P(PAIR, AUX, None),
         P(),

time: 152 us -> 154 us (1.013)
  blocking collectives: 84 us -> 50.5 us
  starting transfers between devices: 24.6 us -> 47.6 us
  waiting for transfers between devices: 22.9 us -> 38.1 us
  Pallas kernels: 18.9 us -> 15.9 us
    all_to_all x3 -> x2, blocking collectives: 84 us -> 50.5 us  [exchange(): return lax.all_to_all(copies, axis, split_axis=0, concat_axis=0, tiled=True)]
    ppermute x1 -> x5, starting transfers between devices: 2.42 us -> 25.8 us  [shift_z(): return lax.ppermute(value, ('zl', 'zh'), moves)]
    ppermute x1, waiting for transfers between devices: 5.75 us -> 14.2 us  [body(): other = lax.ppermute(own, 'zh', SWAP)]
    ppermute x1 -> x5, waiting for transfers between devices: 5.83 us -> 12 us  [shift_z(): return lax.ppermute(value, ('zl', 'zh'), moves)]
    pallas_call x2, Pallas kernels: 14.3 us -> 11.4 us  [ladder(): pl.pallas_call(kernel, out_shape=jax.ShapeDtypeStruct(out, jnp.float32),...]
  transfers between devices with their start and end apart: 6 -> 10, of which waited for: 4 -> 5; matrix products, arithmetic and copies ran while one was open for 0% -> 1% of each run, Pallas kernels for 5% -> 3%
where the time goes in v2:
time: 154 us; the launch traced here: 153 us
  blocking collectives  50.5 us (33%)
  starting transfers between devices  47.6 us (31%)
  waiting for transfers between devices  38.1 us (25%)
  Pallas kernels  15.9 us (10%)
    all_to_all x2, blocking collectives, exchange(): return lax.all_to_all(copies, axis, split_axis=0, concat_axis=0, tiled=True)  50.5 us
    ppermute x5, starting transfers between devices, shift_z(): return lax.ppermute(value, ('zl', 'zh'), moves)  25.8 us
    ppermute x1, waiting for transfers between devices, body(): other = lax.ppermute(own, 'zh', SWAP)  14.2 us
    ppermute x5, waiting for transfers between devices, shift_z(): return lax.ppermute(value, ('zl', 'zh'), moves)  12 us
    pallas_call x2, Pallas kernels, ladder(): pl.pallas_call(kernel, out_shape=jax.ShapeDtypeStruct(out, jnp.float32),...  11.4 us
    ppermute x1, starting transfers between devices, body(): other = lax.ppermute(own, 'zh', SWAP)  10.5 us
    ppermute x1, waiting for transfers between devices, body(): far = lax.ppermute(below, 'y', UP)  7.89 us
    ppermute x1, waiting for transfers between devices, body(): below = lax.ppermute(tau, 'y', UP)  3.9 us
  transfers between devices with their start and end apart: 10, of which 5 were waited for; matrix products, arithmetic and copies ran while one was open for 1% of the time, Pallas kernels for 3%

profile of v2, /device:TPU:2, one launch (start us, length us, event | category | flops | bytes accessed | tf_op | source)
XLA Modules:
  0.0 153.4 jit_solution(16969401392921475430)
XLA Ops:
  0.0 3.2 %start.1 = (bf16[64,512]{1,0:T(8,128)(2,1)}, bf16[32,512]{1,0:T(8,128)(2,1)}, bf16[32,512]{1,0:T(8,128)(2,1)}, bf16[2,64,512]{2,1,0:T(8,128)(2,1)}, bf16[2,2,64,512]{3,2,1,0:T(8,128)(2,1)}, /*index=5*/f32[2,128]{1,0:T(2,128)}) custom-call(s32[2,2]{1,0:T(2,128)} %pairs_ref.1, f32[256]{0:T(256)} %occ_energy_ref.1, f32[8]{0:T(128)} %vir_energy_ref.1, ...), custom_call_target="tpu_custom_call" | custom-call | flops 16777216 | bytes 3145728 | tf_op jit(solution)/shard_map/start/pallas_call | solution.py:72
  3.2 5.2 %collective-permute-start = (bf16[64,512]{1,0:T(8,128)(2,1)}, bf16[64,512]{1,0:T(8,128)(2,1)S(1)}, u32[]{:S(2)}, u32[]{:S(2)}) collective-permute-start(bf16[64,512]{1,0:T(8,128)(2,1)} %get-tuple-element.11), channel_id=1, source_target_pairs={{0,128},{64,192},{128,256},{192,320},{256,384},{320,448},{384,1},{... | collective-permute-start | bytes 196616 | tf_op jit(solution)/shard_map/ppermute | solution.py:219
  8.4 8.6 %collective-permute-start.1 = (bf16[64,512]{1,0:T(8,128)(2,1)}, bf16[64,512]{1,0:T(8,128)(2,1)S(1)}, u32[]{:S(2)}, u32[]{:S(2)}) collective-permute-start(bf16[64,512]{1,0:T(8,128)(2,1)} %get-tuple-element.11), channel_id=1, source_target_pairs={{0,385},{64,449},{128,0},{192,64},{256,128},{320,192},{384,256},{4... | collective-permute-start | bytes 196616 | tf_op jit(solution)/shard_map/ppermute | solution.py:219
  17.0 3.3 %collective-permute-start.2 = (bf16[32,512]{1,0:T(8,128)(2,1)}, bf16[32,512]{1,0:T(8,128)(2,1)S(1)}, u32[]{:S(2)}, u32[]{:S(2)}) collective-permute-start(bf16[32,512]{1,0:T(8,128)(2,1)} %get-tuple-element.12), channel_id=1, source_target_pairs={{0,256},{64,320},{128,384},{192,448},{256,1},{320,65},{384,129},{4... | collective-permute-start | bytes 98312 | tf_op jit(solution)/shard_map/ppermute | solution.py:219
  20.3 6.5 %collective-permute-start.3 = (bf16[32,512]{1,0:T(8,128)(2,1)}, bf16[32,512]{1,0:T(8,128)(2,1)S(1)}, u32[]{:S(2)}, u32[]{:S(2)}) collective-permute-start(bf16[32,512]{1,0:T(8,128)(2,1)} %get-tuple-element.13), channel_id=1, source_target_pairs={{0,257},{64,321},{128,385},{192,449},{256,0},{320,64},{384,128},{4... | collective-permute-start | bytes 98312 | tf_op jit(solution)/shard_map/ppermute | solution.py:219
  26.8 0.8 constant_dynamic-update-slice_fusion.4
  27.7 4.9 %collective-permute-done.3 = bf16[32,512]{1,0:T(8,128)(2,1)S(1)} collective-permute-done((bf16[32,512]{1,0:T(8,128)(2,1)}, bf16[32,512]{1,0:T(8,128)(2,1)S(1)}, u32[]{:S(2)}, u32[]{:S(2)}) %collective-permute-start.3) | collective-permute-done | bytes 32800 | tf_op jit(solution)/shard_map/ppermute | solution.py:219
  32.5 2.3 %collective-permute-start.4 = (bf16[256,512]{1,0:T(8,128)(2,1)S(1)}, bf16[256,512]{1,0:T(8,128)(2,1)S(1)}, u32[]{:S(2)}, u32[]{:S(2)}) collective-permute-start(bf16[256,512]{1,0:T(8,128)(2,1)S(1)} %constant_dynamic-update-slice_fusion), channel_id=1, source_target_pairs={{0,64},{64,128},{128,192},{192,256},{256,320},{320,384},{384,448},... | collective-permute-start | bytes 786440 | tf_op jit(solution)/shard_map/ppermute | solution.py:219
  34.9 7.1 %collective-permute-done.4 = bf16[256,512]{1,0:T(8,128)(2,1)S(1)} collective-permute-done((bf16[256,512]{1,0:T(8,128)(2,1)S(1)}, bf16[256,512]{1,0:T(8,128)(2,1)S(1)}, u32[]{:S(2)}, u32[]{:S(2)}) %collective-permute-start.4) | collective-permute-done | bytes 262176 | tf_op jit(solution)/shard_map/ppermute | solution.py:219
  42.0 0.1 pad_maximum_fusion
  42.1 0.2 broadcast_in_dim.13
  42.3 25.7 %all_to_all.10 = bf16[4,2,256,512]{3,2,1,0:T(8,128)(2,1)S(1)} all-to-all(bf16[4,2,256,512]{3,2,1,0:T(8,128)(2,1)S(1)} %broadcast_in_dim.13), channel_id=1, replica_groups=mesh['zl'=8,'x'=4,'k'=2,'y'=4,'zh'=2] {'x'}, dimensions={0} | all-to-all | bytes 4194304 | tf_op jit(solution)/shard_map/all_to_all | solution.py:211
  68.0 1.9 %collective-permute-start.5 = (bf16[2048,512]{1,0:T(8,128)(2,1)S(1)}, bf16[2048,512]{1,0:T(8,128)(2,1)}, u32[]{:S(2)}, u32[]{:S(2)}) collective-permute-start(bf16[2048,512]{1,0:T(8,128)(2,1)S(1)} %bitcast.8), channel_id=1, source_target_pairs={{0,8},{8,0},{1,9},{9,1},{2,10},{10,2},{3,11},{11,3},{4,12},{12,4},... | collective-permute-start | bytes 6291464 | tf_op jit(solution)/shard_map/ppermute | solution.py:244
  69.9 10.5 %collective-permute-start.6 = (bf16[2,64,512]{2,1,0:T(8,128)(2,1)S(1)}, bf16[2,64,512]{2,1,0:T(8,128)(2,1)S(1)}, u32[]{:S(2)}, u32[]{:S(2)}) collective-permute-start(bf16[2,64,512]{2,1,0:T(8,128)(2,1)S(1)} %copy-done.2), channel_id=1, source_target_pairs={{0,1},{1,0},{2,3},{3,2},{4,5},{5,4},{6,7},{7,6},{8,9},{9,8},{10,11... | collective-permute-start | bytes 393224 | tf_op jit(solution)/shard_map/ppermute | solution.py:236
  80.5 14.2 %collective-permute-done.6 = bf16[2,64,512]{2,1,0:T(8,128)(2,1)S(1)} collective-permute-done((bf16[2,64,512]{2,1,0:T(8,128)(2,1)S(1)}, bf16[2,64,512]{2,1,0:T(8,128)(2,1)S(1)}, u32[]{:S(2)}, u32[]{:S(2)}) %collective-permute-start.6) | collective-permute-done | bytes 131104 | tf_op jit(solution)/shard_map/ppermute | solution.py:236
  94.7 3.6 %collective-permute-start.8 = (bf16[2,2,64,512]{3,2,1,0:T(8,128)(2,1)S(1)}, bf16[2,2,64,512]{3,2,1,0:T(8,128)(2,1)S(1)}, u32[]{:S(2)}, u32[]{:S(2)}) collective-permute-start(bf16[2,2,64,512]{3,2,1,0:T(8,128)(2,1)S(1)} %bitcast_dynamic-update-slice_fusion.t0), channel_id=1, source_target_pairs={{0,2},{2,4},{4,6},{6,0},{1,3},{3,5},{5,7},{7,1},{8,10},{10,12},{12... | collective-permute-start | bytes 786440 | tf_op jit(solution)/shard_map/ppermute | solution.py:241
  98.4 3.6 %collective-permute-start.7 = (bf16[2,2,64,512]{3,2,1,0:T(8,128)(2,1)S(1)}, bf16[2,2,64,512]{3,2,1,0:T(8,128)(2,1)S(1)}, u32[]{:S(2)}, u32[]{:S(2)}) collective-permute-start(bf16[2,2,64,512]{3,2,1,0:T(8,128)(2,1)S(1)} %bitcast_dynamic-update-slice_fusion.t0), channel_id=1, source_target_pairs={{0,6},{2,0},{4,2},{6,4},{1,7},{3,1},{5,3},{7,5},{8,14},{10,8},{12,... | collective-permute-start | bytes 786440 | tf_op jit(solution)/shard_map/ppermute | solution.py:242
  101.9 3.9 %collective-permute-done.8.t3 = bf16[2,2,64,512]{3,2,1,0:T(8,128)(2,1)S(1)} collective-permute-done((bf16[2,2,64,512]{3,2,1,0:T(8,128)(2,1)S(1)}, bf16[2,2,64,512]{3,2,1,0:T(8,128)(2,1)S(1)}, u32[]{:S(2)}, u32[]{:S(2)}) %collective-permute-start.8) | collective-permute-done | bytes 262176 | tf_op jit(solution)/shard_map/ppermute | solution.py:241
  105.8 2.2 %collective-permute-start.9 = (bf16[2,2,64,512]{3,2,1,0:T(8,128)(2,1)S(1)}, bf16[2,2,64,512]{3,2,1,0:T(8,128)(2,1)S(1)}, u32[]{:S(2)}, u32[]{:S(2)}) collective-permute-start(bf16[2,2,64,512]{3,2,1,0:T(8,128)(2,1)S(1)} %collective-permute-done.8.t3), channel_id=1, source_target_pairs={{0,2},{2,4},{4,6},{6,0},{1,3},{3,5},{5,7},{7,1},{8,10},{10,12},{12... | collective-permute-start | bytes 786440 | tf_op jit(solution)/shard_map/ppermute | solution.py:243
  108.1 7.9 %collective-permute-done.9.t2 = bf16[2,2,64,512]{3,2,1,0:T(8,128)(2,1)S(1)} collective-permute-done((bf16[2,2,64,512]{3,2,1,0:T(8,128)(2,1)S(1)}, bf16[2,2,64,512]{3,2,1,0:T(8,128)(2,1)S(1)}, u32[]{:S(2)}, u32[]{:S(2)}) %collective-permute-start.9) | collective-permute-done | bytes 262176 | tf_op jit(solution)/shard_map/ppermute | solution.py:243
  115.9 5.1 %ladder.2.earlier_ref = f32[2,8,128]{2,1,0:T(8,128)S(1)} custom-call(bf16[2048,512]{1,0:T(8,128)(2,1)S(1)} %bitcast.9, bf16[2,2,64,512]{3,2,1,0:T(8,128)(2,1)S(1)} %bitcast_dynamic-update-slice_fusion.t0, bf16[2,2,64,512]{3,2,1,0:T(8,128)(2,1)S(1)} %collective-permute-done.7.t1, bf16[2,2,64,512]{3,2,1,0:T(8,128)(2,1)S(1)} %collective-permute-done.9.t2, ...), custom_call_target="tpu_custom_call" | custom-call | flops 3221225472 | bytes 3145728 | tf_op jit(solution)/shard_map/ladder/pallas_call | solution.py:174
  121.1 6.2 %ladder.3 = f32[8,2,128]{2,1,0:T(2,128)S(1)} custom-call(bf16[2048,512]{1,0:T(8,128)(2,1)} %collective-permute-done.5.slab_ref, bf16[2,2,64,512]{3,2,1,0:T(8,128)(2,1)S(1)} %bitcast_dynamic-update-slice_fusion.t0, bf16[2,2,64,512]{3,2,1,0:T(8,128)(2,1)S(1)} %collective-permute-done.7.t1, bf16[2,2,64,512]{3,2,1,0:T(8,128)(2,1)S(1)} %collective-permute-done.9.t2, ...), custom_call_target="tpu_custom_call" | custom-call | flops 3221225472 | bytes 3145728 | tf_op jit(solution)/shard_map/ladder/pallas_call | solution.py:174
  127.3 24.8 %all_to_all.11.parts_ref = f32[8,2,128]{2,1,0:T(2,128)} all-to-all(f32[8,2,128]{2,1,0:T(2,128)S(1)} %ladder.3), channel_id=1, replica_groups=mesh['zl'=8,'x'=4,'k'=2,'y'=4,'zh'=2] {'y','zh'}, dimensions={0} | all-to-all | bytes 16384 | tf_op jit(solution)/shard_map/all_to_all | solution.py:211
  152.1 1.3 last.1
  (16 shorter events, 0.1 us)
Async XLA Ops:
  3.2 24.4 %collective-permute-start = (bf16[64,512]{1,0:T(8,128)(2,1)}, bf16[64,512]{1,0:T(8,128)(2,1)S(1)}, u32[]{:S(2)}, u32[]{:S(2)}) collective-permute-start(bf16[64,512]{1,0:T(8,128)(2,1)} %get-tuple-element.11), channel_id=1, source_target_pairs={{0,128},{64,192},{128,256},{192,320},{256,384},{320,448},{384,1},{... | collective-permute-start | bytes 196616 | tf_op jit(solution)/shard_map/ppermute | solution.py:219
  8.4 19.2 %collective-permute-start.1 = (bf16[64,512]{1,0:T(8,128)(2,1)}, bf16[64,512]{1,0:T(8,128)(2,1)S(1)}, u32[]{:S(2)}, u32[]{:S(2)}) collective-permute-start(bf16[64,512]{1,0:T(8,128)(2,1)} %get-tuple-element.11), channel_id=1, source_target_pairs={{0,385},{64,449},{128,0},{192,64},{256,128},{320,192},{384,256},{4... | collective-permute-start | bytes 196616 | tf_op jit(solution)/shard_map/ppermute | solution.py:219
  17.0 10.7 %collective-permute-start.2 = (bf16[32,512]{1,0:T(8,128)(2,1)}, bf16[32,512]{1,0:T(8,128)(2,1)S(1)}, u32[]{:S(2)}, u32[]{:S(2)}) collective-permute-start(bf16[32,512]{1,0:T(8,128)(2,1)} %get-tuple-element.12), channel_id=1, source_target_pairs={{0,256},{64,320},{128,384},{192,448},{256,1},{320,65},{384,129},{4... | collective-permute-start | bytes 98312 | tf_op jit(solution)/shard_map/ppermute | solution.py:219
  20.3 12.2 %collective-permute-start.3 = (bf16[32,512]{1,0:T(8,128)(2,1)}, bf16[32,512]{1,0:T(8,128)(2,1)S(1)}, u32[]{:S(2)}, u32[]{:S(2)}) collective-permute-start(bf16[32,512]{1,0:T(8,128)(2,1)} %get-tuple-element.13), channel_id=1, source_target_pairs={{0,257},{64,321},{128,385},{192,449},{256,0},{320,64},{384,128},{4... | collective-permute-start | bytes 98312 | tf_op jit(solution)/shard_map/ppermute | solution.py:219
  32.5 9.5 %collective-permute-start.4 = (bf16[256,512]{1,0:T(8,128)(2,1)S(1)}, bf16[256,512]{1,0:T(8,128)(2,1)S(1)}, u32[]{:S(2)}, u32[]{:S(2)}) collective-permute-start(bf16[256,512]{1,0:T(8,128)(2,1)S(1)} %constant_dynamic-update-slice_fusion), channel_id=1, source_target_pairs={{0,64},{64,128},{128,192},{192,256},{256,320},{320,384},{384,448},... | collective-permute-start | bytes 786440 | tf_op jit(solution)/shard_map/ppermute | solution.py:219
  42.2 27.7 %copy-start.2 = (bf16[2,64,512]{2,1,0:T(8,128)(2,1)S(1)}, bf16[2,64,512]{2,1,0:T(8,128)(2,1)}, u32[]{:S(2)}) copy-start(bf16[2,64,512]{2,1,0:T(8,128)(2,1)} %get-tuple-element.15) | copy-start | bytes 393220
  42.2 52.5 %copy-start.1 = (bf16[2,2,64,512]{3,2,1,0:T(8,128)(2,1)S(1)}, bf16[2,2,64,512]{3,2,1,0:T(8,128)(2,1)}, u32[]{:S(2)}) copy-start(bf16[2,2,64,512]{3,2,1,0:T(8,128)(2,1)} %get-tuple-element.14) | copy-start | bytes 786436
  68.0 53.1 %collective-permute-start.5 = (bf16[2048,512]{1,0:T(8,128)(2,1)S(1)}, bf16[2048,512]{1,0:T(8,128)(2,1)}, u32[]{:S(2)}, u32[]{:S(2)}) collective-permute-start(bf16[2048,512]{1,0:T(8,128)(2,1)S(1)} %bitcast.8), channel_id=1, source_target_pairs={{0,8},{8,0},{1,9},{9,1},{2,10},{10,2},{3,11},{11,3},{4,12},{12,4},... | collective-permute-start | bytes 6291464 | tf_op jit(solution)/shard_map/ppermute | solution.py:244
  69.9 24.8 %collective-permute-start.6 = (bf16[2,64,512]{2,1,0:T(8,128)(2,1)S(1)}, bf16[2,64,512]{2,1,0:T(8,128)(2,1)S(1)}, u32[]{:S(2)}, u32[]{:S(2)}) collective-permute-start(bf16[2,64,512]{2,1,0:T(8,128)(2,1)S(1)} %copy-done.2), channel_id=1, source_target_pairs={{0,1},{1,0},{2,3},{3,2},{4,5},{5,4},{6,7},{7,6},{8,9},{9,8},{10,11... | collective-permute-start | bytes 393224 | tf_op jit(solution)/shard_map/ppermute | solution.py:236
  94.7 26.4 %copy-start = (bf16[2,64,512]{2,1,0:T(8,128)(2,1)S(1)}, bf16[2,64,512]{2,1,0:T(8,128)(2,1)}, u32[]{:S(2)}) copy-start(bf16[2,64,512]{2,1,0:T(8,128)(2,1)} %doubles_ref.3) | copy-start | bytes 393220
  94.7 11.1 %collective-permute-start.8 = (bf16[2,2,64,512]{3,2,1,0:T(8,128)(2,1)S(1)}, bf16[2,2,64,512]{3,2,1,0:T(8,128)(2,1)S(1)}, u32[]{:S(2)}, u32[]{:S(2)}) collective-permute-start(bf16[2,2,64,512]{3,2,1,0:T(8,128)(2,1)S(1)} %bitcast_dynamic-update-slice_fusion.t0), channel_id=1, source_target_pairs={{0,2},{2,4},{4,6},{6,0},{1,3},{3,5},{5,7},{7,1},{8,10},{10,12},{12... | collective-permute-start | bytes 786440 | tf_op jit(solution)/shard_map/ppermute | solution.py:241
  98.4 9.7 %collective-permute-start.7 = (bf16[2,2,64,512]{3,2,1,0:T(8,128)(2,1)S(1)}, bf16[2,2,64,512]{3,2,1,0:T(8,128)(2,1)S(1)}, u32[]{:S(2)}, u32[]{:S(2)}) collective-permute-start(bf16[2,2,64,512]{3,2,1,0:T(8,128)(2,1)S(1)} %bitcast_dynamic-update-slice_fusion.t0), channel_id=1, source_target_pairs={{0,6},{2,0},{4,2},{6,4},{1,7},{3,1},{5,3},{7,5},{8,14},{10,8},{12,... | collective-permute-start | bytes 786440 | tf_op jit(solution)/shard_map/ppermute | solution.py:242
  105.8 10.1 %collective-permute-start.9 = (bf16[2,2,64,512]{3,2,1,0:T(8,128)(2,1)S(1)}, bf16[2,2,64,512]{3,2,1,0:T(8,128)(2,1)S(1)}, u32[]{:S(2)}, u32[]{:S(2)}) collective-permute-start(bf16[2,2,64,512]{3,2,1,0:T(8,128)(2,1)S(1)} %collective-permute-done.8.t3), channel_id=1, source_target_pairs={{0,2},{2,4},{4,6},{6,0},{1,3},{3,5},{5,7},{7,1},{8,10},{10,12},{12... | collective-permute-start | bytes 786440 | tf_op jit(solution)/shard_map/ppermute | solution.py:243

commit v3 on v1

--- a/solution.py
+++ b/solution.py
@@ -1,3 +1,5 @@
+import functools
+
 import jax
 import jax.numpy as jnp
 from jax import lax
@@ -8,7 +10,6 @@
 
 NWIN = 8
 GROUP = 256
-BLOCK = 512
 PAIR = ("zm", "zb", "x", "k")
 AUX = ("y", "zh")
 SWAP = [(0, 1), (1, 0)]
@@ -84,31 +85,6 @@
     )(pair_list, occ_energy, vir_energy, doubles, singles, vir_slabs, occ_slabs)
 
 
-def gather_tau(refs, tau_ref):
-    y = lax.axis_index("y")
-    for shift, ref in enumerate(refs):
-        halves, pairs, chunk, _ = ref.shape
-        base = lax.rem(y + shift, 4) * (halves * chunk)
-        for half in range(halves):
-            rows = pl.ds(pl.multiple_of(base + half * chunk, chunk), chunk)
-            for pair in range(pairs):
-                tau_ref[pair, rows, :] = ref[half, pair]
-
-
-def add_block(slab_ref, tau_ref, gram_ref):
-    slabs = slab_ref[...]
-    groups = [slabs[s : s + GROUP] for s in range(0, BLOCK, GROUP)]
-    for pair in range(tau_ref.shape[0]):
-        half = jnp.dot(slabs, tau_ref[pair], preferred_element_type=jnp.float32).astype(jnp.bfloat16)
-        total = gram_ref[pair]
-        for number, group in enumerate(groups):
-            rows = half[number * GROUP : (number + 1) * GROUP]
-            total = total + lax.dot_general(
-                rows, group, (((1,), (1,)), ((), ())), preferred_element_type=jnp.float32
-            )
-        gram_ref[pair] = total
-
-
 def fold(gram):
     row = lax.broadcasted_iota(jnp.int32, (GROUP, GROUP), 0) // NWIN
     col = lax.broadcasted_iota(jnp.int32, (GROUP, GROUP), 1) // NWIN
@@ -122,67 +98,72 @@
     return folded
 
 
-def ladder_step(slab_ref, tau_refs, tau_ref, gram_ref):
-    @pl.when(pl.program_id(0) == 0)
-    def _():
-        gram_ref[...] = jnp.zeros_like(gram_ref)
-        gather_tau(tau_refs, tau_ref)
-
-    add_block(slab_ref, tau_ref, gram_ref)
-
-
-def first_kernel(slab_ref, t0, t1, t2, t3, out_ref, tau_ref, gram_ref):
-    ladder_step(slab_ref, (t0, t1, t2, t3), tau_ref, gram_ref)
-
-    @pl.when(pl.program_id(0) == pl.num_programs(0) - 1)
-    def _():
-        for pair in range(gram_ref.shape[0]):
-            out_ref[pair] = fold(gram_ref[pair])
-
-
-def second_kernel(slab_ref, t0, t1, t2, t3, earlier_ref, doubles_ref, out_ref, tau_ref, gram_ref):
-    ladder_step(slab_ref, (t0, t1, t2, t3), tau_ref, gram_ref)
-
-    @pl.when(pl.program_id(0) == pl.num_programs(0) - 1)
-    def _():
-        lane = lax.broadcasted_iota(jnp.int32, (NWIN, 128), 1)
-        holds = (lax.axis_index("y") == 0) & (lax.axis_index("zh") == 0)
-        with_doubles = (lane < 2 * NWIN) & holds
-        for pair in range(gram_ref.shape[0]):
-            residual = fold(gram_ref[pair]) + earlier_ref[pair]
-            doubles = pltpu.roll(doubles_ref[pair].astype(jnp.float32)[:NWIN], NWIN, 1)
-            row = jnp.where(lane < NWIN, residual, jnp.where(with_doubles, doubles, 0.0))
+def ladder_kernel(slab_count, has_earlier, pays, *refs):
+    slab_refs, refs = refs[:slab_count], refs[slab_count:]
+    tau_refs, refs = refs[:2], refs[2:]
+    earlier_ref = refs[0] if has_earlier else None
+    doubles_ref = refs[1] if pays else None
+    out_ref = refs[-1]
+    pairs, virt = tau_refs[0].shape[2], tau_refs[0].shape[4]
+    core = lax.axis_index("k")
+    lane = lax.broadcasted_iota(jnp.int32, (NWIN, 128), 1)
+    holds = (lax.axis_index("y") == 0) & (lax.axis_index("zh") == 0)
+    for owner, tau_ref in enumerate(tau_refs):
+        for pair in range(pairs):
+            tau = tau_ref[:, :, pair].reshape(virt, virt)
+            gram = None
+            for slab_ref in slab_refs:
+                slabs = slab_ref[...]
+                half = jnp.dot(slabs, tau, preferred_element_type=jnp.float32).astype(jnp.bfloat16)
+                for at in range(0, slabs.shape[0], GROUP):
+                    block = lax.dot_general(
+                        half[at : at + GROUP],
+                        slabs[at : at + GROUP],
+                        (((1,), (1,)), ((), ())),
+                        preferred_element_type=jnp.float32,
+                    )
+                    gram = block if gram is None else gram + block
+            residual = fold(gram)
+            if has_earlier:
+                residual = residual + earlier_ref[owner * pairs + pair]
+            if not pays:
+                out_ref[owner * pairs + pair] = residual
+                continue
+            row = jnp.where(lane < NWIN, residual, 0.0)
+            if owner == 0:
+                doubles = pltpu.roll(doubles_ref[pair].astype(jnp.float32)[:NWIN], NWIN, 1)
+                doubles = jnp.where((lane < 2 * NWIN) & holds, doubles, 0.0)
+                row = jnp.where(lane < NWIN, residual, doubles)
+            to = core if owner == 0 else 1 - core
             for a in range(NWIN):
-                out_ref[a, pair : pair + 1, :] = row[a : a + 1]
+                out_ref[to * NWIN + a, pair : pair + 1, :] = row[a : a + 1]
 
 
 def ladder(slabs, taus, earlier=None, doubles=None):
-    rows, virt = slabs.shape
-    pairs = taus[0].shape[1]
-    whole = pl.BlockSpec(taus[0].shape, lambda i: (0, 0, 0, 0))
-    specs = [pl.BlockSpec((BLOCK, virt), lambda i: (i, 0))] + [whole] * 4
-    operands = [slabs, *taus]
-    if earlier is None:
-        kernel, out = first_kernel, (pairs, NWIN, 128)
-    else:
-        kernel, out = second_kernel, (NWIN, pairs, 128)
-        specs += [pl.BlockSpec(earlier.shape, lambda i: (0, 0, 0)), pl.BlockSpec((pairs, 16, 128), lambda i: (0, 0, 0))]
-        operands += [earlier, doubles]
+    pairs, virt = taus[0].shape[2], taus[0].shape[4]
+    rows = sum(slab.shape[0] for slab in slabs)
+    has_earlier, pays = earlier is not None, doubles is not None
+    specs, operands = [VMEM] * (len(slabs) + 2), [*slabs, *taus]
+    out = (2 * pairs, NWIN, 128)
+    if has_earlier:
+        specs.append(VMEM)
+        operands.append(earlier)
+    if pays:
+        specs.append(pl.BlockSpec((pairs, 16, 128), lambda i: (0, 0, 0)))
+        operands.append(doubles)
+        out = (2 * NWIN, pairs, 128)
     return pl.pallas_call(
-        kernel,
+        functools.partial(ladder_kernel, len(slabs), has_earlier, pays),
         out_shape=jax.ShapeDtypeStruct(out, jnp.float32),
-        grid=(rows // BLOCK,),
+        grid=(1,),
         in_specs=specs,
-        out_specs=pl.BlockSpec(out, lambda i: (0, 0, 0)),
-        scratch_shapes=[
-            pltpu.VMEM((pairs, virt, virt), jnp.bfloat16),
-            pltpu.VMEM((pairs, GROUP, GROUP), jnp.float32),
-        ],
+        out_specs=VMEM,
         cost_estimate=pl.CostEstimate(
-            flops=pairs * rows * virt * (virt + GROUP) * 2,
-            bytes_accessed=2 * rows * virt + 2 * pairs * virt * virt,
+            flops=2 * pairs * rows * virt * (virt + GROUP) * 2,
+            bytes_accessed=2 * rows * virt + 4 * pairs * virt * virt,
             transcendentals=0,
         ),
+        compiler_params=pltpu.CompilerParams(vmem_limit_bytes=24 << 20),
         name="ladder",
     )(*operands)
 
@@ -214,20 +195,25 @@
 def body(doubles, singles, vir_slabs, occ_slabs, occ_energy, vir_energy, pair_list):
     virt = doubles.shape[2]
     zh = lax.axis_index("zh")
-    copies, own, tau, denominator = start(doubles, singles, vir_slabs, occ_slabs, occ_energy, vir_energy, pair_list)
+    copies, own, tau, denominator = start(
+        doubles, singles, vir_slabs, occ_slabs, occ_energy, vir_energy, pair_list
+    )
     dressed = exchange(copies, "zm").reshape(-1, virt)
+    other = lax.ppermute(own, "zh", SWAP)
     dressed_next = lax.ppermute(dressed, "zb", SWAP)
-    other = lax.ppermute(own, "zh", SWAP)
-    dressed = spread(jnp.stack([dressed, dressed_next]), "x").reshape(-1, virt)
     tau = lax.dynamic_update_index_in_dim(tau, other, 1 - zh, 0)
-    below = lax.ppermute(tau, "y", UP)
-    above = lax.ppermute(tau, "y", DOWN)
-    far = lax.ppermute(below, "y", UP)
-    dressed_other = lax.ppermute(dressed, "k", SWAP)
-    taus = (tau, above, far, below)
-    parts = ladder(dressed, taus)
-    parts = ladder(dressed_other, taus, parts, doubles)
-    parts = exchange(parts, AUX)
+    tau = spread(tau, "y")
+    mine = jnp.concatenate([dressed, dressed_next])
+    below = lax.ppermute(mine, "x", UP)
+    above = lax.ppermute(mine, "x", DOWN)
+    tau_other = lax.ppermute(tau, "k", SWAP)
+    far_up = lax.ppermute(below[: dressed.shape[0]], "x", UP)
+    far_down = lax.ppermute(above[dressed.shape[0] :], "x", DOWN)
+    taus = (tau, tau_other)
+    parts = ladder((mine,), taus)
+    parts = ladder((below, above), taus, parts)
+    parts = ladder((far_up, far_down), taus, parts, doubles)
+    parts = exchange(parts, ("k",) + AUX)
     return last(parts, denominator)[:, None, :]
 
 

time: 152 us -> 140 us (0.921)
  the two profiles are of different devices: /device:TPU:2 before, /device:TPU:1 now
where the time goes in v3:
time: 140 us; the launch traced here: 139 us
  starting transfers between devices  51.8 us (37%)
  blocking collectives  42.7 us (30%)
  waiting for transfers between devices  28.6 us (20%)
  Pallas kernels  14 us (10%)
  local copies, waits for them, and re-layouts  1.74 us (1%)
    all_to_all x2, blocking collectives, exchange(): return lax.all_to_all(copies, axis, split_axis=0, concat_axis=0, tiled=True)  42.7 us
    all_to_all x1, starting transfers between devices, exchange(): return lax.all_to_all(copies, axis, split_axis=0, concat_axis=0, tiled=True)  16.6 us
    ppermute x1, starting transfers between devices, body(): other = lax.ppermute(own, 'zh', SWAP)  16.2 us
    all_to_all x1, waiting for transfers between devices, exchange(): return lax.all_to_all(copies, axis, split_axis=0, concat_axis=0, tiled=True)  10.3 us
    pallas_call x3, Pallas kernels, ladder(): pl.pallas_call(functools.partial(ladder_kernel, len(slabs), has_earlier,...  9.37 us
    ppermute x1, waiting for transfers between devices, body(): below = lax.ppermute(mine, 'x', UP)  8.43 us
    ppermute x1, waiting for transfers between devices, body(): dressed_next = lax.ppermute(dressed, 'zb', SWAP)  7.04 us
    ppermute x1, starting transfers between devices, body(): far_down = lax.ppermute(above[dressed.shape[0]:], 'x', DOWN)  4.57 us
  transfers between devices with their start and end apart: 8, of which 4 were waited for; matrix products, arithmetic and copies ran while one was open for 0% of the time, Pallas kernels for 5%

profile of v3, /device:TPU:1, one launch (start us, length us, event | category | flops | bytes accessed | tf_op | source)
XLA Modules:
  0.0 139.0 jit_solution(8510937301245442757)
XLA Ops:
  0.0 3.2 %start.1 = (bf16[4,64,512]{2,1,0:T(8,128)(2,1)}, bf16[2,64,512]{2,1,0:T(8,128)(2,1)}, bf16[2,2,64,512]{3,2,1,0:T(8,128)(2,1)}, f32[2,128]{1,0:T(2,128)}) custom-call(s32[2,2]{1,0:T(2,128)} %pairs_ref.1, f32[256]{0:T(256)} %occ_energy_ref.1, f32[8]{0:T(128)} %vir_energy_ref.1, bf16[2,64,512]{2,1,0:T(8,128)(2,1)} %refs_5_.1, bf16[256,512]{1,0:T(8,128)(2,1)} %singles_ref.1, ...), custom_call_target="tpu_custom_call" | custom-call | flops 16777216 | bytes 3145728 | tf_op jit(solution)/shard_map/start/pallas_call | solution.py:72
  3.2 16.2 %collective-permute-start.5 = (bf16[2,64,512]{2,1,0:T(8,128)(2,1)}, bf16[2,64,512]{2,1,0:T(8,128)(2,1)S(1)}, u32[]{:S(2)}, u32[]{:S(2)}) collective-permute-start(bf16[2,64,512]{2,1,0:T(8,128)(2,1)} %get-tuple-element.11), channel_id=1, source_target_pairs={{0,1},{1,0},{2,3},{3,2},{4,5},{5,4},{6,7},{7,6},{8,9},{9,8},{10,11... | collective-permute-start | bytes 393224 | tf_op jit(solution)/shard_map/ppermute | solution.py:202
  19.5 2.9 %collective-permute-done.5 = bf16[2,64,512]{2,1,0:T(8,128)(2,1)S(1)} collective-permute-done((bf16[2,64,512]{2,1,0:T(8,128)(2,1)}, bf16[2,64,512]{2,1,0:T(8,128)(2,1)S(1)}, u32[]{:S(2)}, u32[]{:S(2)}) %collective-permute-start.5) | collective-permute-done | bytes 131104 | tf_op jit(solution)/shard_map/ppermute | solution.py:202
  22.3 0.7 bitcast_dynamic-update-slice_fusion
  23.0 1.0 broadcast_in_dim.14
  24.1 17.9 %all_to_all.15.refs_1_.refs_2_ = bf16[4,2,2,64,512]{4,3,2,1,0:T(8,128)(2,1)S(1)} all-to-all(bf16[4,2,2,64,512]{4,3,2,1,0:T(8,128)(2,1)S(1)} %broadcast_in_dim.14), channel_id=1, replica_groups=mesh['zm'=4,'zb'=2,'x'=4,'k'=2,'y'=4,'zh'=2] {'y'}, dimensions={0} | all-to-all | bytes 2097152 | tf_op jit(solution)/shard_map/all_to_all | solution.py:188
  42.0 16.6 %all-to-all-start = ((bf16[4,64,512]{2,1,0:T(8,128)(2,1)}), bf16[4,64,512]{2,1,0:T(8,128)(2,1)S(1)}, u32[]{:S(2)}, u32[]{:S(2)}) async-start(bf16[4,64,512]{2,1,0:T(8,128)(2,1)} %get-tuple-element.9), calls=%async_computation | async-start | bytes 524288 | tf_op jit(solution)/shard_map/all_to_all | solution.py:188
  58.6 4.0 %collective-permute-start.6 = (bf16[4,2,2,64,512]{4,3,2,1,0:T(8,128)(2,1)S(1)}, bf16[4,2,2,64,512]{4,3,2,1,0:T(8,128)(2,1)S(1)}, u32[]{:S(2)}, u32[]{:S(2)}) collective-permute-start(bf16[4,2,2,64,512]{4,3,2,1,0:T(8,128)(2,1)S(1)} %all_to_all.15.refs_1_.refs_2_), channel_id=1, source_target_pairs={{0,8},{8,0},{1,9},{9,1},{2,10},{10,2},{3,11},{11,3},{4,12},{12,4},... | collective-permute-start | bytes 3145736 | tf_op jit(solution)/shard_map/ppermute | solution.py:209
  62.6 10.3 %all-to-all-done = bf16[4,64,512]{2,1,0:T(8,128)(2,1)S(1)} async-done(((bf16[4,64,512]{2,1,0:T(8,128)(2,1)}), bf16[4,64,512]{2,1,0:T(8,128)(2,1)S(1)}, u32[]{:S(2)}, u32[]{:S(2)}) %all-to-all-start) | async-done | bytes 262176 | tf_op jit(solution)/shard_map/all_to_all | solution.py:188
  72.9 1.9 %collective-permute-start = (bf16[256,512]{1,0:T(8,128)(2,1)S(1)}, bf16[256,512]{1,0:T(8,128)(2,1)S(1)}, u32[]{:S(2)}, u32[]{:S(2)}) collective-permute-start(bf16[256,512]{1,0:T(8,128)(2,1)S(1)} %bitcast.6), channel_id=1, source_target_pairs={{0,64},{64,0},{1,65},{65,1},{2,66},{66,2},{3,67},{67,3},{4,68},{68... | collective-permute-start | bytes 786440 | tf_op jit(solution)/shard_map/ppermute | solution.py:203
  74.8 7.0 %collective-permute-done = bf16[256,512]{1,0:T(8,128)(2,1)S(1)} collective-permute-done((bf16[256,512]{1,0:T(8,128)(2,1)S(1)}, bf16[256,512]{1,0:T(8,128)(2,1)S(1)}, u32[]{:S(2)}, u32[]{:S(2)}) %collective-permute-start) | collective-permute-done | bytes 262176 | tf_op jit(solution)/shard_map/ppermute | solution.py:203
  81.9 3.1 %collective-permute-start.1 = (bf16[512,512]{1,0:T(8,128)(2,1)S(1)}, bf16[512,512]{1,0:T(8,128)(2,1)S(1)}, u32[]{:S(2)}, u32[]{:S(2)}) collective-permute-start(bf16[512,512]{1,0:T(8,128)(2,1)S(1)} %pad_maximum_fusion.refs_0_), channel_id=1, source_target_pairs={{0,16},{16,32},{32,48},{48,0},{1,17},{17,33},{33,49},{49,1},{2,18}... | collective-permute-start | bytes 1572872 | tf_op jit(solution)/shard_map/ppermute | solution.py:207
  85.0 3.4 %collective-permute-start.3 = (bf16[512,512]{1,0:T(8,128)(2,1)S(1)}, bf16[512,512]{1,0:T(8,128)(2,1)S(1)}, u32[]{:S(2)}, u32[]{:S(2)}) collective-permute-start(bf16[512,512]{1,0:T(8,128)(2,1)S(1)} %pad_maximum_fusion.refs_0_), channel_id=1, source_target_pairs={{0,48},{16,0},{32,16},{48,32},{1,49},{17,1},{33,17},{49,33},{2,50}... | collective-permute-start | bytes 1572872 | tf_op jit(solution)/shard_map/ppermute | solution.py:208
  88.4 8.4 %collective-permute-done.1.refs_0_ = bf16[512,512]{1,0:T(8,128)(2,1)S(1)} collective-permute-done((bf16[512,512]{1,0:T(8,128)(2,1)S(1)}, bf16[512,512]{1,0:T(8,128)(2,1)S(1)}, u32[]{:S(2)}, u32[]{:S(2)}) %collective-permute-start.1) | collective-permute-done | bytes 524320 | tf_op jit(solution)/shard_map/ppermute | solution.py:207
  96.8 1.9 %collective-permute-start.2 = (bf16[256,512]{1,0:T(8,128)(2,1)S(1)}, bf16[256,512]{1,0:T(8,128)(2,1)S(1)}, u32[]{:S(2)}, u32[]{:S(2)}) collective-permute-start(bf16[256,512]{1,0:T(8,128)(2,1)S(1)} %slice.8), channel_id=1, source_target_pairs={{0,16},{16,32},{32,48},{48,0},{1,17},{17,33},{33,49},{49,1},{2,18}... | collective-permute-start | bytes 786440 | tf_op jit(solution)/shard_map/ppermute | solution.py:210
  98.8 4.6 %collective-permute-start.4 = (bf16[256,512]{1,0:T(8,128)(2,1)S(1)}, bf16[256,512]{1,0:T(8,128)(2,1)S(1)}, u32[]{:S(2)}, u32[]{:S(2)}) collective-permute-start(bf16[256,512]{1,0:T(8,128)(2,1)S(1)} %slice.9), channel_id=1, source_target_pairs={{0,48},{16,0},{32,16},{48,32},{1,49},{17,1},{33,17},{49,33},{2,50}... | collective-permute-start | bytes 786440 | tf_op jit(solution)/shard_map/ppermute | solution.py:211
  103.4 2.6 %ladder.3.refs_4_ = f32[4,8,128]{2,1,0:T(8,128)S(1)} custom-call(bf16[512,512]{1,0:T(8,128)(2,1)S(1)} %pad_maximum_fusion.refs_0_, bf16[4,2,2,64,512]{4,3,2,1,0:T(8,128)(2,1)S(1)} %all_to_all.15.refs_1_.refs_2_, bf16[4,2,2,64,512]{4,3,2,1,0:T(8,128)(2,1)S(1)} %collective-permute-done.6.refs_2_.refs_3_), custom_call_target="tpu_custom_call" | custom-call | flops 1610612736 | bytes 2621440 | tf_op jit(solution)/shard_map/ladder/pallas_call | solution.py:155
  106.1 4.3 %ladder.4.refs_4_ = f32[4,8,128]{2,1,0:T(8,128)S(1)} custom-call(bf16[512,512]{1,0:T(8,128)(2,1)S(1)} %collective-permute-done.1.refs_0_, bf16[512,512]{1,0:T(8,128)(2,1)S(1)} %collective-permute-done.3.refs_1_, bf16[4,2,2,64,512]{4,3,2,1,0:T(8,128)(2,1)S(1)} %all_to_all.15.refs_1_.refs_2_, ...), custom_call_target="tpu_custom_call" | custom-call | flops 3221225472 | bytes 3145728 | tf_op jit(solution)/shard_map/ladder/pallas_call | solution.py:155
  110.3 0.0 collective-permute-done.2.refs_0_
  110.3 0.0 collective-permute-done.4.refs_1_
  110.3 0.0 copy-done
  110.3 2.5 %ladder.5 = f32[16,2,128]{2,1,0:T(2,128)S(1)} custom-call(bf16[256,512]{1,0:T(8,128)(2,1)S(1)} %collective-permute-done.2.refs_0_, bf16[256,512]{1,0:T(8,128)(2,1)S(1)} %collective-permute-done.4.refs_1_, bf16[4,2,2,64,512]{4,3,2,1,0:T(8,128)(2,1)S(1)} %all_to_all.15.refs_1_.refs_2_, bf16[4,2,2,64,512]{4,3,2,1,0:T(8,128)(2,1)S(1)} %collective-permute-done.6.refs_2_.refs_3_, ...), custom_call_target="tpu_custom_call" | custom-call | flops 1610612736 | bytes 2621440 | tf_op jit(solution)/shard_map/ladder/pallas_call | solution.py:155
  112.8 24.8 %all_to_all.16.parts_ref = f32[16,2,128]{2,1,0:T(2,128)} all-to-all(f32[16,2,128]{2,1,0:T(2,128)S(1)} %ladder.5), channel_id=1, replica_groups=mesh['zm'=4,'zb'=2,'x'=4,'k'=2,'y'=4,'zh'=2] {'k','y','zh'}, dimensions={0} | all-to-all | bytes 32768 | tf_op jit(solution)/shard_map/all_to_all | solution.py:188
  137.6 1.4 last.1
  (6 shorter events, 0.1 us)
Async XLA Ops:
  3.2 19.1 %collective-permute-start.5 = (bf16[2,64,512]{2,1,0:T(8,128)(2,1)}, bf16[2,64,512]{2,1,0:T(8,128)(2,1)S(1)}, u32[]{:S(2)}, u32[]{:S(2)}) collective-permute-start(bf16[2,64,512]{2,1,0:T(8,128)(2,1)} %get-tuple-element.11), channel_id=1, source_target_pairs={{0,1},{1,0},{2,3},{3,2},{4,5},{5,4},{6,7},{7,6},{8,9},{9,8},{10,11... | collective-permute-start | bytes 393224 | tf_op jit(solution)/shard_map/ppermute | solution.py:202
  42.0 30.9 %all-to-all-start = ((bf16[4,64,512]{2,1,0:T(8,128)(2,1)}), bf16[4,64,512]{2,1,0:T(8,128)(2,1)S(1)}, u32[]{:S(2)}, u32[]{:S(2)}) async-start(bf16[4,64,512]{2,1,0:T(8,128)(2,1)} %get-tuple-element.9), calls=%async_computation | async-start | bytes 524288 | tf_op jit(solution)/shard_map/all_to_all | solution.py:188
  58.6 44.8 %collective-permute-start.6 = (bf16[4,2,2,64,512]{4,3,2,1,0:T(8,128)(2,1)S(1)}, bf16[4,2,2,64,512]{4,3,2,1,0:T(8,128)(2,1)S(1)}, u32[]{:S(2)}, u32[]{:S(2)}) collective-permute-start(bf16[4,2,2,64,512]{4,3,2,1,0:T(8,128)(2,1)S(1)} %all_to_all.15.refs_1_.refs_2_), channel_id=1, source_target_pairs={{0,8},{8,0},{1,9},{9,1},{2,10},{10,2},{3,11},{11,3},{4,12},{12,4},... | collective-permute-start | bytes 3145736 | tf_op jit(solution)/shard_map/ppermute | solution.py:209
  72.9 9.0 %collective-permute-start = (bf16[256,512]{1,0:T(8,128)(2,1)S(1)}, bf16[256,512]{1,0:T(8,128)(2,1)S(1)}, u32[]{:S(2)}, u32[]{:S(2)}) collective-permute-start(bf16[256,512]{1,0:T(8,128)(2,1)S(1)} %bitcast.6), channel_id=1, source_target_pairs={{0,64},{64,0},{1,65},{65,1},{2,66},{66,2},{3,67},{67,3},{4,68},{68... | collective-permute-start | bytes 786440 | tf_op jit(solution)/shard_map/ppermute | solution.py:203
  81.9 14.9 %collective-permute-start.1 = (bf16[512,512]{1,0:T(8,128)(2,1)S(1)}, bf16[512,512]{1,0:T(8,128)(2,1)S(1)}, u32[]{:S(2)}, u32[]{:S(2)}) collective-permute-start(bf16[512,512]{1,0:T(8,128)(2,1)S(1)} %pad_maximum_fusion.refs_0_), channel_id=1, source_target_pairs={{0,16},{16,32},{32,48},{48,0},{1,17},{17,33},{33,49},{49,1},{2,18}... | collective-permute-start | bytes 1572872 | tf_op jit(solution)/shard_map/ppermute | solution.py:207
  85.0 13.8 %collective-permute-start.3 = (bf16[512,512]{1,0:T(8,128)(2,1)S(1)}, bf16[512,512]{1,0:T(8,128)(2,1)S(1)}, u32[]{:S(2)}, u32[]{:S(2)}) collective-permute-start(bf16[512,512]{1,0:T(8,128)(2,1)S(1)} %pad_maximum_fusion.refs_0_), channel_id=1, source_target_pairs={{0,48},{16,0},{32,16},{48,32},{1,49},{17,1},{33,17},{49,33},{2,50}... | collective-permute-start | bytes 1572872 | tf_op jit(solution)/shard_map/ppermute | solution.py:208
  96.8 13.5 %collective-permute-start.2 = (bf16[256,512]{1,0:T(8,128)(2,1)S(1)}, bf16[256,512]{1,0:T(8,128)(2,1)S(1)}, u32[]{:S(2)}, u32[]{:S(2)}) collective-permute-start(bf16[256,512]{1,0:T(8,128)(2,1)S(1)} %slice.8), channel_id=1, source_target_pairs={{0,16},{16,32},{32,48},{48,0},{1,17},{17,33},{33,49},{49,1},{2,18}... | collective-permute-start | bytes 786440 | tf_op jit(solution)/shard_map/ppermute | solution.py:210
  98.8 11.5 %collective-permute-start.4 = (bf16[256,512]{1,0:T(8,128)(2,1)S(1)}, bf16[256,512]{1,0:T(8,128)(2,1)S(1)}, u32[]{:S(2)}, u32[]{:S(2)}) collective-permute-start(bf16[256,512]{1,0:T(8,128)(2,1)S(1)} %slice.9), channel_id=1, source_target_pairs={{0,48},{16,0},{32,16},{48,32},{1,49},{17,1},{33,17},{49,33},{2,50}... | collective-permute-start | bytes 786440 | tf_op jit(solution)/shard_map/ppermute | solution.py:211
  106.1 4.3 %copy-start = (bf16[2,64,512]{2,1,0:T(8,128)(2,1)S(1)}, bf16[2,64,512]{2,1,0:T(8,128)(2,1)}, u32[]{:S(2)}) copy-start(bf16[2,64,512]{2,1,0:T(8,128)(2,1)} %refs_5_.1) | copy-start | bytes 393220

commit v4 on v3

--- a/solution.py
+++ b/solution.py
@@ -21,11 +21,10 @@
 
 def start_kernel(
     pairs_ref, occ_energy_ref, vir_energy_ref, doubles_ref, singles_ref, vir_ref, occ_ref,
-    dressed_ref, own_ref, tau_ref, denominator_ref, cols_ref,
+    dressed_ref, own_ref, denominator_ref, cols_ref,
 ):
     local_pairs, chunk, _ = doubles_ref.shape
-    zh = lax.axis_index("zh")
-    aux = lax.axis_index("y") * 2 + zh
+    aux = lax.axis_index("y") * 2 + lax.axis_index("zh")
     singles = singles_ref[...]
     occ = singles.shape[0]
     window = singles[:, :128].astype(jnp.float32).T[:NWIN].astype(jnp.bfloat16)
@@ -55,7 +54,6 @@
         outer = cols[:, pair : pair + 1] * rows[pair : pair + 1, :]
         tau = (doubles_ref[pair].astype(jnp.float32) + outer).astype(jnp.bfloat16)
         own_ref[pair] = tau
-        tau_ref[zh, pair] = tau
     lane = lax.broadcasted_iota(jnp.int32, (1, 128), 1)
     vir = jnp.zeros((1, 128), jnp.float32)
     for b in range(NWIN):
@@ -63,7 +61,7 @@
     for pair in range(local_pairs):
         energy = occ_energy_ref[pairs_ref[pair, 0]] + occ_energy_ref[pairs_ref[pair, 1]]
         value = (energy - vir_energy_ref[aux]) - vir
-        denominator_ref[pair : pair + 1] = jnp.where(lane < NWIN, value, 1.0)
+        denominator_ref[pair : pair + 1] = jnp.where(lane < NWIN, value, 0.0)
 
 
 def start(doubles, singles, vir_slabs, occ_slabs, occ_energy, vir_energy, pair_list):
@@ -74,11 +72,10 @@
         out_shape=(
             jax.ShapeDtypeStruct((4, slabs * NWIN, virt), jnp.bfloat16),
             jax.ShapeDtypeStruct((local_pairs, chunk, virt), jnp.bfloat16),
-            jax.ShapeDtypeStruct((2, local_pairs, chunk, virt), jnp.bfloat16),
             jax.ShapeDtypeStruct((local_pairs, 128), jnp.float32),
         ),
         in_specs=[SMEM] * 3 + [VMEM] * 4,
-        out_specs=(VMEM,) * 4,
+        out_specs=(VMEM,) * 3,
         scratch_shapes=[pltpu.VMEM((virt, 128), jnp.float32)],
         cost_estimate=pl.CostEstimate(flops=slabs * NWIN * occ * virt * 2, bytes_accessed=3 << 20, transcendentals=0),
         name="start",
@@ -168,53 +165,53 @@
     )(*operands)
 
 
-def last_kernel(parts_ref, denominator_ref, out_ref):
-    total = jnp.sum(parts_ref[...], axis=0)
-    value = pltpu.roll(total, 128 - NWIN, 1) + total / denominator_ref[...]
-    out_ref[...] = value[:, :NWIN]
-
-
-def last(parts, denominator):
+def join_kernel(own_ref, other_ref, out_ref):
+    zh = lax.axis_index("zh")
+    for copy in range(out_ref.shape[0]):
+        out_ref[copy, zh] = own_ref[...]
+        out_ref[copy, 1 - zh] = other_ref[...]
+
+
+def join(own, other):
     return pl.pallas_call(
-        last_kernel,
-        out_shape=jax.ShapeDtypeStruct((parts.shape[1], NWIN), jnp.float32),
+        join_kernel,
+        out_shape=jax.ShapeDtypeStruct((4, 2) + own.shape, own.dtype),
         in_specs=[VMEM, VMEM],
         out_specs=VMEM,
-        name="last",
-    )(parts, denominator)
+        compiler_params=pltpu.CompilerParams(vmem_limit_bytes=6 << 20),
+        name="join",
+    )(own, other)
 
 
 def exchange(copies, axis):
     return lax.all_to_all(copies, axis, split_axis=0, concat_axis=0, tiled=True)
 
 
-def spread(value, axis):
-    return exchange(jnp.broadcast_to(value[None], (lax.axis_size(axis),) + value.shape), axis)
-
-
 def body(doubles, singles, vir_slabs, occ_slabs, occ_energy, vir_energy, pair_list):
     virt = doubles.shape[2]
-    zh = lax.axis_index("zh")
-    copies, own, tau, denominator = start(
+    copies, own, denominator = start(
         doubles, singles, vir_slabs, occ_slabs, occ_energy, vir_energy, pair_list
     )
     dressed = exchange(copies, "zm").reshape(-1, virt)
     other = lax.ppermute(own, "zh", SWAP)
     dressed_next = lax.ppermute(dressed, "zb", SWAP)
-    tau = lax.dynamic_update_index_in_dim(tau, other, 1 - zh, 0)
-    tau = spread(tau, "y")
+    copies = join(own, other)
+    tau = exchange(copies, "y")
     mine = jnp.concatenate([dressed, dressed_next])
     below = lax.ppermute(mine, "x", UP)
     above = lax.ppermute(mine, "x", DOWN)
     tau_other = lax.ppermute(tau, "k", SWAP)
     far_up = lax.ppermute(below[: dressed.shape[0]], "x", UP)
     far_down = lax.ppermute(above[dressed.shape[0] :], "x", DOWN)
+    denominator = lax.optimization_barrier(denominator[:, :NWIN] + denominator[:, 64 : 64 + NWIN])
     taus = (tau, tau_other)
     parts = ladder((mine,), taus)
     parts = ladder((below, above), taus, parts)
     parts = ladder((far_up, far_down), taus, parts, doubles)
     parts = exchange(parts, ("k",) + AUX)
-    return last(parts, denominator)[:, None, :]
+    total = jnp.sum(parts, axis=0)
+    residual = total[:, :NWIN] / denominator
+    return (total[:, NWIN : 2 * NWIN] + residual)[:, None, :]
 
 
 def solution(mesh):

time: 140 us -> 139 us (level)
  blocking collectives: 42.7 us -> 17.9 us
  waiting for transfers between devices: 28.6 us -> 42.8 us
  starting transfers between devices: 51.8 us -> 62.5 us
    all_to_all x2 -> x1, blocking collectives: 42.7 us -> 17.9 us  [exchange(): return lax.all_to_all(copies, axis, split_axis=0, concat_axis=0, tiled=True)]
    all_to_all x1 -> x2, waiting for transfers between devices: 10.3 us -> 24.4 us  [exchange(): return lax.all_to_all(copies, axis, split_axis=0, concat_axis=0, tiled=True)]
    all_to_all x1 -> x2, starting transfers between devices: 16.6 us -> 27.3 us  [exchange(): return lax.all_to_all(copies, axis, split_axis=0, concat_axis=0, tiled=True)]
  transfers between devices with their start and end apart: 8 -> 9, of which waited for: 4 -> 5; matrix products, arithmetic and copies ran while one was open for 0% -> 0% of each run, Pallas kernels for 5% -> 5%
where the time goes in v4:
time: 139 us; the launch traced here: 138 us
  starting transfers between devices  62.5 us (45%)
  waiting for transfers between devices  42.8 us (31%)
  blocking collectives  17.9 us (13%)
  Pallas kernels  13.2 us (9%)
    all_to_all x2, starting transfers between devices, exchange(): return lax.all_to_all(copies, axis, split_axis=0, concat_axis=0, tiled=True)  27.3 us
    all_to_all x2, waiting for transfers between devices, exchange(): return lax.all_to_all(copies, axis, split_axis=0, concat_axis=0, tiled=True)  24.4 us
    all_to_all x1, blocking collectives, exchange(): return lax.all_to_all(copies, axis, split_axis=0, concat_axis=0, tiled=True)  17.9 us
    ppermute x1, starting transfers between devices, body(): other = lax.ppermute(own, 'zh', SWAP)  16.2 us
    pallas_call x3, Pallas kernels, ladder(): pl.pallas_call(functools.partial(ladder_kernel, len(slabs), has_earlier,...  9.98 us
    ppermute x1, waiting for transfers between devices, body(): below = lax.ppermute(mine, 'x', UP)  8.43 us
    ppermute x1, waiting for transfers between devices, body(): dressed_next = lax.ppermute(dressed, 'zb', SWAP)  7.04 us
    ppermute x1, starting transfers between devices, body(): far_down = lax.ppermute(above[dressed.shape[0]:], 'x', DOWN)  4.57 us
  transfers between devices with their start and end apart: 9, of which 5 were waited for; matrix products, arithmetic and copies ran while one was open for 0% of the time, Pallas kernels for 5%

profile of v4, /device:TPU:1, one launch (start us, length us, event | category | flops | bytes accessed | tf_op | source)
XLA Modules:
  0.0 138.2 jit_solution(10683983902922930956)
XLA Ops:
  0.0 3.1 %start.1 = (bf16[4,64,512]{2,1,0:T(8,128)(2,1)}, bf16[2,64,512]{2,1,0:T(8,128)(2,1)}, f32[2,128]{1,0:T(2,128)}) custom-call(s32[2,2]{1,0:T(2,128)} %pairs_ref.1, f32[256]{0:T(256)} %occ_energy_ref.1, f32[8]{0:T(128)} %vir_energy_ref.1, bf16[2,64,512]{2,1,0:T(8,128)(2,1)} %refs_5_.1, bf16[256,512]{1,0:T(8,128)(2,1)} %singles_ref.1, ...), custom_call_target="tpu_custom_call" | custom-call | flops 16777216 | bytes 3145728 | tf_op jit(solution)/shard_map/start/pallas_call | solution.py:70
  3.1 16.2 %collective-permute-start.5 = (bf16[2,64,512]{2,1,0:T(8,128)(2,1)}, bf16[2,64,512]{2,1,0:T(8,128)(2,1)S(1)}, u32[]{:S(2)}, u32[]{:S(2)}) collective-permute-start(bf16[2,64,512]{2,1,0:T(8,128)(2,1)} %get-tuple-element.9.own_ref), channel_id=1, source_target_pairs={{0,1},{1,0},{2,3},{3,2},{4,5},{5,4},{6,7},{7,6},{8,9},{9,8},{10,11... | collective-permute-start | bytes 393224 | tf_op jit(solution)/shard_map/ppermute | solution.py:196
  19.4 2.9 %collective-permute-done.5.other_ref = bf16[2,64,512]{2,1,0:T(8,128)(2,1)S(1)} collective-permute-done((bf16[2,64,512]{2,1,0:T(8,128)(2,1)}, bf16[2,64,512]{2,1,0:T(8,128)(2,1)S(1)}, u32[]{:S(2)}, u32[]{:S(2)}) %collective-permute-start.5) | collective-permute-done | bytes 131104 | tf_op jit(solution)/shard_map/ppermute | solution.py:196
  22.2 0.9 copy-done.1
  23.1 0.1 join.1
  23.2 17.9 %all_to_all.15.refs_1_.refs_2_ = bf16[4,2,2,64,512]{4,3,2,1,0:T(8,128)(2,1)S(1)} all-to-all(bf16[4,2,2,64,512]{4,3,2,1,0:T(8,128)(2,1)S(1)} %join.1), channel_id=1, replica_groups=mesh['zm'=4,'zb'=2,'x'=4,'k'=2,'y'=4,'zh'=2] {'y'}, dimensions={0} | all-to-all | bytes 2097152 | tf_op jit(solution)/shard_map/all_to_all | solution.py:187
  41.1 16.6 %all-to-all-start = ((bf16[4,64,512]{2,1,0:T(8,128)(2,1)}), bf16[4,64,512]{2,1,0:T(8,128)(2,1)S(1)}, u32[]{:S(2)}, u32[]{:S(2)}) async-start(bf16[4,64,512]{2,1,0:T(8,128)(2,1)} %get-tuple-element.8), calls=%async_computation | async-start | bytes 524288 | tf_op jit(solution)/shard_map/all_to_all | solution.py:187
  57.8 4.0 %collective-permute-start.6 = (bf16[4,2,2,64,512]{4,3,2,1,0:T(8,128)(2,1)S(1)}, bf16[4,2,2,64,512]{4,3,2,1,0:T(8,128)(2,1)S(1)}, u32[]{:S(2)}, u32[]{:S(2)}) collective-permute-start(bf16[4,2,2,64,512]{4,3,2,1,0:T(8,128)(2,1)S(1)} %all_to_all.15.refs_1_.refs_2_), channel_id=1, source_target_pairs={{0,8},{8,0},{1,9},{9,1},{2,10},{10,2},{3,11},{11,3},{4,12},{12,4},... | collective-permute-start | bytes 3145736 | tf_op jit(solution)/shard_map/ppermute | solution.py:203
  61.8 10.3 %all-to-all-done = bf16[4,64,512]{2,1,0:T(8,128)(2,1)S(1)} async-done(((bf16[4,64,512]{2,1,0:T(8,128)(2,1)}), bf16[4,64,512]{2,1,0:T(8,128)(2,1)S(1)}, u32[]{:S(2)}, u32[]{:S(2)}) %all-to-all-start) | async-done | bytes 262176 | tf_op jit(solution)/shard_map/all_to_all | solution.py:187
  72.1 1.9 %collective-permute-start = (bf16[256,512]{1,0:T(8,128)(2,1)S(1)}, bf16[256,512]{1,0:T(8,128)(2,1)S(1)}, u32[]{:S(2)}, u32[]{:S(2)}) collective-permute-start(bf16[256,512]{1,0:T(8,128)(2,1)S(1)} %bitcast.4), channel_id=1, source_target_pairs={{0,64},{64,0},{1,65},{65,1},{2,66},{66,2},{3,67},{67,3},{4,68},{68... | collective-permute-start | bytes 786440 | tf_op jit(solution)/shard_map/ppermute | solution.py:197
  74.0 7.0 %collective-permute-done = bf16[256,512]{1,0:T(8,128)(2,1)S(1)} collective-permute-done((bf16[256,512]{1,0:T(8,128)(2,1)S(1)}, bf16[256,512]{1,0:T(8,128)(2,1)S(1)}, u32[]{:S(2)}, u32[]{:S(2)}) %collective-permute-start) | collective-permute-done | bytes 262176 | tf_op jit(solution)/shard_map/ppermute | solution.py:197
  81.1 3.1 %collective-permute-start.1 = (bf16[512,512]{1,0:T(8,128)(2,1)S(1)}, bf16[512,512]{1,0:T(8,128)(2,1)S(1)}, u32[]{:S(2)}, u32[]{:S(2)}) collective-permute-start(bf16[512,512]{1,0:T(8,128)(2,1)S(1)} %pad_maximum_fusion.refs_0_), channel_id=1, source_target_pairs={{0,16},{16,32},{32,48},{48,0},{1,17},{17,33},{33,49},{49,1},{2,18}... | collective-permute-start | bytes 1572872 | tf_op jit(solution)/shard_map/ppermute | solution.py:201
  84.2 3.4 %collective-permute-start.3 = (bf16[512,512]{1,0:T(8,128)(2,1)S(1)}, bf16[512,512]{1,0:T(8,128)(2,1)S(1)}, u32[]{:S(2)}, u32[]{:S(2)}) collective-permute-start(bf16[512,512]{1,0:T(8,128)(2,1)S(1)} %pad_maximum_fusion.refs_0_), channel_id=1, source_target_pairs={{0,48},{16,0},{32,16},{48,32},{1,49},{17,1},{33,17},{49,33},{2,50}... | collective-permute-start | bytes 1572872 | tf_op jit(solution)/shard_map/ppermute | solution.py:202
  87.6 8.4 %collective-permute-done.1.refs_0_ = bf16[512,512]{1,0:T(8,128)(2,1)S(1)} collective-permute-done((bf16[512,512]{1,0:T(8,128)(2,1)S(1)}, bf16[512,512]{1,0:T(8,128)(2,1)S(1)}, u32[]{:S(2)}, u32[]{:S(2)}) %collective-permute-start.1) | collective-permute-done | bytes 524320 | tf_op jit(solution)/shard_map/ppermute | solution.py:201
  96.0 1.9 %collective-permute-start.2 = (bf16[256,512]{1,0:T(8,128)(2,1)S(1)}, bf16[256,512]{1,0:T(8,128)(2,1)S(1)}, u32[]{:S(2)}, u32[]{:S(2)}) collective-permute-start(bf16[256,512]{1,0:T(8,128)(2,1)S(1)} %slice.24), channel_id=1, source_target_pairs={{0,16},{16,32},{32,48},{48,0},{1,17},{17,33},{33,49},{49,1},{2,18}... | collective-permute-start | bytes 786440 | tf_op jit(solution)/shard_map/ppermute | solution.py:204
  98.0 4.6 %collective-permute-start.4 = (bf16[256,512]{1,0:T(8,128)(2,1)S(1)}, bf16[256,512]{1,0:T(8,128)(2,1)S(1)}, u32[]{:S(2)}, u32[]{:S(2)}) collective-permute-start(bf16[256,512]{1,0:T(8,128)(2,1)S(1)} %slice.25), channel_id=1, source_target_pairs={{0,48},{16,0},{32,16},{48,32},{1,49},{17,1},{33,17},{49,33},{2,50}... | collective-permute-start | bytes 786440 | tf_op jit(solution)/shard_map/ppermute | solution.py:205
  102.6 2.6 %ladder.3.refs_4_ = f32[4,8,128]{2,1,0:T(8,128)S(1)} custom-call(bf16[512,512]{1,0:T(8,128)(2,1)S(1)} %pad_maximum_fusion.refs_0_, bf16[4,2,2,64,512]{4,3,2,1,0:T(8,128)(2,1)S(1)} %all_to_all.15.refs_1_.refs_2_, bf16[4,2,2,64,512]{4,3,2,1,0:T(8,128)(2,1)S(1)} %collective-permute-done.6.refs_2_.refs_3_), custom_call_target="tpu_custom_call" | custom-call | flops 1610612736 | bytes 2621440 | tf_op jit(solution)/shard_map/ladder/pallas_call | solution.py:152
  105.3 4.3 %ladder.4.refs_4_ = f32[4,8,128]{2,1,0:T(8,128)S(1)} custom-call(bf16[512,512]{1,0:T(8,128)(2,1)S(1)} %collective-permute-done.1.refs_0_, bf16[512,512]{1,0:T(8,128)(2,1)S(1)} %collective-permute-done.3.refs_1_, bf16[4,2,2,64,512]{4,3,2,1,0:T(8,128)(2,1)S(1)} %all_to_all.15.refs_1_.refs_2_, ...), custom_call_target="tpu_custom_call" | custom-call | flops 3221225472 | bytes 3145728 | tf_op jit(solution)/shard_map/ladder/pallas_call | solution.py:152
  109.5 0.0 collective-permute-done.4.refs_1_
  109.5 3.1 %ladder.5 = f32[16,2,128]{2,1,0:T(2,128)} custom-call(bf16[256,512]{1,0:T(8,128)(2,1)S(1)} %collective-permute-done.2.refs_0_, bf16[256,512]{1,0:T(8,128)(2,1)S(1)} %collective-permute-done.4.refs_1_, bf16[4,2,2,64,512]{4,3,2,1,0:T(8,128)(2,1)S(1)} %all_to_all.15.refs_1_.refs_2_, bf16[4,2,2,64,512]{4,3,2,1,0:T(8,128)(2,1)S(1)} %collective-permute-done.6.refs_2_.refs_3_, ...), custom_call_target="tpu_custom_call" | custom-call | flops 1610612736 | bytes 2621440 | tf_op jit(solution)/shard_map/ladder/pallas_call | solution.py:152
  112.6 10.7 %all-to-all-start.2 = ((f32[16,2,128]{2,1,0:T(2,128)}), f32[16,2,128]{2,1,0:T(2,128)S(1)}, u32[]{:S(2)}, u32[]{:S(2)}) async-start(f32[16,2,128]{2,1,0:T(2,128)} %ladder.5), calls=%async_computation.2 | async-start | bytes 32768 | tf_op jit(solution)/shard_map/all_to_all | solution.py:187
  123.3 0.1 slice_add_fusion
  123.4 14.1 %all-to-all-done.2 = f32[16,2,128]{2,1,0:T(2,128)S(1)} async-done(((f32[16,2,128]{2,1,0:T(2,128)}), f32[16,2,128]{2,1,0:T(2,128)S(1)}, u32[]{:S(2)}, u32[]{:S(2)}) %all-to-all-start.2) | async-done | bytes 16416 | tf_op jit(solution)/shard_map/all_to_all | solution.py:187
  137.5 0.6 divide_add_fusion
  (12 shorter events, 0.1 us)
Async XLA Ops:
  3.1 19.1 %collective-permute-start.5 = (bf16[2,64,512]{2,1,0:T(8,128)(2,1)}, bf16[2,64,512]{2,1,0:T(8,128)(2,1)S(1)}, u32[]{:S(2)}, u32[]{:S(2)}) collective-permute-start(bf16[2,64,512]{2,1,0:T(8,128)(2,1)} %get-tuple-element.9.own_ref), channel_id=1, source_target_pairs={{0,1},{1,0},{2,3},{3,2},{4,5},{5,4},{6,7},{7,6},{8,9},{9,8},{10,11... | collective-permute-start | bytes 393224 | tf_op jit(solution)/shard_map/ppermute | solution.py:196
  22.2 0.9 copy-start.1
  41.1 30.9 %all-to-all-start = ((bf16[4,64,512]{2,1,0:T(8,128)(2,1)}), bf16[4,64,512]{2,1,0:T(8,128)(2,1)S(1)}, u32[]{:S(2)}, u32[]{:S(2)}) async-start(bf16[4,64,512]{2,1,0:T(8,128)(2,1)} %get-tuple-element.8), calls=%async_computation | async-start | bytes 524288 | tf_op jit(solution)/shard_map/all_to_all | solution.py:187
  57.8 44.8 %collective-permute-start.6 = (bf16[4,2,2,64,512]{4,3,2,1,0:T(8,128)(2,1)S(1)}, bf16[4,2,2,64,512]{4,3,2,1,0:T(8,128)(2,1)S(1)}, u32[]{:S(2)}, u32[]{:S(2)}) collective-permute-start(bf16[4,2,2,64,512]{4,3,2,1,0:T(8,128)(2,1)S(1)} %all_to_all.15.refs_1_.refs_2_), channel_id=1, source_target_pairs={{0,8},{8,0},{1,9},{9,1},{2,10},{10,2},{3,11},{11,3},{4,12},{12,4},... | collective-permute-start | bytes 3145736 | tf_op jit(solution)/shard_map/ppermute | solution.py:203
  72.1 9.0 %collective-permute-start = (bf16[256,512]{1,0:T(8,128)(2,1)S(1)}, bf16[256,512]{1,0:T(8,128)(2,1)S(1)}, u32[]{:S(2)}, u32[]{:S(2)}) collective-permute-start(bf16[256,512]{1,0:T(8,128)(2,1)S(1)} %bitcast.4), channel_id=1, source_target_pairs={{0,64},{64,0},{1,65},{65,1},{2,66},{66,2},{3,67},{67,3},{4,68},{68... | collective-permute-start | bytes 786440 | tf_op jit(solution)/shard_map/ppermute | solution.py:197
  81.1 14.9 %collective-permute-start.1 = (bf16[512,512]{1,0:T(8,128)(2,1)S(1)}, bf16[512,512]{1,0:T(8,128)(2,1)S(1)}, u32[]{:S(2)}, u32[]{:S(2)}) collective-permute-start(bf16[512,512]{1,0:T(8,128)(2,1)S(1)} %pad_maximum_fusion.refs_0_), channel_id=1, source_target_pairs={{0,16},{16,32},{32,48},{48,0},{1,17},{17,33},{33,49},{49,1},{2,18}... | collective-permute-start | bytes 1572872 | tf_op jit(solution)/shard_map/ppermute | solution.py:201
  84.2 13.8 %collective-permute-start.3 = (bf16[512,512]{1,0:T(8,128)(2,1)S(1)}, bf16[512,512]{1,0:T(8,128)(2,1)S(1)}, u32[]{:S(2)}, u32[]{:S(2)}) collective-permute-start(bf16[512,512]{1,0:T(8,128)(2,1)S(1)} %pad_maximum_fusion.refs_0_), channel_id=1, source_target_pairs={{0,48},{16,0},{32,16},{48,32},{1,49},{17,1},{33,17},{49,33},{2,50}... | collective-permute-start | bytes 1572872 | tf_op jit(solution)/shard_map/ppermute | solution.py:202
  96.0 13.5 %collective-permute-start.2 = (bf16[256,512]{1,0:T(8,128)(2,1)S(1)}, bf16[256,512]{1,0:T(8,128)(2,1)S(1)}, u32[]{:S(2)}, u32[]{:S(2)}) collective-permute-start(bf16[256,512]{1,0:T(8,128)(2,1)S(1)} %slice.24), channel_id=1, source_target_pairs={{0,16},{16,32},{32,48},{48,0},{1,17},{17,33},{33,49},{49,1},{2,18}... | collective-permute-start | bytes 786440 | tf_op jit(solution)/shard_map/ppermute | solution.py:204
  98.0 11.5 %collective-permute-start.4 = (bf16[256,512]{1,0:T(8,128)(2,1)S(1)}, bf16[256,512]{1,0:T(8,128)(2,1)S(1)}, u32[]{:S(2)}, u32[]{:S(2)}) collective-permute-start(bf16[256,512]{1,0:T(8,128)(2,1)S(1)} %slice.25), channel_id=1, source_target_pairs={{0,48},{16,0},{32,16},{48,32},{1,49},{17,1},{33,17},{49,33},{2,50}... | collective-permute-start | bytes 786440 | tf_op jit(solution)/shard_map/ppermute | solution.py:205
  105.3 4.3 %copy-start = (bf16[2,64,512]{2,1,0:T(8,128)(2,1)S(1)}, bf16[2,64,512]{2,1,0:T(8,128)(2,1)}, u32[]{:S(2)}) copy-start(bf16[2,64,512]{2,1,0:T(8,128)(2,1)} %refs_5_.1) | copy-start | bytes 393220
  109.5 13.8 %copy-start.2 = (f32[2,128]{1,0:T(2,128)S(1)}, f32[2,128]{1,0:T(2,128)}, u32[]{:S(2)}) copy-start(f32[2,128]{1,0:T(2,128)} %get-tuple-element.10) | copy-start | bytes 3076
  112.6 24.9 %all-to-all-start.2 = ((f32[16,2,128]{2,1,0:T(2,128)}), f32[16,2,128]{2,1,0:T(2,128)S(1)}, u32[]{:S(2)}, u32[]{:S(2)}) async-start(f32[16,2,128]{2,1,0:T(2,128)} %ladder.5), calls=%async_computation.2 | async-start | bytes 32768 | tf_op jit(solution)/shard_map/all_to_all | solution.py:187

commit v5 on v4

--- a/solution.py
+++ b/solution.py
@@ -95,6 +95,15 @@
     return folded
 
 
+def slab_blocks(slab_refs):
+    for ref in slab_refs:
+        if len(ref.shape) == 2:
+            yield ref[...]
+            continue
+        for step in range(1, ref.shape[0]):
+            yield ref[lax.rem(lax.axis_index("x") + step, ref.shape[0])]
+
+
 def ladder_kernel(slab_count, has_earlier, pays, *refs):
     slab_refs, refs = refs[:slab_count], refs[slab_count:]
     tau_refs, refs = refs[:2], refs[2:]
@@ -109,8 +118,7 @@
         for pair in range(pairs):
             tau = tau_ref[:, :, pair].reshape(virt, virt)
             gram = None
-            for slab_ref in slab_refs:
-                slabs = slab_ref[...]
+            for slabs in slab_blocks(slab_refs):
                 half = jnp.dot(slabs, tau, preferred_element_type=jnp.float32).astype(jnp.bfloat16)
                 for at in range(0, slabs.shape[0], GROUP):
                     block = lax.dot_general(
@@ -138,7 +146,7 @@
 
 def ladder(slabs, taus, earlier=None, doubles=None):
     pairs, virt = taus[0].shape[2], taus[0].shape[4]
-    rows = sum(slab.shape[0] for slab in slabs)
+    rows = sum(slab.size // virt for slab in slabs)
     has_earlier, pays = earlier is not None, doubles is not None
     specs, operands = [VMEM] * (len(slabs) + 2), [*slabs, *taus]
     out = (2 * pairs, NWIN, 128)
@@ -167,20 +175,36 @@
 
 def join_kernel(own_ref, other_ref, out_ref):
     zh = lax.axis_index("zh")
-    for copy in range(out_ref.shape[0]):
-        out_ref[copy, zh] = own_ref[...]
-        out_ref[copy, 1 - zh] = other_ref[...]
+    out_ref[zh] = own_ref[...]
+    out_ref[1 - zh] = other_ref[...]
 
 
 def join(own, other):
     return pl.pallas_call(
         join_kernel,
-        out_shape=jax.ShapeDtypeStruct((4, 2) + own.shape, own.dtype),
+        out_shape=jax.ShapeDtypeStruct((2,) + own.shape, own.dtype),
         in_specs=[VMEM, VMEM],
         out_specs=VMEM,
-        compiler_params=pltpu.CompilerParams(vmem_limit_bytes=6 << 20),
+        compiler_params=pltpu.CompilerParams(vmem_limit_bytes=4 << 20),
         name="join",
     )(own, other)
+
+
+def assemble_kernel(own_ref, above_ref, far_ref, below_ref, out_ref):
+    y = lax.axis_index("y")
+    for step, ref in enumerate((own_ref, above_ref, far_ref, below_ref)):
+        out_ref[lax.rem(y + step, 4)] = ref[...]
+
+
+def assemble(own, above, far, below):
+    return pl.pallas_call(
+        assemble_kernel,
+        out_shape=jax.ShapeDtypeStruct((4,) + own.shape, own.dtype),
+        in_specs=[VMEM] * 4,
+        out_specs=VMEM,
+        compiler_params=pltpu.CompilerParams(vmem_limit_bytes=6 << 20),
+        name="assemble",
+    )(own, above, far, below)
 
 
 def exchange(copies, axis):
@@ -195,22 +219,20 @@
     dressed = exchange(copies, "zm").reshape(-1, virt)
     other = lax.ppermute(own, "zh", SWAP)
     dressed_next = lax.ppermute(dressed, "zb", SWAP)
-    copies = join(own, other)
-    tau = exchange(copies, "y")
+    tau = join(own, other)
+    below = lax.ppermute(tau, "y", UP)
+    above = lax.ppermute(tau, "y", DOWN)
+    far = lax.ppermute(below, "y", UP)
     mine = jnp.concatenate([dressed, dressed_next])
-    below = lax.ppermute(mine, "x", UP)
-    above = lax.ppermute(mine, "x", DOWN)
+    slabs = exchange(jnp.broadcast_to(mine[None], (4,) + mine.shape), "x")
+    tau = assemble(tau, above, far, below)
     tau_other = lax.ppermute(tau, "k", SWAP)
-    far_up = lax.ppermute(below[: dressed.shape[0]], "x", UP)
-    far_down = lax.ppermute(above[dressed.shape[0] :], "x", DOWN)
-    denominator = lax.optimization_barrier(denominator[:, :NWIN] + denominator[:, 64 : 64 + NWIN])
     taus = (tau, tau_other)
     parts = ladder((mine,), taus)
-    parts = ladder((below, above), taus, parts)
-    parts = ladder((far_up, far_down), taus, parts, doubles)
+    parts = ladder((slabs,), taus, parts, doubles)
     parts = exchange(parts, ("k",) + AUX)
     total = jnp.sum(parts, axis=0)
-    residual = total[:, :NWIN] / denominator
+    residual = total[:, :NWIN] / denominator[:, :NWIN]
     return (total[:, NWIN : 2 * NWIN] + residual)[:, None, :]
 
 

time: 139 us -> 130 us (0.935)
  blocking collectives: 17.9 us -> 54.3 us
  starting transfers between devices: 62.5 us -> 35 us
  waiting for transfers between devices: 42.8 us -> 20.3 us
  local copies, waits for them, and re-layouts: 0.95 us -> 6.83 us
  Pallas kernels: 13.2 us -> 11.8 us
    all_to_all x1 -> x2, blocking collectives: 17.9 us -> 54.3 us  [exchange(): return lax.all_to_all(copies, axis, split_axis=0, concat_axis=0, tiled=True)]
    all_to_all x2 -> x1, waiting for transfers between devices: 24.4 us -> 0.01 us  [exchange(): return lax.all_to_all(copies, axis, split_axis=0, concat_axis=0, tiled=True)]
    all_to_all x2 -> x1, starting transfers between devices: 27.3 us -> 4.01 us  [exchange(): return lax.all_to_all(copies, axis, split_axis=0, concat_axis=0, tiled=True)]
    ppermute x1, waiting for transfers between devices: 2.85 us -> 11.3 us  [body(): other = lax.ppermute(own, 'zh', SWAP)]
    ppermute x1, starting transfers between devices: 16.2 us -> 8.6 us  [body(): other = lax.ppermute(own, 'zh', SWAP)]
    ppermute x1, waiting for transfers between devices: 7.04 us -> 0.01 us  [body(): dressed_next = lax.ppermute(dressed, 'zb', SWAP)]
    ppermute x1, starting transfers between devices: 4.01 us -> 8.92 us  [body(): tau_other = lax.ppermute(tau, 'k', SWAP)]
    ppermute x4 -> x3, starting transfers between devices: 13 us -> 8.48 us  [the longest x1 3.34 us: body(): above = lax.ppermute(tau, 'y', DOWN)]
  transfers between devices with their start and end apart: 9 -> 7, of which waited for: 5 -> 4; matrix products, arithmetic and copies ran while one was open for 0% -> 1% of each run, Pallas kernels for 5% -> 2%
where the time goes in v5:
time: 130 us; the launch traced here: 129 us
  blocking collectives  54.3 us (42%)
  starting transfers between devices  35 us (27%)
  waiting for transfers between devices  20.3 us (16%)
  Pallas kernels  11.8 us (9%)
  local copies, waits for them, and re-layouts  6.83 us (5%)
    all_to_all x2, blocking collectives, exchange(): return lax.all_to_all(copies, axis, split_axis=0, concat_axis=0, tiled=True)  54.3 us
    ppermute x1, waiting for transfers between devices, body(): other = lax.ppermute(own, 'zh', SWAP)  11.3 us
    ppermute x1, starting transfers between devices, body(): tau_other = lax.ppermute(tau, 'k', SWAP)  8.92 us
    ppermute x1, starting transfers between devices, body(): other = lax.ppermute(own, 'zh', SWAP)  8.6 us
    pallas_call x2, Pallas kernels, ladder(): pl.pallas_call(functools.partial(ladder_kernel, len(slabs), has_earlier,...  8.53 us
    unnamed x14, local copies, waits for them, and re-layouts  5.34 us
    ppermute x1, starting transfers between devices, body(): dressed_next = lax.ppermute(dressed, 'zb', SWAP)  5.01 us
    ppermute x1, waiting for transfers between devices, body(): far = lax.ppermute(below, 'y', UP)  4.88 us
  transfers between devices with their start and end apart: 7, of which 4 were waited for; matrix products, arithmetic and copies ran while one was open for 1% of the time, Pallas kernels for 2%

profile of v5, /device:TPU:1, one launch (start us, length us, event | category | flops | bytes accessed | tf_op | source)
XLA Modules:
  0.0 129.0 jit_solution(17172122946158757119)
XLA Ops:
  0.0 3.1 %start.1 = (bf16[4,64,512]{2,1,0:T(8,128)(2,1)}, bf16[2,64,512]{2,1,0:T(8,128)(2,1)}, f32[2,128]{1,0:T(2,128)}) custom-call(s32[2,2]{1,0:T(2,128)} %pairs_ref.1, f32[256]{0:T(256)} %occ_energy_ref.1, f32[8]{0:T(128)} %vir_energy_ref.1, bf16[2,64,512]{2,1,0:T(8,128)(2,1)} %refs_4_.1, bf16[256,512]{1,0:T(8,128)(2,1)} %singles_ref.1, ...), custom_call_target="tpu_custom_call" | custom-call | flops 16777216 | bytes 3145728 | tf_op jit(solution)/shard_map/start/pallas_call | solution.py:70
  3.1 26.0 %all_to_all.15 = bf16[4,64,512]{2,1,0:T(8,128)(2,1)S(1)} all-to-all(bf16[4,64,512]{2,1,0:T(8,128)(2,1)} %get-tuple-element.8), channel_id=1, replica_groups=mesh['zm'=4,'zb'=2,'x'=4,'k'=2,'y'=4,'zh'=2] {'zm'}, dimensions={0} | all-to-all | bytes 524288 | tf_op jit(solution)/shard_map/all_to_all | solution.py:211
  29.2 5.0 %collective-permute-start = (bf16[256,512]{1,0:T(8,128)(2,1)S(1)}, bf16[256,512]{1,0:T(8,128)(2,1)S(1)}, u32[]{:S(2)}, u32[]{:S(2)}) collective-permute-start(bf16[256,512]{1,0:T(8,128)(2,1)S(1)} %bitcast.4), channel_id=1, source_target_pairs={{0,64},{64,0},{1,65},{65,1},{2,66},{66,2},{3,67},{67,3},{4,68},{68... | collective-permute-start | bytes 786440 | tf_op jit(solution)/shard_map/ppermute | solution.py:221
  34.2 8.6 %collective-permute-start.1 = (bf16[2,64,512]{2,1,0:T(8,128)(2,1)}, bf16[2,64,512]{2,1,0:T(8,128)(2,1)S(1)}, u32[]{:S(2)}, u32[]{:S(2)}) collective-permute-start(bf16[2,64,512]{2,1,0:T(8,128)(2,1)} %get-tuple-element.9.own_ref), channel_id=1, source_target_pairs={{0,1},{1,0},{2,3},{3,2},{4,5},{5,4},{6,7},{7,6},{8,9},{9,8},{10,11... | collective-permute-start | bytes 393224 | tf_op jit(solution)/shard_map/ppermute | solution.py:220
  42.8 11.3 %collective-permute-done.1.other_ref = bf16[2,64,512]{2,1,0:T(8,128)(2,1)S(1)} collective-permute-done((bf16[2,64,512]{2,1,0:T(8,128)(2,1)}, bf16[2,64,512]{2,1,0:T(8,128)(2,1)S(1)}, u32[]{:S(2)}, u32[]{:S(2)}) %collective-permute-start.1) | collective-permute-done | bytes 131104 | tf_op jit(solution)/shard_map/ppermute | solution.py:220
  54.1 0.9 copy-done.3
  55.0 3.2 %collective-permute-start.3 = (bf16[2,2,64,512]{3,2,1,0:T(8,128)(2,1)S(1)}, bf16[2,2,64,512]{3,2,1,0:T(8,128)(2,1)S(1)}, u32[]{:S(2)}, u32[]{:S(2)}) collective-permute-start(bf16[2,2,64,512]{3,2,1,0:T(8,128)(2,1)S(1)} %join.1.own_ref), channel_id=1, source_target_pairs={{0,2},{2,4},{4,6},{6,0},{1,3},{3,5},{5,7},{7,1},{8,10},{10,12},{12... | collective-permute-start | bytes 786440 | tf_op jit(solution)/shard_map/ppermute | solution.py:223
  58.3 1.5 %broadcast_in_dim.4 = bf16[4,512,512]{2,1,0:T(8,128)(2,1)} broadcast(bf16[512,512]{1,0:T(8,128)(2,1)S(1)} %pad_maximum_fusion.refs_0_), dimensions={1,2} | broadcast | bytes 2621440 | tf_op jit(solution)/shard_map/broadcast_in_dim | solution.py:227
  59.8 4.0 %all-to-all-start.1 = ((bf16[4,512,512]{2,1,0:T(8,128)(2,1)}), bf16[4,512,512]{2,1,0:T(8,128)(2,1)S(1)}, u32[]{:S(2)}, u32[]{:S(2)}) async-start(bf16[4,512,512]{2,1,0:T(8,128)(2,1)} %broadcast_in_dim.4), calls=%async_computation.1 | async-start | bytes 4194304 | tf_op jit(solution)/shard_map/all_to_all | solution.py:211
  63.8 3.3 %collective-permute-start.2 = (bf16[2,2,64,512]{3,2,1,0:T(8,128)(2,1)S(1)}, bf16[2,2,64,512]{3,2,1,0:T(8,128)(2,1)S(1)}, u32[]{:S(2)}, u32[]{:S(2)}) collective-permute-start(bf16[2,2,64,512]{3,2,1,0:T(8,128)(2,1)S(1)} %join.1.own_ref), channel_id=1, source_target_pairs={{0,6},{2,0},{4,2},{6,4},{1,7},{3,1},{5,3},{7,5},{8,14},{10,8},{12,... | collective-permute-start | bytes 786440 | tf_op jit(solution)/shard_map/ppermute | solution.py:224
  67.2 1.9 %collective-permute-start.4 = (bf16[2,2,64,512]{3,2,1,0:T(8,128)(2,1)S(1)}, bf16[2,2,64,512]{3,2,1,0:T(8,128)(2,1)S(1)}, u32[]{:S(2)}, u32[]{:S(2)}) collective-permute-start(bf16[2,2,64,512]{3,2,1,0:T(8,128)(2,1)S(1)} %collective-permute-done.3.below_ref), channel_id=1, source_target_pairs={{0,2},{2,4},{4,6},{6,0},{1,3},{3,5},{5,7},{7,1},{8,10},{10,12},{12... | collective-permute-start | bytes 786440 | tf_op jit(solution)/shard_map/ppermute | solution.py:225
  69.1 1.8 %collective-permute-done.2.above_ref = bf16[2,2,64,512]{3,2,1,0:T(8,128)(2,1)S(1)} collective-permute-done((bf16[2,2,64,512]{3,2,1,0:T(8,128)(2,1)S(1)}, bf16[2,2,64,512]{3,2,1,0:T(8,128)(2,1)S(1)}, u32[]{:S(2)}, u32[]{:S(2)}) %collective-permute-start.2) | collective-permute-done | bytes 262176 | tf_op jit(solution)/shard_map/ppermute | solution.py:224
  70.9 4.9 %collective-permute-done.4.far_ref = bf16[2,2,64,512]{3,2,1,0:T(8,128)(2,1)S(1)} collective-permute-done((bf16[2,2,64,512]{3,2,1,0:T(8,128)(2,1)S(1)}, bf16[2,2,64,512]{3,2,1,0:T(8,128)(2,1)S(1)}, u32[]{:S(2)}, u32[]{:S(2)}) %collective-permute-start.4) | collective-permute-done | bytes 262176 | tf_op jit(solution)/shard_map/ppermute | solution.py:225
  75.8 0.1 assemble.1.refs_1_
  75.9 8.9 %collective-permute-start.5 = (bf16[4,2,2,64,512]{4,3,2,1,0:T(8,128)(2,1)S(1)}, bf16[4,2,2,64,512]{4,3,2,1,0:T(8,128)(2,1)S(1)}, u32[]{:S(2)}, u32[]{:S(2)}) collective-permute-start(bf16[4,2,2,64,512]{4,3,2,1,0:T(8,128)(2,1)S(1)} %assemble.1.refs_1_), channel_id=1, source_target_pairs={{0,8},{8,0},{1,9},{9,1},{2,10},{10,2},{3,11},{11,3},{4,12},{12,4},... | collective-permute-start | bytes 3145736 | tf_op jit(solution)/shard_map/ppermute | solution.py:229
  84.8 2.3 %collective-permute-done.5.refs_2_ = bf16[4,2,2,64,512]{4,3,2,1,0:T(8,128)(2,1)S(1)} collective-permute-done((bf16[4,2,2,64,512]{4,3,2,1,0:T(8,128)(2,1)S(1)}, bf16[4,2,2,64,512]{4,3,2,1,0:T(8,128)(2,1)S(1)}, u32[]{:S(2)}, u32[]{:S(2)}) %collective-permute-start.5) | collective-permute-done | bytes 1048608 | tf_op jit(solution)/shard_map/ppermute | solution.py:229
  87.1 2.6 %ladder.2.refs_3_ = f32[4,8,128]{2,1,0:T(8,128)S(1)} custom-call(bf16[512,512]{1,0:T(8,128)(2,1)S(1)} %pad_maximum_fusion.refs_0_, bf16[4,2,2,64,512]{4,3,2,1,0:T(8,128)(2,1)S(1)} %assemble.1.refs_1_, bf16[4,2,2,64,512]{4,3,2,1,0:T(8,128)(2,1)S(1)} %collective-permute-done.5.refs_2_), custom_call_target="tpu_custom_call" | custom-call | flops 1610612736 | bytes 2621440 | tf_op jit(solution)/shard_map/ladder/pallas_call | solution.py:160
  89.7 1.0 copy-done
  90.7 1.0 copy-done.4
  91.7 1.2 copy-done.1
  92.9 1.2 copy-done.5
  94.2 5.9 %ladder.3 = f32[16,2,128]{2,1,0:T(2,128)S(1)} custom-call(bf16[4,512,512]{2,1,0:T(8,128)(2,1)S(1)} %all-to-all-done.1.refs_0_, bf16[4,2,2,64,512]{4,3,2,1,0:T(8,128)(2,1)S(1)} %copy-done.1, bf16[4,2,2,64,512]{4,3,2,1,0:T(8,128)(2,1)S(1)} %copy-done.5, f32[4,8,128]{2,1,0:T(8,128)S(1)} %ladder.2.refs_3_, bf16[2,64,512]{2,1,0:T(8,128)(2,1)S(1)} %copy-done.2), custom_call_target="tpu_custom_call" | custom-call | flops 6442450944 | bytes 4194304 | tf_op jit(solution)/shard_map/ladder/pallas_call | solution.py:160
  100.0 28.3 %all_to_all.16 = f32[16,2,128]{2,1,0:T(2,128)S(1)} all-to-all(f32[16,2,128]{2,1,0:T(2,128)S(1)} %ladder.3), channel_id=1, replica_groups=mesh['zm'=4,'zb'=2,'x'=4,'k'=2,'y'=4,'zh'=2] {'k','y','zh'}, dimensions={0} | all-to-all | bytes 32768 | tf_op jit(solution)/shard_map/all_to_all | solution.py:211
  128.3 0.6 divide_add_fusion
  (15 shorter events, 0.1 us)
Async XLA Ops:
  29.2 29.1 %collective-permute-start = (bf16[256,512]{1,0:T(8,128)(2,1)S(1)}, bf16[256,512]{1,0:T(8,128)(2,1)S(1)}, u32[]{:S(2)}, u32[]{:S(2)}) collective-permute-start(bf16[256,512]{1,0:T(8,128)(2,1)S(1)} %bitcast.4), channel_id=1, source_target_pairs={{0,64},{64,0},{1,65},{65,1},{2,66},{66,2},{3,67},{67,3},{4,68},{68... | collective-permute-start | bytes 786440 | tf_op jit(solution)/shard_map/ppermute | solution.py:221
  34.2 19.9 %collective-permute-start.1 = (bf16[2,64,512]{2,1,0:T(8,128)(2,1)}, bf16[2,64,512]{2,1,0:T(8,128)(2,1)S(1)}, u32[]{:S(2)}, u32[]{:S(2)}) collective-permute-start(bf16[2,64,512]{2,1,0:T(8,128)(2,1)} %get-tuple-element.9.own_ref), channel_id=1, source_target_pairs={{0,1},{1,0},{2,3},{3,2},{4,5},{5,4},{6,7},{7,6},{8,9},{9,8},{10,11... | collective-permute-start | bytes 393224 | tf_op jit(solution)/shard_map/ppermute | solution.py:220
  54.1 0.9 copy-start.3
  55.0 12.1 %collective-permute-start.3 = (bf16[2,2,64,512]{3,2,1,0:T(8,128)(2,1)S(1)}, bf16[2,2,64,512]{3,2,1,0:T(8,128)(2,1)S(1)}, u32[]{:S(2)}, u32[]{:S(2)}) collective-permute-start(bf16[2,2,64,512]{3,2,1,0:T(8,128)(2,1)S(1)} %join.1.own_ref), channel_id=1, source_target_pairs={{0,2},{2,4},{4,6},{6,0},{1,3},{3,5},{5,7},{7,1},{8,10},{10,12},{12... | collective-permute-start | bytes 786440 | tf_op jit(solution)/shard_map/ppermute | solution.py:223
  59.8 31.9 %all-to-all-start.1 = ((bf16[4,512,512]{2,1,0:T(8,128)(2,1)}), bf16[4,512,512]{2,1,0:T(8,128)(2,1)S(1)}, u32[]{:S(2)}, u32[]{:S(2)}) async-start(bf16[4,512,512]{2,1,0:T(8,128)(2,1)} %broadcast_in_dim.4), calls=%async_computation.1 | async-start | bytes 4194304 | tf_op jit(solution)/shard_map/all_to_all | solution.py:211
  63.8 7.1 %collective-permute-start.2 = (bf16[2,2,64,512]{3,2,1,0:T(8,128)(2,1)S(1)}, bf16[2,2,64,512]{3,2,1,0:T(8,128)(2,1)S(1)}, u32[]{:S(2)}, u32[]{:S(2)}) collective-permute-start(bf16[2,2,64,512]{3,2,1,0:T(8,128)(2,1)S(1)} %join.1.own_ref), channel_id=1, source_target_pairs={{0,6},{2,0},{4,2},{6,4},{1,7},{3,1},{5,3},{7,5},{8,14},{10,8},{12,... | collective-permute-start | bytes 786440 | tf_op jit(solution)/shard_map/ppermute | solution.py:224
  67.2 8.6 %collective-permute-start.4 = (bf16[2,2,64,512]{3,2,1,0:T(8,128)(2,1)S(1)}, bf16[2,2,64,512]{3,2,1,0:T(8,128)(2,1)S(1)}, u32[]{:S(2)}, u32[]{:S(2)}) collective-permute-start(bf16[2,2,64,512]{3,2,1,0:T(8,128)(2,1)S(1)} %collective-permute-done.3.below_ref), channel_id=1, source_target_pairs={{0,2},{2,4},{4,6},{6,0},{1,3},{3,5},{5,7},{7,1},{8,10},{10,12},{12... | collective-permute-start | bytes 786440 | tf_op jit(solution)/shard_map/ppermute | solution.py:225
  75.9 15.8 %copy-start.2 = (bf16[2,64,512]{2,1,0:T(8,128)(2,1)S(1)}, bf16[2,64,512]{2,1,0:T(8,128)(2,1)}, u32[]{:S(2)}) copy-start(bf16[2,64,512]{2,1,0:T(8,128)(2,1)} %refs_4_.1) | copy-start | bytes 393220
  75.9 11.2 %collective-permute-start.5 = (bf16[4,2,2,64,512]{4,3,2,1,0:T(8,128)(2,1)S(1)}, bf16[4,2,2,64,512]{4,3,2,1,0:T(8,128)(2,1)S(1)}, u32[]{:S(2)}, u32[]{:S(2)}) collective-permute-start(bf16[4,2,2,64,512]{4,3,2,1,0:T(8,128)(2,1)S(1)} %assemble.1.refs_1_), channel_id=1, source_target_pairs={{0,8},{8,0},{1,9},{9,1},{2,10},{10,2},{3,11},{11,3},{4,12},{12,4},... | collective-permute-start | bytes 3145736 | tf_op jit(solution)/shard_map/ppermute | solution.py:229
  89.7 1.0 copy-start
  90.7 1.0 copy-start.4
  91.7 1.2 copy-start.1
  92.9 1.2 copy-start.5
  94.1 34.2 %copy-start.6 = (f32[2,128]{1,0:T(2,128)S(1)}, f32[2,128]{1,0:T(2,128)}, u32[]{:S(2)}) copy-start(f32[2,128]{1,0:T(2,128)} %get-tuple-element.10) | copy-start | bytes 3076

commit v6 on v5

--- a/solution.py
+++ b/solution.py
@@ -15,6 +15,7 @@
 SWAP = [(0, 1), (1, 0)]
 UP = [(i, (i + 1) % 4) for i in range(4)]
 DOWN = [(i, (i + 3) % 4) for i in range(4)]
+FAR = [(i, (i + 2) % 4) for i in range(4)]
 SMEM = pl.BlockSpec(memory_space=pltpu.SMEM)
 VMEM = pl.BlockSpec(memory_space=pltpu.VMEM)
 
@@ -100,8 +101,8 @@
         if len(ref.shape) == 2:
             yield ref[...]
             continue
-        for step in range(1, ref.shape[0]):
-            yield ref[lax.rem(lax.axis_index("x") + step, ref.shape[0])]
+        for chip in range(ref.shape[0]):
+            yield ref[chip]
 
 
 def ladder_kernel(slab_count, has_earlier, pays, *refs):
@@ -223,13 +224,16 @@
     below = lax.ppermute(tau, "y", UP)
     above = lax.ppermute(tau, "y", DOWN)
     far = lax.ppermute(below, "y", UP)
-    mine = jnp.concatenate([dressed, dressed_next])
-    slabs = exchange(jnp.broadcast_to(mine[None], (4,) + mine.shape), "x")
+    slabs = exchange(jnp.broadcast_to(dressed[None], (4,) + dressed.shape), "x")
+    next_far = lax.ppermute(dressed_next, "x", FAR)
+    next_below = lax.ppermute(dressed_next, "x", UP)
     tau = assemble(tau, above, far, below)
     tau_other = lax.ppermute(tau, "k", SWAP)
+    next_above = lax.ppermute(dressed_next, "x", DOWN)
     taus = (tau, tau_other)
-    parts = ladder((mine,), taus)
-    parts = ladder((slabs,), taus, parts, doubles)
+    parts = ladder((slabs,), taus)
+    parts = ladder((dressed_next, next_below), taus, parts)
+    parts = ladder((next_far, next_above), taus, parts, doubles)
     parts = exchange(parts, ("k",) + AUX)
     total = jnp.sum(parts, axis=0)
     residual = total[:, :NWIN] / denominator[:, :NWIN]

time: 130 us -> 120 us (0.923)
  blocking collectives: 54.3 us -> 27.7 us
  starting transfers between devices: 35 us -> 60.1 us
  waiting for transfers between devices: 20.3 us -> 14.4 us
  local copies, waits for them, and re-layouts: 6.83 us -> 1.98 us
  Pallas kernels: 11.8 us -> 14.3 us
    all_to_all x2 -> x1, blocking collectives: 54.3 us -> 27.7 us  [exchange(): return lax.all_to_all(copies, axis, split_axis=0, concat_axis=0, tiled=True)]
    ppermute x1, waiting for transfers between devices: 11.3 us -> 0.01 us  [body(): other = lax.ppermute(own, 'zh', SWAP)]
    ppermute x0 -> x3, starting transfers between devices: none -> 9.87 us  [the longest x1 3.4 us: body(): next_above = lax.ppermute(dressed_next, 'x', DOWN)]
    ppermute x1, starting transfers between devices: 8.6 us -> 16.2 us  [body(): other = lax.ppermute(own, 'zh', SWAP)]
    ppermute x1, waiting for transfers between devices: 0.01 us -> 6.58 us  [body(): dressed_next = lax.ppermute(dressed, 'zb', SWAP)]
    ppermute x1, starting transfers between devices: 5.01 us -> 9.93 us  [body(): dressed_next = lax.ppermute(dressed, 'zb', SWAP)]
    all_to_all x1 -> x2, starting transfers between devices: 4.01 us -> 8.63 us  [exchange(): return lax.all_to_all(copies, axis, split_axis=0, concat_axis=0, tiled=True)]
    unnamed x14 -> x8, local copies, waits for them, and re-layouts: 5.34 us -> 0.92 us
  transfers between devices with their start and end apart: 7 -> 11, of which waited for: 4 -> 3; matrix products, arithmetic and copies ran while one was open for 1% -> 1% of each run, Pallas kernels for 2% -> 6%
where the time goes in v6:
time: 120 us; the launch traced here: 119 us
  starting transfers between devices  60.1 us (50%)
  blocking collectives  27.7 us (23%)
  waiting for transfers between devices  14.4 us (12%)
  Pallas kernels  14.3 us (12%)
  local copies, waits for them, and re-layouts  1.98 us (2%)
    all_to_all x1, blocking collectives, exchange(): return lax.all_to_all(copies, axis, split_axis=0, concat_axis=0, tiled=True)  27.7 us
    ppermute x1, starting transfers between devices, body(): other = lax.ppermute(own, 'zh', SWAP)  16.2 us
    pallas_call x3, Pallas kernels, ladder(): pl.pallas_call(functools.partial(ladder_kernel, len(slabs), has_earlier,...  11.1 us
    ppermute x1, starting transfers between devices, body(): dressed_next = lax.ppermute(dressed, 'zb', SWAP)  9.93 us
    all_to_all x2, starting transfers between devices, exchange(): return lax.all_to_all(copies, axis, split_axis=0, concat_axis=0, tiled=True)  8.63 us
    ppermute x1, waiting for transfers between devices, body(): dressed_next = lax.ppermute(dressed, 'zb', SWAP)  6.58 us
    ppermute x1, starting transfers between devices, body(): tau_other = lax.ppermute(tau, 'k', SWAP)  5.91 us
    ppermute x1, waiting for transfers between devices, body(): far = lax.ppermute(below, 'y', UP)  5.62 us
  transfers between devices with their start and end apart: 11, of which 3 were waited for; matrix products, arithmetic and copies ran while one was open for 1% of the time, Pallas kernels for 6%

profile of v6, /device:TPU:1, one launch (start us, length us, event | category | flops | bytes accessed | tf_op | source)
XLA Modules:
  0.0 119.3 jit_solution(10878036950385192540)
XLA Ops:
  0.0 3.1 %start.1 = (bf16[4,64,512]{2,1,0:T(8,128)(2,1)}, bf16[2,64,512]{2,1,0:T(8,128)(2,1)}, f32[2,128]{1,0:T(2,128)}) custom-call(s32[2,2]{1,0:T(2,128)} %pairs_ref.1, f32[256]{0:T(256)} %occ_energy_ref.1, f32[8]{0:T(128)} %vir_energy_ref.1, bf16[2,64,512]{2,1,0:T(8,128)(2,1)} %refs_5_.1, bf16[256,512]{1,0:T(8,128)(2,1)} %singles_ref.1, ...), custom_call_target="tpu_custom_call" | custom-call | flops 16777216 | bytes 3145728 | tf_op jit(solution)/shard_map/start/pallas_call | solution.py:71
  3.1 16.2 %collective-permute-start.3 = (bf16[2,64,512]{2,1,0:T(8,128)(2,1)}, bf16[2,64,512]{2,1,0:T(8,128)(2,1)S(1)}, u32[]{:S(2)}, u32[]{:S(2)}) collective-permute-start(bf16[2,64,512]{2,1,0:T(8,128)(2,1)} %get-tuple-element.9.own_ref), channel_id=1, source_target_pairs={{0,1},{1,0},{2,3},{3,2},{4,5},{5,4},{6,7},{7,6},{8,9},{9,8},{10,11... | collective-permute-start | bytes 393224 | tf_op jit(solution)/shard_map/ppermute | solution.py:221
  19.4 4.3 %all-to-all-start = ((bf16[4,64,512]{2,1,0:T(8,128)(2,1)}), bf16[4,64,512]{2,1,0:T(8,128)(2,1)S(1)}, u32[]{:S(2)}, u32[]{:S(2)}) async-start(bf16[4,64,512]{2,1,0:T(8,128)(2,1)} %get-tuple-element.8), calls=%async_computation | async-start | bytes 524288 | tf_op jit(solution)/shard_map/all_to_all | solution.py:212
  23.7 0.9 copy-done.1
  24.6 3.2 %collective-permute-start.5 = (bf16[2,2,64,512]{3,2,1,0:T(8,128)(2,1)S(1)}, bf16[2,2,64,512]{3,2,1,0:T(8,128)(2,1)S(1)}, u32[]{:S(2)}, u32[]{:S(2)}) collective-permute-start(bf16[2,2,64,512]{3,2,1,0:T(8,128)(2,1)S(1)} %join.1.own_ref), channel_id=1, source_target_pairs={{0,2},{2,4},{4,6},{6,0},{1,3},{3,5},{5,7},{7,1},{8,10},{10,12},{12... | collective-permute-start | bytes 786440 | tf_op jit(solution)/shard_map/ppermute | solution.py:224
  27.8 3.4 %collective-permute-start.4 = (bf16[2,2,64,512]{3,2,1,0:T(8,128)(2,1)S(1)}, bf16[2,2,64,512]{3,2,1,0:T(8,128)(2,1)S(1)}, u32[]{:S(2)}, u32[]{:S(2)}) collective-permute-start(bf16[2,2,64,512]{3,2,1,0:T(8,128)(2,1)S(1)} %join.1.own_ref), channel_id=1, source_target_pairs={{0,6},{2,0},{4,2},{6,4},{1,7},{3,1},{5,3},{7,5},{8,14},{10,8},{12,... | collective-permute-start | bytes 786440 | tf_op jit(solution)/shard_map/ppermute | solution.py:225
  31.2 2.2 %collective-permute-done.5.below_ref = bf16[2,2,64,512]{3,2,1,0:T(8,128)(2,1)S(1)} collective-permute-done((bf16[2,2,64,512]{3,2,1,0:T(8,128)(2,1)S(1)}, bf16[2,2,64,512]{3,2,1,0:T(8,128)(2,1)S(1)}, u32[]{:S(2)}, u32[]{:S(2)}) %collective-permute-start.5) | collective-permute-done | bytes 262176 | tf_op jit(solution)/shard_map/ppermute | solution.py:224
  33.4 3.0 %collective-permute-start.6 = (bf16[2,2,64,512]{3,2,1,0:T(8,128)(2,1)S(1)}, bf16[2,2,64,512]{3,2,1,0:T(8,128)(2,1)S(1)}, u32[]{:S(2)}, u32[]{:S(2)}) collective-permute-start(bf16[2,2,64,512]{3,2,1,0:T(8,128)(2,1)S(1)} %collective-permute-done.5.below_ref), channel_id=1, source_target_pairs={{0,2},{2,4},{4,6},{6,0},{1,3},{3,5},{5,7},{7,1},{8,10},{10,12},{12... | collective-permute-start | bytes 786440 | tf_op jit(solution)/shard_map/ppermute | solution.py:226
  36.4 5.6 %collective-permute-done.6.far_ref = bf16[2,2,64,512]{3,2,1,0:T(8,128)(2,1)S(1)} collective-permute-done((bf16[2,2,64,512]{3,2,1,0:T(8,128)(2,1)S(1)}, bf16[2,2,64,512]{3,2,1,0:T(8,128)(2,1)S(1)}, u32[]{:S(2)}, u32[]{:S(2)}) %collective-permute-start.6) | collective-permute-done | bytes 262176 | tf_op jit(solution)/shard_map/ppermute | solution.py:226
  42.0 0.1 assemble.1.refs_1_.refs_2_
  42.1 5.9 %collective-permute-start.7 = (bf16[4,2,2,64,512]{4,3,2,1,0:T(8,128)(2,1)S(1)}, bf16[4,2,2,64,512]{4,3,2,1,0:T(8,128)(2,1)S(1)}, u32[]{:S(2)}, u32[]{:S(2)}) collective-permute-start(bf16[4,2,2,64,512]{4,3,2,1,0:T(8,128)(2,1)S(1)} %assemble.1.refs_1_.refs_2_), channel_id=1, source_target_pairs={{0,8},{8,0},{1,9},{9,1},{2,10},{10,2},{3,11},{11,3},{4,12},{12,4},... | collective-permute-start | bytes 3145736 | tf_op jit(solution)/shard_map/ppermute | solution.py:231
  48.0 1.1 broadcast_in_dim.8
  49.1 4.3 %all-to-all-start.1 = ((bf16[4,256,512]{2,1,0:T(8,128)(2,1)}), bf16[4,256,512]{2,1,0:T(8,128)(2,1)S(1)}, u32[]{:S(2)}, u32[]{:S(2)}) async-start(bf16[4,256,512]{2,1,0:T(8,128)(2,1)} %broadcast_in_dim.8), calls=%async_computation.1 | async-start | bytes 2097152 | tf_op jit(solution)/shard_map/all_to_all | solution.py:212
  53.4 9.9 %collective-permute-start = (bf16[256,512]{1,0:T(8,128)(2,1)}, bf16[256,512]{1,0:T(8,128)(2,1)S(1)}, u32[]{:S(2)}, u32[]{:S(2)}) collective-permute-start(bf16[256,512]{1,0:T(8,128)(2,1)} %bitcast.5), channel_id=1, source_target_pairs={{0,64},{64,0},{1,65},{65,1},{2,66},{66,2},{3,67},{67,3},{4,68},{68... | collective-permute-start | bytes 786440 | tf_op jit(solution)/shard_map/ppermute | solution.py:222
  63.3 6.6 %collective-permute-done.refs_0_ = bf16[256,512]{1,0:T(8,128)(2,1)S(1)} collective-permute-done((bf16[256,512]{1,0:T(8,128)(2,1)}, bf16[256,512]{1,0:T(8,128)(2,1)S(1)}, u32[]{:S(2)}, u32[]{:S(2)}) %collective-permute-start) | collective-permute-done | bytes 262176 | tf_op jit(solution)/shard_map/ppermute | solution.py:222
  69.9 3.1 %collective-permute-start.8 = (bf16[256,512]{1,0:T(8,128)(2,1)S(1)}, bf16[256,512]{1,0:T(8,128)(2,1)}, u32[]{:S(2)}, u32[]{:S(2)}) collective-permute-start(bf16[256,512]{1,0:T(8,128)(2,1)S(1)} %collective-permute-done.refs_0_), channel_id=1, source_target_pairs={{0,16},{16,32},{32,48},{48,0},{1,17},{17,33},{33,49},{49,1},{2,18}... | collective-permute-start | bytes 786440 | tf_op jit(solution)/shard_map/ppermute | solution.py:229
  73.0 3.4 %collective-permute-start.2 = (bf16[256,512]{1,0:T(8,128)(2,1)S(1)}, bf16[256,512]{1,0:T(8,128)(2,1)}, u32[]{:S(2)}, u32[]{:S(2)}) collective-permute-start(bf16[256,512]{1,0:T(8,128)(2,1)S(1)} %collective-permute-done.refs_0_), channel_id=1, source_target_pairs={{0,48},{16,0},{32,16},{48,32},{1,49},{17,1},{33,17},{49,33},{2,50}... | collective-permute-start | bytes 786440 | tf_op jit(solution)/shard_map/ppermute | solution.py:232
  76.4 3.4 %collective-permute-start.1 = (bf16[256,512]{1,0:T(8,128)(2,1)S(1)}, bf16[256,512]{1,0:T(8,128)(2,1)}, u32[]{:S(2)}, u32[]{:S(2)}) collective-permute-start(bf16[256,512]{1,0:T(8,128)(2,1)S(1)} %collective-permute-done.refs_0_), channel_id=1, source_target_pairs={{0,32},{16,48},{32,0},{48,16},{1,33},{17,49},{33,1},{49,17},{2,34}... | collective-permute-start | bytes 786440 | tf_op jit(solution)/shard_map/ppermute | solution.py:228
  79.8 4.1 %ladder.3.refs_4_ = f32[4,8,128]{2,1,0:T(8,128)S(1)} custom-call(bf16[4,256,512]{2,1,0:T(8,128)(2,1)S(1)} %all-to-all-done.1.refs_0_, bf16[4,2,2,64,512]{4,3,2,1,0:T(8,128)(2,1)S(1)} %assemble.1.refs_1_.refs_2_, bf16[4,2,2,64,512]{4,3,2,1,0:T(8,128)(2,1)S(1)} %collective-permute-done.7.refs_2_.refs_3_), custom_call_target="tpu_custom_call" | custom-call | flops 3221225472 | bytes 3145728 | tf_op jit(solution)/shard_map/ladder/pallas_call | solution.py:161
  84.0 3.5 %ladder.4.refs_4_ = f32[4,8,128]{2,1,0:T(8,128)S(1)} custom-call(bf16[256,512]{1,0:T(8,128)(2,1)S(1)} %collective-permute-done.refs_0_, bf16[256,512]{1,0:T(8,128)(2,1)} %collective-permute-done.8.refs_1_, bf16[4,2,2,64,512]{4,3,2,1,0:T(8,128)(2,1)S(1)} %assemble.1.refs_1_.refs_2_, bf16[4,2,2,64,512]{4,3,2,1,0:T(8,128)(2,1)S(1)} %collective-permute-done.7.refs_2_.refs_3_, ...), custom_call_target="tpu_custom_call" | custom-call | flops 1610612736 | bytes 2621440 | tf_op jit(solution)/shard_map/ladder/pallas_call | solution.py:161
  87.4 0.0 collective-permute-done.1.refs_0_
  87.5 3.5 %ladder.5 = f32[16,2,128]{2,1,0:T(2,128)S(1)} custom-call(bf16[256,512]{1,0:T(8,128)(2,1)} %collective-permute-done.1.refs_0_, bf16[256,512]{1,0:T(8,128)(2,1)} %collective-permute-done.2.refs_1_, bf16[4,2,2,64,512]{4,3,2,1,0:T(8,128)(2,1)S(1)} %assemble.1.refs_1_.refs_2_, bf16[4,2,2,64,512]{4,3,2,1,0:T(8,128)(2,1)S(1)} %collective-permute-done.7.refs_2_.refs_3_, ...), custom_call_target="tpu_custom_call" | custom-call | flops 1610612736 | bytes 2621440 | tf_op jit(solution)/shard_map/ladder/pallas_call | solution.py:161
  91.0 27.7 %all_to_all.15 = f32[16,2,128]{2,1,0:T(2,128)S(1)} all-to-all(f32[16,2,128]{2,1,0:T(2,128)S(1)} %ladder.5), channel_id=1, replica_groups=mesh['zm'=4,'zb'=2,'x'=4,'k'=2,'y'=4,'zh'=2] {'k','y','zh'}, dimensions={0} | all-to-all | bytes 32768 | tf_op jit(solution)/shard_map/all_to_all | solution.py:212
  118.7 0.6 divide_add_fusion
  (16 shorter events, 0.1 us)
Async XLA Ops:
  3.1 20.5 %collective-permute-start.3 = (bf16[2,64,512]{2,1,0:T(8,128)(2,1)}, bf16[2,64,512]{2,1,0:T(8,128)(2,1)S(1)}, u32[]{:S(2)}, u32[]{:S(2)}) collective-permute-start(bf16[2,64,512]{2,1,0:T(8,128)(2,1)} %get-tuple-element.9.own_ref), channel_id=1, source_target_pairs={{0,1},{1,0},{2,3},{3,2},{4,5},{5,4},{6,7},{7,6},{8,9},{9,8},{10,11... | collective-permute-start | bytes 393224 | tf_op jit(solution)/shard_map/ppermute | solution.py:221
  19.4 28.6 %all-to-all-start = ((bf16[4,64,512]{2,1,0:T(8,128)(2,1)}), bf16[4,64,512]{2,1,0:T(8,128)(2,1)S(1)}, u32[]{:S(2)}, u32[]{:S(2)}) async-start(bf16[4,64,512]{2,1,0:T(8,128)(2,1)} %get-tuple-element.8), calls=%async_computation | async-start | bytes 524288 | tf_op jit(solution)/shard_map/all_to_all | solution.py:212
  23.7 0.9 copy-start.1
  24.6 8.7 %collective-permute-start.5 = (bf16[2,2,64,512]{3,2,1,0:T(8,128)(2,1)S(1)}, bf16[2,2,64,512]{3,2,1,0:T(8,128)(2,1)S(1)}, u32[]{:S(2)}, u32[]{:S(2)}) collective-permute-start(bf16[2,2,64,512]{3,2,1,0:T(8,128)(2,1)S(1)} %join.1.own_ref), channel_id=1, source_target_pairs={{0,2},{2,4},{4,6},{6,0},{1,3},{3,5},{5,7},{7,1},{8,10},{10,12},{12... | collective-permute-start | bytes 786440 | tf_op jit(solution)/shard_map/ppermute | solution.py:224
  27.8 8.5 %collective-permute-start.4 = (bf16[2,2,64,512]{3,2,1,0:T(8,128)(2,1)S(1)}, bf16[2,2,64,512]{3,2,1,0:T(8,128)(2,1)S(1)}, u32[]{:S(2)}, u32[]{:S(2)}) collective-permute-start(bf16[2,2,64,512]{3,2,1,0:T(8,128)(2,1)S(1)} %join.1.own_ref), channel_id=1, source_target_pairs={{0,6},{2,0},{4,2},{6,4},{1,7},{3,1},{5,3},{7,5},{8,14},{10,8},{12,... | collective-permute-start | bytes 786440 | tf_op jit(solution)/shard_map/ppermute | solution.py:225
  33.4 8.6 %collective-permute-start.6 = (bf16[2,2,64,512]{3,2,1,0:T(8,128)(2,1)S(1)}, bf16[2,2,64,512]{3,2,1,0:T(8,128)(2,1)S(1)}, u32[]{:S(2)}, u32[]{:S(2)}) collective-permute-start(bf16[2,2,64,512]{3,2,1,0:T(8,128)(2,1)S(1)} %collective-permute-done.5.below_ref), channel_id=1, source_target_pairs={{0,2},{2,4},{4,6},{6,0},{1,3},{3,5},{5,7},{7,1},{8,10},{10,12},{12... | collective-permute-start | bytes 786440 | tf_op jit(solution)/shard_map/ppermute | solution.py:226
  42.1 37.8 %collective-permute-start.7 = (bf16[4,2,2,64,512]{4,3,2,1,0:T(8,128)(2,1)S(1)}, bf16[4,2,2,64,512]{4,3,2,1,0:T(8,128)(2,1)S(1)}, u32[]{:S(2)}, u32[]{:S(2)}) collective-permute-start(bf16[4,2,2,64,512]{4,3,2,1,0:T(8,128)(2,1)S(1)} %assemble.1.refs_1_.refs_2_), channel_id=1, source_target_pairs={{0,8},{8,0},{1,9},{9,1},{2,10},{10,2},{3,11},{11,3},{4,12},{12,4},... | collective-permute-start | bytes 3145736 | tf_op jit(solution)/shard_map/ppermute | solution.py:231
  48.0 1.1 copy-start.2
  49.1 30.8 %all-to-all-start.1 = ((bf16[4,256,512]{2,1,0:T(8,128)(2,1)}), bf16[4,256,512]{2,1,0:T(8,128)(2,1)S(1)}, u32[]{:S(2)}, u32[]{:S(2)}) async-start(bf16[4,256,512]{2,1,0:T(8,128)(2,1)} %broadcast_in_dim.8), calls=%async_computation.1 | async-start | bytes 2097152 | tf_op jit(solution)/shard_map/all_to_all | solution.py:212
  53.4 16.5 %collective-permute-start = (bf16[256,512]{1,0:T(8,128)(2,1)}, bf16[256,512]{1,0:T(8,128)(2,1)S(1)}, u32[]{:S(2)}, u32[]{:S(2)}) collective-permute-start(bf16[256,512]{1,0:T(8,128)(2,1)} %bitcast.5), channel_id=1, source_target_pairs={{0,64},{64,0},{1,65},{65,1},{2,66},{66,2},{3,67},{67,3},{4,68},{68... | collective-permute-start | bytes 786440 | tf_op jit(solution)/shard_map/ppermute | solution.py:222
  69.9 14.0 %collective-permute-start.8 = (bf16[256,512]{1,0:T(8,128)(2,1)S(1)}, bf16[256,512]{1,0:T(8,128)(2,1)}, u32[]{:S(2)}, u32[]{:S(2)}) collective-permute-start(bf16[256,512]{1,0:T(8,128)(2,1)S(1)} %collective-permute-done.refs_0_), channel_id=1, source_target_pairs={{0,16},{16,32},{32,48},{48,0},{1,17},{17,33},{33,49},{49,1},{2,18}... | collective-permute-start | bytes 786440 | tf_op jit(solution)/shard_map/ppermute | solution.py:229
  73.0 14.4 %collective-permute-start.2 = (bf16[256,512]{1,0:T(8,128)(2,1)S(1)}, bf16[256,512]{1,0:T(8,128)(2,1)}, u32[]{:S(2)}, u32[]{:S(2)}) collective-permute-start(bf16[256,512]{1,0:T(8,128)(2,1)S(1)} %collective-permute-done.refs_0_), channel_id=1, source_target_pairs={{0,48},{16,0},{32,16},{48,32},{1,49},{17,1},{33,17},{49,33},{2,50}... | collective-permute-start | bytes 786440 | tf_op jit(solution)/shard_map/ppermute | solution.py:232
  76.4 11.0 %collective-permute-start.1 = (bf16[256,512]{1,0:T(8,128)(2,1)S(1)}, bf16[256,512]{1,0:T(8,128)(2,1)}, u32[]{:S(2)}, u32[]{:S(2)}) collective-permute-start(bf16[256,512]{1,0:T(8,128)(2,1)S(1)} %collective-permute-done.refs_0_), channel_id=1, source_target_pairs={{0,32},{16,48},{32,0},{48,16},{1,33},{17,49},{33,1},{49,17},{2,34}... | collective-permute-start | bytes 786440 | tf_op jit(solution)/shard_map/ppermute | solution.py:228
  84.0 3.5 %copy-start = (bf16[2,64,512]{2,1,0:T(8,128)(2,1)S(1)}, bf16[2,64,512]{2,1,0:T(8,128)(2,1)}, u32[]{:S(2)}) copy-start(bf16[2,64,512]{2,1,0:T(8,128)(2,1)} %refs_5_.1) | copy-start | bytes 393220
  87.4 31.3 %copy-start.3 = (f32[2,128]{1,0:T(2,128)S(1)}, f32[2,128]{1,0:T(2,128)}, u32[]{:S(2)}) copy-start(f32[2,128]{1,0:T(2,128)} %get-tuple-element.10) | copy-start | bytes 3076

commit v7 on v6

--- a/solution.py
+++ b/solution.py
@@ -96,40 +96,53 @@
     return folded
 
 
-def slab_blocks(slab_refs):
-    for ref in slab_refs:
-        if len(ref.shape) == 2:
-            yield ref[...]
-            continue
-        for chip in range(ref.shape[0]):
-            yield ref[chip]
-
-
-def ladder_kernel(slab_count, has_earlier, pays, *refs):
-    slab_refs, refs = refs[:slab_count], refs[slab_count:]
+def add_rows(slabs, tau_refs, gram_ref, opens):
+    for owner, tau_ref in enumerate(tau_refs):
+        pairs, virt = tau_ref.shape[2], tau_ref.shape[4]
+        for pair in range(pairs):
+            tau = tau_ref[:, :, pair].reshape(virt, virt)
+            half = jnp.dot(slabs, tau, preferred_element_type=jnp.float32).astype(jnp.bfloat16)
+            gram = None if opens else gram_ref[owner * pairs + pair]
+            for at in range(0, slabs.shape[0], GROUP):
+                block = lax.dot_general(
+                    half[at : at + GROUP],
+                    slabs[at : at + GROUP],
+                    (((1,), (1,)), ((), ())),
+                    preferred_element_type=jnp.float32,
+                )
+                gram = block if gram is None else gram + block
+            gram_ref[owner * pairs + pair] = gram
+
+
+def ladder_kernel(near_count, far_count, has_earlier, pays, *refs):
+    near_refs, refs = refs[:near_count], refs[near_count:]
+    far_refs, refs = refs[:far_count], refs[far_count:]
     tau_refs, refs = refs[:2], refs[2:]
     earlier_ref = refs[0] if has_earlier else None
     doubles_ref = refs[1] if pays else None
-    out_ref = refs[-1]
-    pairs, virt = tau_refs[0].shape[2], tau_refs[0].shape[4]
+    refs = refs[has_earlier + pays :]
+    out_ref, gram_ref = refs[0], refs[1]
+    copies = [
+        pltpu.make_async_copy(ref, refs[2].at[at], refs[3].at[at]) for at, ref in enumerate(far_refs)
+    ]
+    for copy in copies:
+        copy.start()
+    opens = True
+    for ref in near_refs:
+        slabs = ref[...].reshape(-1, ref.shape[-1])
+        add_rows(slabs, tau_refs, gram_ref, opens)
+        opens = False
+    for at, copy in enumerate(copies):
+        copy.wait()
+        add_rows(refs[2][at], tau_refs, gram_ref, opens)
+        opens = False
+    pairs = tau_refs[0].shape[2]
     core = lax.axis_index("k")
     lane = lax.broadcasted_iota(jnp.int32, (NWIN, 128), 1)
     holds = (lax.axis_index("y") == 0) & (lax.axis_index("zh") == 0)
-    for owner, tau_ref in enumerate(tau_refs):
+    for owner in range(2):
         for pair in range(pairs):
-            tau = tau_ref[:, :, pair].reshape(virt, virt)
-            gram = None
-            for slabs in slab_blocks(slab_refs):
-                half = jnp.dot(slabs, tau, preferred_element_type=jnp.float32).astype(jnp.bfloat16)
-                for at in range(0, slabs.shape[0], GROUP):
-                    block = lax.dot_general(
-                        half[at : at + GROUP],
-                        slabs[at : at + GROUP],
-                        (((1,), (1,)), ((), ())),
-                        preferred_element_type=jnp.float32,
-                    )
-                    gram = block if gram is None else gram + block
-            residual = fold(gram)
+            residual = fold(gram_ref[owner * pairs + pair])
             if has_earlier:
                 residual = residual + earlier_ref[owner * pairs + pair]
             if not pays:
@@ -145,11 +158,12 @@
                 out_ref[to * NWIN + a, pair : pair + 1, :] = row[a : a + 1]
 
 
-def ladder(slabs, taus, earlier=None, doubles=None):
+def ladder(near, far, taus, earlier=None, doubles=None):
     pairs, virt = taus[0].shape[2], taus[0].shape[4]
-    rows = sum(slab.size // virt for slab in slabs)
+    rows = sum(slab.size // virt for slab in (*near, *far))
     has_earlier, pays = earlier is not None, doubles is not None
-    specs, operands = [VMEM] * (len(slabs) + 2), [*slabs, *taus]
+    specs = [VMEM] * len(near) + [pl.BlockSpec(memory_space=pl.ANY)] * len(far) + [VMEM] * 2
+    operands = [*near, *far, *taus]
     out = (2 * pairs, NWIN, 128)
     if has_earlier:
         specs.append(VMEM)
@@ -158,12 +172,17 @@
         specs.append(pl.BlockSpec((pairs, 16, 128), lambda i: (0, 0, 0)))
         operands.append(doubles)
         out = (2 * NWIN, pairs, 128)
-    return pl.pallas_call(
-        functools.partial(ladder_kernel, len(slabs), has_earlier, pays),
+    scratch = [pltpu.VMEM((2 * pairs, GROUP, GROUP), jnp.float32)]
+    if far:
+        scratch.append(pltpu.VMEM((len(far),) + far[0].shape, far[0].dtype))
+        scratch.append(pltpu.SemaphoreType.DMA((len(far),)))
+    return pl.pallas_call(
+        functools.partial(ladder_kernel, len(near), len(far), has_earlier, pays),
         out_shape=jax.ShapeDtypeStruct(out, jnp.float32),
         grid=(1,),
         in_specs=specs,
         out_specs=VMEM,
+        scratch_shapes=scratch,
         cost_estimate=pl.CostEstimate(
             flops=2 * pairs * rows * virt * (virt + GROUP) * 2,
             bytes_accessed=2 * rows * virt + 4 * pairs * virt * virt,
@@ -231,9 +250,9 @@
     tau_other = lax.ppermute(tau, "k", SWAP)
     next_above = lax.ppermute(dressed_next, "x", DOWN)
     taus = (tau, tau_other)
-    parts = ladder((slabs,), taus)
-    parts = ladder((dressed_next, next_below), taus, parts)
-    parts = ladder((next_far, next_above), taus, parts, doubles)
+    parts = ladder((slabs,), (), taus)
+    parts = ladder((dressed_next,), (next_far, next_below), taus, parts)
+    parts = ladder((next_above,), (), taus, parts, doubles)
     parts = exchange(parts, ("k",) + AUX)
     total = jnp.sum(parts, axis=0)
     residual = total[:, :NWIN] / denominator[:, :NWIN]

time: 120 us -> 122 us (1.017)
  waiting for transfers between devices: 14.4 us -> 16 us
    ppermute x1, waiting for transfers between devices: 0.01 us -> 1.59 us  [body(): next_far = lax.ppermute(dressed_next, 'x', FAR)]
  transfers between devices with their start and end apart: 11 -> 11, of which waited for: 3 -> 4; matrix products, arithmetic and copies ran while one was open for 1% -> 1% of each run, Pallas kernels for 6% -> 7%
where the time goes in v7:
time: 122 us; the launch traced here: 121 us
  starting transfers between devices  60.7 us (50%)
  blocking collectives  27.7 us (23%)
  waiting for transfers between devices  16 us (13%)
  Pallas kernels  13.9 us (11%)
  local copies, waits for them, and re-layouts  1.98 us (2%)
    all_to_all x1, blocking collectives, exchange(): return lax.all_to_all(copies, axis, split_axis=0, concat_axis=0, tiled=True)  27.7 us
    ppermute x1, starting transfers between devices, body(): other = lax.ppermute(own, 'zh', SWAP)  16.2 us
    pallas_call x3, Pallas kernels, ladder(): pl.pallas_call(functools.partial(ladder_kernel, len(near), len(far), has_...  10.7 us
    ppermute x1, starting transfers between devices, body(): dressed_next = lax.ppermute(dressed, 'zb', SWAP)  9.93 us
    all_to_all x2, starting transfers between devices, exchange(): return lax.all_to_all(copies, axis, split_axis=0, concat_axis=0, tiled=True)  8.63 us
    ppermute x1, waiting for transfers between devices, body(): dressed_next = lax.ppermute(dressed, 'zb', SWAP)  6.58 us
    ppermute x1, starting transfers between devices, body(): tau_other = lax.ppermute(tau, 'k', SWAP)  5.91 us
    ppermute x1, waiting for transfers between devices, body(): far = lax.ppermute(below, 'y', UP)  5.62 us
  transfers between devices with their start and end apart: 11, of which 4 were waited for; matrix products, arithmetic and copies ran while one was open for 1% of the time, Pallas kernels for 7%

profile of v7, /device:TPU:1, one launch (start us, length us, event | category | flops | bytes accessed | tf_op | source)
XLA Modules:
  0.0 121.2 jit_solution(5896904494604279892)
XLA Ops:
  0.0 3.1 %start.1 = (bf16[4,64,512]{2,1,0:T(8,128)(2,1)}, bf16[2,64,512]{2,1,0:T(8,128)(2,1)}, f32[2,128]{1,0:T(2,128)}) custom-call(s32[2,2]{1,0:T(2,128)} %pairs_ref.1, f32[256]{0:T(256)} %occ_energy_ref.1, f32[8]{0:T(128)} %vir_energy_ref.1, bf16[2,64,512]{2,1,0:T(8,128)(2,1)} %refs_4_.1, bf16[256,512]{1,0:T(8,128)(2,1)} %singles_ref.1, ...), custom_call_target="tpu_custom_call" | custom-call | flops 16777216 | bytes 3145728 | tf_op jit(solution)/shard_map/start/pallas_call | solution.py:71
  3.1 16.2 %collective-permute-start.2 = (bf16[2,64,512]{2,1,0:T(8,128)(2,1)}, bf16[2,64,512]{2,1,0:T(8,128)(2,1)S(1)}, u32[]{:S(2)}, u32[]{:S(2)}) collective-permute-start(bf16[2,64,512]{2,1,0:T(8,128)(2,1)} %get-tuple-element.9.own_ref), channel_id=1, source_target_pairs={{0,1},{1,0},{2,3},{3,2},{4,5},{5,4},{6,7},{7,6},{8,9},{9,8},{10,11... | collective-permute-start | bytes 393224 | tf_op jit(solution)/shard_map/ppermute | solution.py:240
  19.4 4.3 %all-to-all-start = ((bf16[4,64,512]{2,1,0:T(8,128)(2,1)}), bf16[4,64,512]{2,1,0:T(8,128)(2,1)S(1)}, u32[]{:S(2)}, u32[]{:S(2)}) async-start(bf16[4,64,512]{2,1,0:T(8,128)(2,1)} %get-tuple-element.8), calls=%async_computation | async-start | bytes 524288 | tf_op jit(solution)/shard_map/all_to_all | solution.py:231
  23.7 0.9 copy-done.1
  24.6 3.2 %collective-permute-start.4 = (bf16[2,2,64,512]{3,2,1,0:T(8,128)(2,1)S(1)}, bf16[2,2,64,512]{3,2,1,0:T(8,128)(2,1)S(1)}, u32[]{:S(2)}, u32[]{:S(2)}) collective-permute-start(bf16[2,2,64,512]{3,2,1,0:T(8,128)(2,1)S(1)} %join.1.own_ref), channel_id=1, source_target_pairs={{0,2},{2,4},{4,6},{6,0},{1,3},{3,5},{5,7},{7,1},{8,10},{10,12},{12... | collective-permute-start | bytes 786440 | tf_op jit(solution)/shard_map/ppermute | solution.py:243
  27.8 3.4 %collective-permute-start.3 = (bf16[2,2,64,512]{3,2,1,0:T(8,128)(2,1)S(1)}, bf16[2,2,64,512]{3,2,1,0:T(8,128)(2,1)S(1)}, u32[]{:S(2)}, u32[]{:S(2)}) collective-permute-start(bf16[2,2,64,512]{3,2,1,0:T(8,128)(2,1)S(1)} %join.1.own_ref), channel_id=1, source_target_pairs={{0,6},{2,0},{4,2},{6,4},{1,7},{3,1},{5,3},{7,5},{8,14},{10,8},{12,... | collective-permute-start | bytes 786440 | tf_op jit(solution)/shard_map/ppermute | solution.py:244
  31.2 2.2 %collective-permute-done.4.below_ref = bf16[2,2,64,512]{3,2,1,0:T(8,128)(2,1)S(1)} collective-permute-done((bf16[2,2,64,512]{3,2,1,0:T(8,128)(2,1)S(1)}, bf16[2,2,64,512]{3,2,1,0:T(8,128)(2,1)S(1)}, u32[]{:S(2)}, u32[]{:S(2)}) %collective-permute-start.4) | collective-permute-done | bytes 262176 | tf_op jit(solution)/shard_map/ppermute | solution.py:243
  33.4 3.0 %collective-permute-start.5 = (bf16[2,2,64,512]{3,2,1,0:T(8,128)(2,1)S(1)}, bf16[2,2,64,512]{3,2,1,0:T(8,128)(2,1)S(1)}, u32[]{:S(2)}, u32[]{:S(2)}) collective-permute-start(bf16[2,2,64,512]{3,2,1,0:T(8,128)(2,1)S(1)} %collective-permute-done.4.below_ref), channel_id=1, source_target_pairs={{0,2},{2,4},{4,6},{6,0},{1,3},{3,5},{5,7},{7,1},{8,10},{10,12},{12... | collective-permute-start | bytes 786440 | tf_op jit(solution)/shard_map/ppermute | solution.py:245
  36.4 5.6 %collective-permute-done.5.far_ref = bf16[2,2,64,512]{3,2,1,0:T(8,128)(2,1)S(1)} collective-permute-done((bf16[2,2,64,512]{3,2,1,0:T(8,128)(2,1)S(1)}, bf16[2,2,64,512]{3,2,1,0:T(8,128)(2,1)S(1)}, u32[]{:S(2)}, u32[]{:S(2)}) %collective-permute-start.5) | collective-permute-done | bytes 262176 | tf_op jit(solution)/shard_map/ppermute | solution.py:245
  42.0 0.1 assemble.1.refs_1_.refs_3_
  42.1 5.9 %collective-permute-start.6 = (bf16[4,2,2,64,512]{4,3,2,1,0:T(8,128)(2,1)S(1)}, bf16[4,2,2,64,512]{4,3,2,1,0:T(8,128)(2,1)S(1)}, u32[]{:S(2)}, u32[]{:S(2)}) collective-permute-start(bf16[4,2,2,64,512]{4,3,2,1,0:T(8,128)(2,1)S(1)} %assemble.1.refs_1_.refs_3_), channel_id=1, source_target_pairs={{0,8},{8,0},{1,9},{9,1},{2,10},{10,2},{3,11},{11,3},{4,12},{12,4},... | collective-permute-start | bytes 3145736 | tf_op jit(solution)/shard_map/ppermute | solution.py:250
  48.0 1.1 broadcast_in_dim.8
  49.1 4.3 %all-to-all-start.1 = ((bf16[4,256,512]{2,1,0:T(8,128)(2,1)}), bf16[4,256,512]{2,1,0:T(8,128)(2,1)S(1)}, u32[]{:S(2)}, u32[]{:S(2)}) async-start(bf16[4,256,512]{2,1,0:T(8,128)(2,1)} %broadcast_in_dim.8), calls=%async_computation.1 | async-start | bytes 2097152 | tf_op jit(solution)/shard_map/all_to_all | solution.py:231
  53.4 9.9 %collective-permute-start = (bf16[256,512]{1,0:T(8,128)(2,1)}, bf16[256,512]{1,0:T(8,128)(2,1)S(1)}, u32[]{:S(2)}, u32[]{:S(2)}) collective-permute-start(bf16[256,512]{1,0:T(8,128)(2,1)} %bitcast.5), channel_id=1, source_target_pairs={{0,64},{64,0},{1,65},{65,1},{2,66},{66,2},{3,67},{67,3},{4,68},{68... | collective-permute-start | bytes 786440 | tf_op jit(solution)/shard_map/ppermute | solution.py:241
  63.3 6.6 %collective-permute-done.refs_0_ = bf16[256,512]{1,0:T(8,128)(2,1)S(1)} collective-permute-done((bf16[256,512]{1,0:T(8,128)(2,1)}, bf16[256,512]{1,0:T(8,128)(2,1)S(1)}, u32[]{:S(2)}, u32[]{:S(2)}) %collective-permute-start) | collective-permute-done | bytes 262176 | tf_op jit(solution)/shard_map/ppermute | solution.py:241
  69.9 3.1 %collective-permute-start.8 = (bf16[256,512]{1,0:T(8,128)(2,1)S(1)}, bf16[256,512]{1,0:T(8,128)(2,1)}, u32[]{:S(2)}, u32[]{:S(2)}) collective-permute-start(bf16[256,512]{1,0:T(8,128)(2,1)S(1)} %collective-permute-done.refs_0_), channel_id=1, source_target_pairs={{0,16},{16,32},{32,48},{48,0},{1,17},{17,33},{33,49},{49,1},{2,18}... | collective-permute-start | bytes 786440 | tf_op jit(solution)/shard_map/ppermute | solution.py:248
  73.0 4.3 %collective-permute-start.7 = (bf16[256,512]{1,0:T(8,128)(2,1)S(1)}, bf16[256,512]{1,0:T(8,128)(2,1)}, u32[]{:S(2)}, u32[]{:S(2)}) collective-permute-start(bf16[256,512]{1,0:T(8,128)(2,1)S(1)} %collective-permute-done.refs_0_), channel_id=1, source_target_pairs={{0,32},{16,48},{32,0},{48,16},{1,33},{17,49},{33,1},{49,17},{2,34}... | collective-permute-start | bytes 786440 | tf_op jit(solution)/shard_map/ppermute | solution.py:247
  77.3 3.1 %collective-permute-start.1 = (bf16[256,512]{1,0:T(8,128)(2,1)S(1)}, bf16[256,512]{1,0:T(8,128)(2,1)}, u32[]{:S(2)}, u32[]{:S(2)}) collective-permute-start(bf16[256,512]{1,0:T(8,128)(2,1)S(1)} %collective-permute-done.refs_0_), channel_id=1, source_target_pairs={{0,48},{16,0},{32,16},{48,32},{1,49},{17,1},{33,17},{49,33},{2,50}... | collective-permute-start | bytes 786440 | tf_op jit(solution)/shard_map/ppermute | solution.py:251
  80.4 4.3 %ladder.3.refs_5_ = f32[4,8,128]{2,1,0:T(8,128)S(1)} custom-call(bf16[4,256,512]{2,1,0:T(8,128)(2,1)S(1)} %all-to-all-done.1.refs_0_, bf16[4,2,2,64,512]{4,3,2,1,0:T(8,128)(2,1)S(1)} %assemble.1.refs_1_.refs_3_, bf16[4,2,2,64,512]{4,3,2,1,0:T(8,128)(2,1)S(1)} %collective-permute-done.6.refs_2_.refs_4_), custom_call_target="tpu_custom_call" | custom-call | flops 3221225472 | bytes 3145728 | tf_op jit(solution)/shard_map/ladder/pallas_call | solution.py:179
  84.8 1.6 %collective-permute-done.7.refs_1_ = bf16[256,512]{1,0:T(8,128)(2,1)} collective-permute-done((bf16[256,512]{1,0:T(8,128)(2,1)S(1)}, bf16[256,512]{1,0:T(8,128)(2,1)}, u32[]{:S(2)}, u32[]{:S(2)}) %collective-permute-start.7) | collective-permute-done | bytes 262176 | tf_op jit(solution)/shard_map/ppermute | solution.py:247
  86.4 3.9 %ladder.4.refs_3_ = f32[4,8,128]{2,1,0:T(8,128)S(1)} custom-call(bf16[256,512]{1,0:T(8,128)(2,1)S(1)} %collective-permute-done.refs_0_, bf16[256,512]{1,0:T(8,128)(2,1)} %collective-permute-done.7.refs_1_, bf16[256,512]{1,0:T(8,128)(2,1)} %collective-permute-done.8.refs_2_, bf16[4,2,2,64,512]{4,3,2,1,0:T(8,128)(2,1)S(1)} %assemble.1.refs_1_.refs_3_, ...), custom_call_target="tpu_custom_call" | custom-call | flops 2415919104 | bytes 2883584 | tf_op jit(solution)/shard_map/ladder/pallas_call | solution.py:179
  90.3 2.5 %ladder.5 = f32[16,2,128]{2,1,0:T(2,128)S(1)} custom-call(bf16[256,512]{1,0:T(8,128)(2,1)} %collective-permute-done.1.refs_0_, bf16[4,2,2,64,512]{4,3,2,1,0:T(8,128)(2,1)S(1)} %assemble.1.refs_1_.refs_3_, bf16[4,2,2,64,512]{4,3,2,1,0:T(8,128)(2,1)S(1)} %collective-permute-done.6.refs_2_.refs_4_, f32[4,8,128]{2,1,0:T(8,128)S(1)} %ladder.4.refs_3_, ...), custom_call_target="tpu_custom_call" | custom-call | flops 805306368 | bytes 2359296 | tf_op jit(solution)/shard_map/ladder/pallas_call | solution.py:179
  92.8 27.7 %all_to_all.15 = f32[16,2,128]{2,1,0:T(2,128)S(1)} all-to-all(f32[16,2,128]{2,1,0:T(2,128)S(1)} %ladder.5), channel_id=1, replica_groups=mesh['zm'=4,'zb'=2,'x'=4,'k'=2,'y'=4,'zh'=2] {'k','y','zh'}, dimensions={0} | all-to-all | bytes 32768 | tf_op jit(solution)/shard_map/all_to_all | solution.py:231
  120.5 0.6 divide_add_fusion
  (16 shorter events, 0.1 us)
Async XLA Ops:
  3.1 20.5 %collective-permute-start.2 = (bf16[2,64,512]{2,1,0:T(8,128)(2,1)}, bf16[2,64,512]{2,1,0:T(8,128)(2,1)S(1)}, u32[]{:S(2)}, u32[]{:S(2)}) collective-permute-start(bf16[2,64,512]{2,1,0:T(8,128)(2,1)} %get-tuple-element.9.own_ref), channel_id=1, source_target_pairs={{0,1},{1,0},{2,3},{3,2},{4,5},{5,4},{6,7},{7,6},{8,9},{9,8},{10,11... | collective-permute-start | bytes 393224 | tf_op jit(solution)/shard_map/ppermute | solution.py:240
  19.4 28.6 %all-to-all-start = ((bf16[4,64,512]{2,1,0:T(8,128)(2,1)}), bf16[4,64,512]{2,1,0:T(8,128)(2,1)S(1)}, u32[]{:S(2)}, u32[]{:S(2)}) async-start(bf16[4,64,512]{2,1,0:T(8,128)(2,1)} %get-tuple-element.8), calls=%async_computation | async-start | bytes 524288 | tf_op jit(solution)/shard_map/all_to_all | solution.py:231
  23.7 0.9 copy-start.1
  24.6 8.7 %collective-permute-start.4 = (bf16[2,2,64,512]{3,2,1,0:T(8,128)(2,1)S(1)}, bf16[2,2,64,512]{3,2,1,0:T(8,128)(2,1)S(1)}, u32[]{:S(2)}, u32[]{:S(2)}) collective-permute-start(bf16[2,2,64,512]{3,2,1,0:T(8,128)(2,1)S(1)} %join.1.own_ref), channel_id=1, source_target_pairs={{0,2},{2,4},{4,6},{6,0},{1,3},{3,5},{5,7},{7,1},{8,10},{10,12},{12... | collective-permute-start | bytes 786440 | tf_op jit(solution)/shard_map/ppermute | solution.py:243
  27.8 8.5 %collective-permute-start.3 = (bf16[2,2,64,512]{3,2,1,0:T(8,128)(2,1)S(1)}, bf16[2,2,64,512]{3,2,1,0:T(8,128)(2,1)S(1)}, u32[]{:S(2)}, u32[]{:S(2)}) collective-permute-start(bf16[2,2,64,512]{3,2,1,0:T(8,128)(2,1)S(1)} %join.1.own_ref), channel_id=1, source_target_pairs={{0,6},{2,0},{4,2},{6,4},{1,7},{3,1},{5,3},{7,5},{8,14},{10,8},{12,... | collective-permute-start | bytes 786440 | tf_op jit(solution)/shard_map/ppermute | solution.py:244
  33.4 8.6 %collective-permute-start.5 = (bf16[2,2,64,512]{3,2,1,0:T(8,128)(2,1)S(1)}, bf16[2,2,64,512]{3,2,1,0:T(8,128)(2,1)S(1)}, u32[]{:S(2)}, u32[]{:S(2)}) collective-permute-start(bf16[2,2,64,512]{3,2,1,0:T(8,128)(2,1)S(1)} %collective-permute-done.4.below_ref), channel_id=1, source_target_pairs={{0,2},{2,4},{4,6},{6,0},{1,3},{3,5},{5,7},{7,1},{8,10},{10,12},{12... | collective-permute-start | bytes 786440 | tf_op jit(solution)/shard_map/ppermute | solution.py:245
  42.1 38.4 %collective-permute-start.6 = (bf16[4,2,2,64,512]{4,3,2,1,0:T(8,128)(2,1)S(1)}, bf16[4,2,2,64,512]{4,3,2,1,0:T(8,128)(2,1)S(1)}, u32[]{:S(2)}, u32[]{:S(2)}) collective-permute-start(bf16[4,2,2,64,512]{4,3,2,1,0:T(8,128)(2,1)S(1)} %assemble.1.refs_1_.refs_3_), channel_id=1, source_target_pairs={{0,8},{8,0},{1,9},{9,1},{2,10},{10,2},{3,11},{11,3},{4,12},{12,4},... | collective-permute-start | bytes 3145736 | tf_op jit(solution)/shard_map/ppermute | solution.py:250
  48.0 1.1 copy-start.2
  49.1 31.4 %all-to-all-start.1 = ((bf16[4,256,512]{2,1,0:T(8,128)(2,1)}), bf16[4,256,512]{2,1,0:T(8,128)(2,1)S(1)}, u32[]{:S(2)}, u32[]{:S(2)}) async-start(bf16[4,256,512]{2,1,0:T(8,128)(2,1)} %broadcast_in_dim.8), calls=%async_computation.1 | async-start | bytes 2097152 | tf_op jit(solution)/shard_map/all_to_all | solution.py:231
  53.4 16.5 %collective-permute-start = (bf16[256,512]{1,0:T(8,128)(2,1)}, bf16[256,512]{1,0:T(8,128)(2,1)S(1)}, u32[]{:S(2)}, u32[]{:S(2)}) collective-permute-start(bf16[256,512]{1,0:T(8,128)(2,1)} %bitcast.5), channel_id=1, source_target_pairs={{0,64},{64,0},{1,65},{65,1},{2,66},{66,2},{3,67},{67,3},{4,68},{68... | collective-permute-start | bytes 786440 | tf_op jit(solution)/shard_map/ppermute | solution.py:241
  69.9 14.8 %collective-permute-start.8 = (bf16[256,512]{1,0:T(8,128)(2,1)S(1)}, bf16[256,512]{1,0:T(8,128)(2,1)}, u32[]{:S(2)}, u32[]{:S(2)}) collective-permute-start(bf16[256,512]{1,0:T(8,128)(2,1)S(1)} %collective-permute-done.refs_0_), channel_id=1, source_target_pairs={{0,16},{16,32},{32,48},{48,0},{1,17},{17,33},{33,49},{49,1},{2,18}... | collective-permute-start | bytes 786440 | tf_op jit(solution)/shard_map/ppermute | solution.py:248
  73.0 13.3 %collective-permute-start.7 = (bf16[256,512]{1,0:T(8,128)(2,1)S(1)}, bf16[256,512]{1,0:T(8,128)(2,1)}, u32[]{:S(2)}, u32[]{:S(2)}) collective-permute-start(bf16[256,512]{1,0:T(8,128)(2,1)S(1)} %collective-permute-done.refs_0_), channel_id=1, source_target_pairs={{0,32},{16,48},{32,0},{48,16},{1,33},{17,49},{33,1},{49,17},{2,34}... | collective-permute-start | bytes 786440 | tf_op jit(solution)/shard_map/ppermute | solution.py:247
  77.3 12.9 %collective-permute-start.1 = (bf16[256,512]{1,0:T(8,128)(2,1)S(1)}, bf16[256,512]{1,0:T(8,128)(2,1)}, u32[]{:S(2)}, u32[]{:S(2)}) collective-permute-start(bf16[256,512]{1,0:T(8,128)(2,1)S(1)} %collective-permute-done.refs_0_), channel_id=1, source_target_pairs={{0,48},{16,0},{32,16},{48,32},{1,49},{17,1},{33,17},{49,33},{2,50}... | collective-permute-start | bytes 786440 | tf_op jit(solution)/shard_map/ppermute | solution.py:251
  84.8 5.5 %copy-start = (bf16[2,64,512]{2,1,0:T(8,128)(2,1)S(1)}, bf16[2,64,512]{2,1,0:T(8,128)(2,1)}, u32[]{:S(2)}) copy-start(bf16[2,64,512]{2,1,0:T(8,128)(2,1)} %refs_4_.1) | copy-start | bytes 393220
  90.3 30.3 %copy-start.3 = (f32[2,128]{1,0:T(2,128)S(1)}, f32[2,128]{1,0:T(2,128)}, u32[]{:S(2)}) copy-start(f32[2,128]{1,0:T(2,128)} %get-tuple-element.10) | copy-start | bytes 3076

commit v8 on v7

--- a/solution.py
+++ b/solution.py
@@ -83,17 +83,23 @@
     )(pair_list, occ_energy, vir_energy, doubles, singles, vir_slabs, occ_slabs)
 
 
-def fold(gram):
-    row = lax.broadcasted_iota(jnp.int32, (GROUP, GROUP), 0) // NWIN
-    col = lax.broadcasted_iota(jnp.int32, (GROUP, GROUP), 1) // NWIN
-    kept = jnp.where(row == col, gram, 0.0)
-    folded = jnp.sum(kept.reshape(GROUP // NWIN, NWIN, GROUP), axis=0)
-    folded = folded[:, :128] + folded[:, 128:]
+def diagonal(gram_ref, index):
+    place = lax.broadcasted_iota(jnp.int32, (NWIN, 128), 1) // NWIN
+    total = jnp.zeros((NWIN, 128), jnp.float32)
+    per_row = 128 // NWIN
+    for q in range(GROUP // NWIN):
+        lanes = q // per_row * 128
+        block = gram_ref[index, q * NWIN : (q + 1) * NWIN, lanes : lanes + 128]
+        total = total + jnp.where(place == q % per_row, block, 0.0)
+    return total
+
+
+def fold(blocks):
     shift = 64
     while shift >= NWIN:
-        folded = folded + pltpu.roll(folded, shift, 1)
+        blocks = blocks + pltpu.roll(blocks, shift, 1)
         shift //= 2
-    return folded
+    return blocks
 
 
 def add_rows(slabs, tau_refs, gram_ref, opens):
@@ -142,12 +148,13 @@
     holds = (lax.axis_index("y") == 0) & (lax.axis_index("zh") == 0)
     for owner in range(2):
         for pair in range(pairs):
-            residual = fold(gram_ref[owner * pairs + pair])
+            residual = diagonal(gram_ref, owner * pairs + pair)
             if has_earlier:
                 residual = residual + earlier_ref[owner * pairs + pair]
             if not pays:
                 out_ref[owner * pairs + pair] = residual
                 continue
+            residual = fold(residual)
             row = jnp.where(lane < NWIN, residual, 0.0)
             if owner == 0:
                 doubles = pltpu.roll(doubles_ref[pair].astype(jnp.float32)[:NWIN], NWIN, 1)
@@ -251,8 +258,8 @@
     next_above = lax.ppermute(dressed_next, "x", DOWN)
     taus = (tau, tau_other)
     parts = ladder((slabs,), (), taus)
-    parts = ladder((dressed_next,), (next_far, next_below), taus, parts)
-    parts = ladder((next_above,), (), taus, parts, doubles)
+    parts = ladder((dressed_next,), (next_below, next_above), taus, parts)
+    parts = ladder((next_far,), (), taus, parts, doubles)
     parts = exchange(parts, ("k",) + AUX)
     total = jnp.sum(parts, axis=0)
     residual = total[:, :NWIN] / denominator[:, :NWIN]

time: 122 us -> 125 us (1.025)
  blocking collectives: 27.7 us -> 32.5 us
    all_to_all x1, blocking collectives: 27.7 us -> 32.5 us  [exchange(): return lax.all_to_all(copies, axis, split_axis=0, concat_axis=0, tiled=True)]
    ppermute x1, waiting for transfers between devices: 1.59 us -> 0.2 us  [body(): next_far = lax.ppermute(dressed_next, 'x', FAR)]
  transfers between devices with their start and end apart: 11 -> 11, of which waited for: 4 -> 5; matrix products, arithmetic and copies ran while one was open for 1% -> 1% of each run, Pallas kernels for 7% -> 6%
where the time goes in v8:
time: 125 us; the launch traced here: 124 us
  starting transfers between devices  60.1 us (48%)
  blocking collectives  32.5 us (26%)
  waiting for transfers between devices  15.5 us (12%)
  Pallas kernels  13.4 us (11%)
  local copies, waits for them, and re-layouts  1.98 us (2%)
    all_to_all x1, blocking collectives, exchange(): return lax.all_to_all(copies, axis, split_axis=0, concat_axis=0, tiled=True)  32.5 us
    ppermute x1, starting transfers between devices, body(): other = lax.ppermute(own, 'zh', SWAP)  16.2 us
    pallas_call x3, Pallas kernels, ladder(): pl.pallas_call(functools.partial(ladder_kernel, len(near), len(far), has_...  10.1 us
    ppermute x1, starting transfers between devices, body(): dressed_next = lax.ppermute(dressed, 'zb', SWAP)  9.93 us
    all_to_all x2, starting transfers between devices, exchange(): return lax.all_to_all(copies, axis, split_axis=0, concat_axis=0, tiled=True)  8.63 us
    ppermute x1, waiting for transfers between devices, body(): dressed_next = lax.ppermute(dressed, 'zb', SWAP)  6.58 us
    ppermute x1, starting transfers between devices, body(): tau_other = lax.ppermute(tau, 'k', SWAP)  5.91 us
    ppermute x1, waiting for transfers between devices, body(): far = lax.ppermute(below, 'y', UP)  5.62 us
  transfers between devices with their start and end apart: 11, of which 5 were waited for; matrix products, arithmetic and copies ran while one was open for 1% of the time, Pallas kernels for 6%

profile of v8, /device:TPU:1, one launch (start us, length us, event | category | flops | bytes accessed | tf_op | source)
XLA Modules:
  0.0 124.3 jit_solution(18425247133809703131)
XLA Ops:
  0.0 3.1 %start.1 = (bf16[4,64,512]{2,1,0:T(8,128)(2,1)}, bf16[2,64,512]{2,1,0:T(8,128)(2,1)}, f32[2,128]{1,0:T(2,128)}) custom-call(s32[2,2]{1,0:T(2,128)} %pairs_ref.1, f32[256]{0:T(256)} %occ_energy_ref.1, f32[8]{0:T(128)} %vir_energy_ref.1, bf16[2,64,512]{2,1,0:T(8,128)(2,1)} %refs_4_.1, bf16[256,512]{1,0:T(8,128)(2,1)} %singles_ref.1, ...), custom_call_target="tpu_custom_call" | custom-call | flops 16777216 | bytes 3145728 | tf_op jit(solution)/shard_map/start/pallas_call | solution.py:71
  3.1 16.2 %collective-permute-start.2 = (bf16[2,64,512]{2,1,0:T(8,128)(2,1)}, bf16[2,64,512]{2,1,0:T(8,128)(2,1)S(1)}, u32[]{:S(2)}, u32[]{:S(2)}) collective-permute-start(bf16[2,64,512]{2,1,0:T(8,128)(2,1)} %get-tuple-element.9.own_ref), channel_id=1, source_target_pairs={{0,1},{1,0},{2,3},{3,2},{4,5},{5,4},{6,7},{7,6},{8,9},{9,8},{10,11... | collective-permute-start | bytes 393224 | tf_op jit(solution)/shard_map/ppermute | solution.py:247
  19.4 4.3 %all-to-all-start = ((bf16[4,64,512]{2,1,0:T(8,128)(2,1)}), bf16[4,64,512]{2,1,0:T(8,128)(2,1)S(1)}, u32[]{:S(2)}, u32[]{:S(2)}) async-start(bf16[4,64,512]{2,1,0:T(8,128)(2,1)} %get-tuple-element.8), calls=%async_computation | async-start | bytes 524288 | tf_op jit(solution)/shard_map/all_to_all | solution.py:238
  23.7 0.9 copy-done.1
  24.6 3.2 %collective-permute-start.4 = (bf16[2,2,64,512]{3,2,1,0:T(8,128)(2,1)S(1)}, bf16[2,2,64,512]{3,2,1,0:T(8,128)(2,1)S(1)}, u32[]{:S(2)}, u32[]{:S(2)}) collective-permute-start(bf16[2,2,64,512]{3,2,1,0:T(8,128)(2,1)S(1)} %join.1.own_ref), channel_id=1, source_target_pairs={{0,2},{2,4},{4,6},{6,0},{1,3},{3,5},{5,7},{7,1},{8,10},{10,12},{12... | collective-permute-start | bytes 786440 | tf_op jit(solution)/shard_map/ppermute | solution.py:250
  27.8 3.4 %collective-permute-start.3 = (bf16[2,2,64,512]{3,2,1,0:T(8,128)(2,1)S(1)}, bf16[2,2,64,512]{3,2,1,0:T(8,128)(2,1)S(1)}, u32[]{:S(2)}, u32[]{:S(2)}) collective-permute-start(bf16[2,2,64,512]{3,2,1,0:T(8,128)(2,1)S(1)} %join.1.own_ref), channel_id=1, source_target_pairs={{0,6},{2,0},{4,2},{6,4},{1,7},{3,1},{5,3},{7,5},{8,14},{10,8},{12,... | collective-permute-start | bytes 786440 | tf_op jit(solution)/shard_map/ppermute | solution.py:251
  31.2 2.2 %collective-permute-done.4.below_ref = bf16[2,2,64,512]{3,2,1,0:T(8,128)(2,1)S(1)} collective-permute-done((bf16[2,2,64,512]{3,2,1,0:T(8,128)(2,1)S(1)}, bf16[2,2,64,512]{3,2,1,0:T(8,128)(2,1)S(1)}, u32[]{:S(2)}, u32[]{:S(2)}) %collective-permute-start.4) | collective-permute-done | bytes 262176 | tf_op jit(solution)/shard_map/ppermute | solution.py:250
  33.4 3.0 %collective-permute-start.5 = (bf16[2,2,64,512]{3,2,1,0:T(8,128)(2,1)S(1)}, bf16[2,2,64,512]{3,2,1,0:T(8,128)(2,1)S(1)}, u32[]{:S(2)}, u32[]{:S(2)}) collective-permute-start(bf16[2,2,64,512]{3,2,1,0:T(8,128)(2,1)S(1)} %collective-permute-done.4.below_ref), channel_id=1, source_target_pairs={{0,2},{2,4},{4,6},{6,0},{1,3},{3,5},{5,7},{7,1},{8,10},{10,12},{12... | collective-permute-start | bytes 786440 | tf_op jit(solution)/shard_map/ppermute | solution.py:252
  36.4 5.6 %collective-permute-done.5.far_ref = bf16[2,2,64,512]{3,2,1,0:T(8,128)(2,1)S(1)} collective-permute-done((bf16[2,2,64,512]{3,2,1,0:T(8,128)(2,1)S(1)}, bf16[2,2,64,512]{3,2,1,0:T(8,128)(2,1)S(1)}, u32[]{:S(2)}, u32[]{:S(2)}) %collective-permute-start.5) | collective-permute-done | bytes 262176 | tf_op jit(solution)/shard_map/ppermute | solution.py:252
  42.1 5.9 %collective-permute-start.6 = (bf16[4,2,2,64,512]{4,3,2,1,0:T(8,128)(2,1)S(1)}, bf16[4,2,2,64,512]{4,3,2,1,0:T(8,128)(2,1)S(1)}, u32[]{:S(2)}, u32[]{:S(2)}) collective-permute-start(bf16[4,2,2,64,512]{4,3,2,1,0:T(8,128)(2,1)S(1)} %assemble.1.refs_1_.refs_3_), channel_id=1, source_target_pairs={{0,8},{8,0},{1,9},{9,1},{2,10},{10,2},{3,11},{11,3},{4,12},{12,4},... | collective-permute-start | bytes 3145736 | tf_op jit(solution)/shard_map/ppermute | solution.py:257
  48.0 1.1 broadcast_in_dim.8
  49.1 4.3 %all-to-all-start.1 = ((bf16[4,256,512]{2,1,0:T(8,128)(2,1)}), bf16[4,256,512]{2,1,0:T(8,128)(2,1)S(1)}, u32[]{:S(2)}, u32[]{:S(2)}) async-start(bf16[4,256,512]{2,1,0:T(8,128)(2,1)} %broadcast_in_dim.8), calls=%async_computation.1 | async-start | bytes 2097152 | tf_op jit(solution)/shard_map/all_to_all | solution.py:238
  53.4 9.9 %collective-permute-start = (bf16[256,512]{1,0:T(8,128)(2,1)}, bf16[256,512]{1,0:T(8,128)(2,1)S(1)}, u32[]{:S(2)}, u32[]{:S(2)}) collective-permute-start(bf16[256,512]{1,0:T(8,128)(2,1)} %bitcast.5), channel_id=1, source_target_pairs={{0,64},{64,0},{1,65},{65,1},{2,66},{66,2},{3,67},{67,3},{4,68},{68... | collective-permute-start | bytes 786440 | tf_op jit(solution)/shard_map/ppermute | solution.py:248
  63.3 6.6 %collective-permute-done.refs_0_ = bf16[256,512]{1,0:T(8,128)(2,1)S(1)} collective-permute-done((bf16[256,512]{1,0:T(8,128)(2,1)}, bf16[256,512]{1,0:T(8,128)(2,1)S(1)}, u32[]{:S(2)}, u32[]{:S(2)}) %collective-permute-start) | collective-permute-done | bytes 262176 | tf_op jit(solution)/shard_map/ppermute | solution.py:248
  69.9 4.3 %collective-permute-start.8 = (bf16[256,512]{1,0:T(8,128)(2,1)S(1)}, bf16[256,512]{1,0:T(8,128)(2,1)}, u32[]{:S(2)}, u32[]{:S(2)}) collective-permute-start(bf16[256,512]{1,0:T(8,128)(2,1)S(1)} %collective-permute-done.refs_0_), channel_id=1, source_target_pairs={{0,48},{16,0},{32,16},{48,32},{1,49},{17,1},{33,17},{49,33},{2,50}... | collective-permute-start | bytes 786440 | tf_op jit(solution)/shard_map/ppermute | solution.py:258
  74.2 1.9 %collective-permute-start.7 = (bf16[256,512]{1,0:T(8,128)(2,1)S(1)}, bf16[256,512]{1,0:T(8,128)(2,1)}, u32[]{:S(2)}, u32[]{:S(2)}) collective-permute-start(bf16[256,512]{1,0:T(8,128)(2,1)S(1)} %collective-permute-done.refs_0_), channel_id=1, source_target_pairs={{0,16},{16,32},{32,48},{48,0},{1,17},{17,33},{33,49},{49,1},{2,18}... | collective-permute-start | bytes 786440 | tf_op jit(solution)/shard_map/ppermute | solution.py:255
  76.2 3.7 %collective-permute-start.1 = (bf16[256,512]{1,0:T(8,128)(2,1)S(1)}, bf16[256,512]{1,0:T(8,128)(2,1)}, u32[]{:S(2)}, u32[]{:S(2)}) collective-permute-start(bf16[256,512]{1,0:T(8,128)(2,1)S(1)} %collective-permute-done.refs_0_), channel_id=1, source_target_pairs={{0,32},{16,48},{32,0},{48,16},{1,33},{17,49},{33,1},{49,17},{2,34}... | collective-permute-start | bytes 786440 | tf_op jit(solution)/shard_map/ppermute | solution.py:254
  79.8 4.0 %ladder.3.refs_5_ = f32[4,8,128]{2,1,0:T(8,128)S(1)} custom-call(bf16[4,256,512]{2,1,0:T(8,128)(2,1)S(1)} %all-to-all-done.1.refs_0_, bf16[4,2,2,64,512]{4,3,2,1,0:T(8,128)(2,1)S(1)} %assemble.1.refs_1_.refs_3_, bf16[4,2,2,64,512]{4,3,2,1,0:T(8,128)(2,1)S(1)} %collective-permute-done.6.refs_2_.refs_4_), custom_call_target="tpu_custom_call" | custom-call | flops 3221225472 | bytes 3145728 | tf_op jit(solution)/shard_map/ladder/pallas_call | solution.py:186
  83.9 0.9 collective-permute-done.7.refs_1_
  84.8 3.6 %ladder.4.refs_3_ = f32[4,8,128]{2,1,0:T(8,128)S(1)} custom-call(bf16[256,512]{1,0:T(8,128)(2,1)S(1)} %collective-permute-done.refs_0_, bf16[256,512]{1,0:T(8,128)(2,1)} %collective-permute-done.7.refs_1_, bf16[256,512]{1,0:T(8,128)(2,1)} %collective-permute-done.8.refs_2_, bf16[4,2,2,64,512]{4,3,2,1,0:T(8,128)(2,1)S(1)} %assemble.1.refs_1_.refs_3_, ...), custom_call_target="tpu_custom_call" | custom-call | flops 2415919104 | bytes 2883584 | tf_op jit(solution)/shard_map/ladder/pallas_call | solution.py:186
  88.4 0.2 collective-permute-done.1.refs_0_
  88.6 2.5 %ladder.5 = f32[16,2,128]{2,1,0:T(2,128)S(1)} custom-call(bf16[256,512]{1,0:T(8,128)(2,1)} %collective-permute-done.1.refs_0_, bf16[4,2,2,64,512]{4,3,2,1,0:T(8,128)(2,1)S(1)} %assemble.1.refs_1_.refs_3_, bf16[4,2,2,64,512]{4,3,2,1,0:T(8,128)(2,1)S(1)} %collective-permute-done.6.refs_2_.refs_4_, f32[4,8,128]{2,1,0:T(8,128)S(1)} %ladder.4.refs_3_, ...), custom_call_target="tpu_custom_call" | custom-call | flops 805306368 | bytes 2359296 | tf_op jit(solution)/shard_map/ladder/pallas_call | solution.py:186
  91.1 32.5 %all_to_all.15 = f32[16,2,128]{2,1,0:T(2,128)S(1)} all-to-all(f32[16,2,128]{2,1,0:T(2,128)S(1)} %ladder.5), channel_id=1, replica_groups=mesh['zm'=4,'zb'=2,'x'=4,'k'=2,'y'=4,'zh'=2] {'k','y','zh'}, dimensions={0} | all-to-all | bytes 32768 | tf_op jit(solution)/shard_map/all_to_all | solution.py:238
  123.7 0.6 divide_add_fusion
  (16 shorter events, 0.2 us)
Async XLA Ops:
  3.1 20.5 %collective-permute-start.2 = (bf16[2,64,512]{2,1,0:T(8,128)(2,1)}, bf16[2,64,512]{2,1,0:T(8,128)(2,1)S(1)}, u32[]{:S(2)}, u32[]{:S(2)}) collective-permute-start(bf16[2,64,512]{2,1,0:T(8,128)(2,1)} %get-tuple-element.9.own_ref), channel_id=1, source_target_pairs={{0,1},{1,0},{2,3},{3,2},{4,5},{5,4},{6,7},{7,6},{8,9},{9,8},{10,11... | collective-permute-start | bytes 393224 | tf_op jit(solution)/shard_map/ppermute | solution.py:247
  19.4 28.6 %all-to-all-start = ((bf16[4,64,512]{2,1,0:T(8,128)(2,1)}), bf16[4,64,512]{2,1,0:T(8,128)(2,1)S(1)}, u32[]{:S(2)}, u32[]{:S(2)}) async-start(bf16[4,64,512]{2,1,0:T(8,128)(2,1)} %get-tuple-element.8), calls=%async_computation | async-start | bytes 524288 | tf_op jit(solution)/shard_map/all_to_all | solution.py:238
  23.7 0.9 copy-start.1
  24.6 8.7 %collective-permute-start.4 = (bf16[2,2,64,512]{3,2,1,0:T(8,128)(2,1)S(1)}, bf16[2,2,64,512]{3,2,1,0:T(8,128)(2,1)S(1)}, u32[]{:S(2)}, u32[]{:S(2)}) collective-permute-start(bf16[2,2,64,512]{3,2,1,0:T(8,128)(2,1)S(1)} %join.1.own_ref), channel_id=1, source_target_pairs={{0,2},{2,4},{4,6},{6,0},{1,3},{3,5},{5,7},{7,1},{8,10},{10,12},{12... | collective-permute-start | bytes 786440 | tf_op jit(solution)/shard_map/ppermute | solution.py:250
  27.8 8.5 %collective-permute-start.3 = (bf16[2,2,64,512]{3,2,1,0:T(8,128)(2,1)S(1)}, bf16[2,2,64,512]{3,2,1,0:T(8,128)(2,1)S(1)}, u32[]{:S(2)}, u32[]{:S(2)}) collective-permute-start(bf16[2,2,64,512]{3,2,1,0:T(8,128)(2,1)S(1)} %join.1.own_ref), channel_id=1, source_target_pairs={{0,6},{2,0},{4,2},{6,4},{1,7},{3,1},{5,3},{7,5},{8,14},{10,8},{12,... | collective-permute-start | bytes 786440 | tf_op jit(solution)/shard_map/ppermute | solution.py:251
  33.4 8.6 %collective-permute-start.5 = (bf16[2,2,64,512]{3,2,1,0:T(8,128)(2,1)S(1)}, bf16[2,2,64,512]{3,2,1,0:T(8,128)(2,1)S(1)}, u32[]{:S(2)}, u32[]{:S(2)}) collective-permute-start(bf16[2,2,64,512]{3,2,1,0:T(8,128)(2,1)S(1)} %collective-permute-done.4.below_ref), channel_id=1, source_target_pairs={{0,2},{2,4},{4,6},{6,0},{1,3},{3,5},{5,7},{7,1},{8,10},{10,12},{12... | collective-permute-start | bytes 786440 | tf_op jit(solution)/shard_map/ppermute | solution.py:252
  42.1 37.8 %collective-permute-start.6 = (bf16[4,2,2,64,512]{4,3,2,1,0:T(8,128)(2,1)S(1)}, bf16[4,2,2,64,512]{4,3,2,1,0:T(8,128)(2,1)S(1)}, u32[]{:S(2)}, u32[]{:S(2)}) collective-permute-start(bf16[4,2,2,64,512]{4,3,2,1,0:T(8,128)(2,1)S(1)} %assemble.1.refs_1_.refs_3_), channel_id=1, source_target_pairs={{0,8},{8,0},{1,9},{9,1},{2,10},{10,2},{3,11},{11,3},{4,12},{12,4},... | collective-permute-start | bytes 3145736 | tf_op jit(solution)/shard_map/ppermute | solution.py:257
  48.0 1.1 copy-start.2
  49.1 30.8 %all-to-all-start.1 = ((bf16[4,256,512]{2,1,0:T(8,128)(2,1)}), bf16[4,256,512]{2,1,0:T(8,128)(2,1)S(1)}, u32[]{:S(2)}, u32[]{:S(2)}) async-start(bf16[4,256,512]{2,1,0:T(8,128)(2,1)} %broadcast_in_dim.8), calls=%async_computation.1 | async-start | bytes 2097152 | tf_op jit(solution)/shard_map/all_to_all | solution.py:238
  53.4 16.5 %collective-permute-start = (bf16[256,512]{1,0:T(8,128)(2,1)}, bf16[256,512]{1,0:T(8,128)(2,1)S(1)}, u32[]{:S(2)}, u32[]{:S(2)}) collective-permute-start(bf16[256,512]{1,0:T(8,128)(2,1)} %bitcast.5), channel_id=1, source_target_pairs={{0,64},{64,0},{1,65},{65,1},{2,66},{66,2},{3,67},{67,3},{4,68},{68... | collective-permute-start | bytes 786440 | tf_op jit(solution)/shard_map/ppermute | solution.py:248
  69.9 14.0 %collective-permute-start.8 = (bf16[256,512]{1,0:T(8,128)(2,1)S(1)}, bf16[256,512]{1,0:T(8,128)(2,1)}, u32[]{:S(2)}, u32[]{:S(2)}) collective-permute-start(bf16[256,512]{1,0:T(8,128)(2,1)S(1)} %collective-permute-done.refs_0_), channel_id=1, source_target_pairs={{0,48},{16,0},{32,16},{48,32},{1,49},{17,1},{33,17},{49,33},{2,50}... | collective-permute-start | bytes 786440 | tf_op jit(solution)/shard_map/ppermute | solution.py:258
  74.2 10.6 %collective-permute-start.7 = (bf16[256,512]{1,0:T(8,128)(2,1)S(1)}, bf16[256,512]{1,0:T(8,128)(2,1)}, u32[]{:S(2)}, u32[]{:S(2)}) collective-permute-start(bf16[256,512]{1,0:T(8,128)(2,1)S(1)} %collective-permute-done.refs_0_), channel_id=1, source_target_pairs={{0,16},{16,32},{32,48},{48,0},{1,17},{17,33},{33,49},{49,1},{2,18}... | collective-permute-start | bytes 786440 | tf_op jit(solution)/shard_map/ppermute | solution.py:255
  76.2 12.5 %collective-permute-start.1 = (bf16[256,512]{1,0:T(8,128)(2,1)S(1)}, bf16[256,512]{1,0:T(8,128)(2,1)}, u32[]{:S(2)}, u32[]{:S(2)}) collective-permute-start(bf16[256,512]{1,0:T(8,128)(2,1)S(1)} %collective-permute-done.refs_0_), channel_id=1, source_target_pairs={{0,32},{16,48},{32,0},{48,16},{1,33},{17,49},{33,1},{49,17},{2,34}... | collective-permute-start | bytes 786440 | tf_op jit(solution)/shard_map/ppermute | solution.py:254
  83.9 4.7 %copy-start = (bf16[2,64,512]{2,1,0:T(8,128)(2,1)S(1)}, bf16[2,64,512]{2,1,0:T(8,128)(2,1)}, u32[]{:S(2)}) copy-start(bf16[2,64,512]{2,1,0:T(8,128)(2,1)} %refs_4_.1) | copy-start | bytes 393220
  88.4 35.3 %copy-start.3 = (f32[2,128]{1,0:T(2,128)S(1)}, f32[2,128]{1,0:T(2,128)}, u32[]{:S(2)}) copy-start(f32[2,128]{1,0:T(2,128)} %get-tuple-element.10) | copy-start | bytes 3076
